TPU v7x, 32 devices: a whole 2x2x4 slice. The times are simulated.
32 devices in a mesh: shard: 8 (over y, x, core), seq: 4 (over z).
Axes of the slice: x: 2, y: 2, z: 4, core: 2. Of those that a mesh axis runs over, the one named last changes fastest.
Arguments:
- inputs: bfloat16 [16, 1376, 1024], P('shard', 'seq'), may hold values from -6 to 6
- teacher: bfloat16 [16, 1376, 1024], P('shard', 'seq'), may hold values from -20 to 20
- cotangent: bfloat16 [16, 1376, 1024], P('shard', 'seq'), may hold values from -6 to 6
- token_valid: int32 [16, 1376], P('shard'), may hold values from 0 to 1, as said below
- image_real: int32 [16], P('shard'), may hold values from 0 to 1, as said below
- w_qkv: bfloat16 [1024, 3072], P('shard'), may hold values from -0.1875 to 0.1875
- q_bias: bfloat16 [1024], P('shard'), may hold values from -3 to 3
- v_bias: bfloat16 [1024], P('shard'), may hold values from -3 to 3
- w_out: bfloat16 [1024, 1024], P('shard'), may hold values from -0.75 to 0.75
- out_bias: bfloat16 [1024], P('shard'), may hold values from -2 to 2
- norm1_gain: bfloat16 [1024], P('shard'), may hold values from 0.5 to 1.5
- norm1_bias: bfloat16 [1024], P('shard'), may hold values from -1 to 1
- scale1: bfloat16 [1024], P('shard'), may hold values from 0.5 to 1.5
- norm2_gain: bfloat16 [1024], P('shard'), may hold values from 0.5 to 1.5
- norm2_bias: bfloat16 [1024], P('shard'), may hold values from -1 to 1
- w_up: bfloat16 [1024, 4096], P('shard'), may hold values from -0.1875 to 0.1875
- up_bias: bfloat16 [4096], P('shard'), may hold values from -3 to 3
- w_down: bfloat16 [4096, 1024], P('shard'), may hold values from -0.1875 to 0.1875
- down_bias: bfloat16 [1024], P('shard'), may hold values from -2 to 2
- scale2: bfloat16 [1024], P('shard'), may hold values from 0.5 to 1.5
Outputs:
- result: bfloat16 [16, 1376, 1024], P('shard', 'seq')
- loss: float32 [], replicated
- grad_inputs: float32 [16, 1376, 1024], P('shard', 'seq')
- grad_w_qkv: float32 [1024, 3072], P('shard')
- grad_q_bias: float32 [1024], P('shard')
- grad_v_bias: float32 [1024], P('shard')
- grad_w_out: float32 [1024, 1024], P('shard')
- grad_out_bias: float32 [1024], P('shard')
- grad_norm1_gain: float32 [1024], P('shard')
- grad_norm1_bias: float32 [1024], P('shard')
- grad_scale1: float32 [1024], P('shard')
- grad_norm2_gain: float32 [1024], P('shard')
- grad_norm2_bias: float32 [1024], P('shard')
- grad_w_up: float32 [1024, 4096], P('shard')
- grad_up_bias: float32 [4096], P('shard')
- grad_w_down: float32 [4096, 1024], P('shard')
- grad_down_bias: float32 [1024], P('shard')
- grad_scale2: float32 [1024], P('shard')
Inputs may be any that keep to these rules, and one draw needn't show every extreme that they name: `token_valid`: each row holds ones first, then zeros, with at least 344 ones and at most 1370. `image_real`: exactly 11 entries are 1.
All inputs are finite; a program needn't handle non-finite values.
Results may differ from a plain program's by a relative error of at most 0.022.
Values may be sent and summed in bfloat16 or wider, within the bound.
No kernel may reach another device: no remote copies, remote signals or barrier semaphores. Data moves between devices by JAX's collectives and lax.ppermute only.
A program may use at most 192 MiB of HBM per device.

v0:
```python
import jax
import jax.numpy as jnp
from jax import lax
from jax.sharding import PartitionSpec as P

HEAD_DIM = 64


def as_sent(x):

    def short(part):
        return part.astype(jnp.bfloat16) if part.dtype == jnp.float32 else part

    return jax.tree.map(short, x)


def layer_norm(values, gain, shift):
    center = values - jnp.mean(values, axis=-1, keepdims=True)
    spread = jnp.mean(center * center, axis=-1, keepdims=True)
    return center * lax.rsqrt(spread + 1e-06) * gain + shift


def norm_back(values, gain, shift, grad):
    _, pull_back = jax.vjp(layer_norm, values, gain, shift)
    return pull_back(grad)


def gelu_exact(values):
    return jax.nn.gelu(values, approximate=False)


def attend_forward(pack):
    query_img, key_img, value_img, key_live = pack
    full_len = query_img.shape[0]
    heads_here = query_img.shape[1] // HEAD_DIM
    score_scale = HEAD_DIM ** (-0.5)
    key_heads = key_img.reshape(full_len, heads_here, HEAD_DIM)
    value_heads = value_img.reshape(full_len, heads_here, HEAD_DIM)
    block_rows = full_len // 2
    mixed_parts = []
    lse_parts = []
    for block_idx in range(2):
        query_block = query_img[block_idx * block_rows : (block_idx + 1) * block_rows].reshape(
            block_rows, heads_here, HEAD_DIM
        )
        scores = (
            jnp.einsum("qhd,khd->hqk", query_block, key_heads, preferred_element_type=jnp.float32)
            * score_scale
        )
        scores = jnp.where(key_live[None, None, :] > 0, scores, -1000000000.0)
        row_peak = jnp.max(scores, axis=-1, keepdims=True)
        exp_scores = jnp.exp(scores - row_peak)
        row_total = jnp.sum(exp_scores, axis=-1, keepdims=True)
        attn_prob = (exp_scores / row_total).astype(jnp.bfloat16)
        mixed_rows = jnp.einsum(
            "hqk,khd->qhd", attn_prob, value_heads, preferred_element_type=jnp.float32
        )
        mixed_parts.append(
            mixed_rows.reshape(block_rows, heads_here * HEAD_DIM).astype(jnp.bfloat16)
        )
        lse_parts.append((row_peak + jnp.log(row_total))[:, :, 0])
    return (jnp.concatenate(mixed_parts, 0), jnp.concatenate(lse_parts, 1))


def attend_backward(pack):
    query_img, key_img, value_img, key_live, lse_img, grad_img = pack
    full_len = query_img.shape[0]
    heads_here = query_img.shape[1] // HEAD_DIM
    score_scale = HEAD_DIM ** (-0.5)
    key_heads = key_img.reshape(full_len, heads_here, HEAD_DIM)
    value_heads = value_img.reshape(full_len, heads_here, HEAD_DIM)
    block_rows = full_len // 2
    key_grad = jnp.zeros((full_len, heads_here, HEAD_DIM), jnp.float32)
    value_grad = jnp.zeros((full_len, heads_here, HEAD_DIM), jnp.float32)
    query_parts = []
    for block_idx in range(2):
        low_row = block_idx * block_rows
        query_block = query_img[low_row : low_row + block_rows].reshape(
            block_rows, heads_here, HEAD_DIM
        )
        grad_block = grad_img[low_row : low_row + block_rows].reshape(
            block_rows, heads_here, HEAD_DIM
        )
        lse_block = lse_img[:, low_row : low_row + block_rows]
        scores = (
            jnp.einsum("qhd,khd->hqk", query_block, key_heads, preferred_element_type=jnp.float32)
            * score_scale
        )
        scores = jnp.where(key_live[None, None, :] > 0, scores, -1000000000.0)
        attn_full = jnp.exp(scores - lse_block[:, :, None])
        attn_prob = attn_full.astype(jnp.bfloat16)
        value_grad = value_grad + jnp.einsum(
            "hqk,qhd->khd", attn_prob, grad_block, preferred_element_type=jnp.float32
        )
        grad_prob = jnp.einsum(
            "qhd,khd->hqk", grad_block, value_heads, preferred_element_type=jnp.float32
        )
        inner_sum = jnp.sum(attn_full * grad_prob, axis=-1, keepdims=True)
        grad_scores = jnp.where(
            key_live[None, None, :] > 0, attn_full * (grad_prob - inner_sum), 0.0
        ).astype(jnp.bfloat16)
        query_block_grad = (
            jnp.einsum("hqk,khd->qhd", grad_scores, key_heads, preferred_element_type=jnp.float32)
            * score_scale
        )
        query_parts.append(
            query_block_grad.reshape(block_rows, heads_here * HEAD_DIM).astype(jnp.bfloat16)
        )
        key_grad = (
            key_grad
            + jnp.einsum(
                "hqk,qhd->khd", grad_scores, query_block, preferred_element_type=jnp.float32
            )
            * score_scale
        )
    width_here = heads_here * HEAD_DIM
    return (
        jnp.concatenate(query_parts, 0),
        key_grad.reshape(full_len, width_here).astype(jnp.bfloat16),
        value_grad.reshape(full_len, width_here).astype(jnp.bfloat16),
    )


def unpack_weights(gathered):
    mats = (gathered[0], gathered[3], gathered[10], gathered[12])
    vecs = tuple(
        (
            gathered[index_pos].astype(jnp.float32)
            for index_pos in (1, 2, 4, 5, 6, 7, 8, 9, 11, 13, 14)
        )
    )
    return (mats, vecs)


def on_device(
    inputs,
    teacher,
    cotangent,
    token_valid,
    image_real,
    w_qkv,
    q_bias,
    v_bias,
    w_out,
    out_bias,
    norm1_gain,
    norm1_bias,
    scale1,
    norm2_gain,
    norm2_bias,
    w_up,
    up_bias,
    w_down,
    down_bias,
    scale2,
):
    gathered = (
        lax.all_gather(w_qkv, "shard", axis=0, tiled=True),
        lax.all_gather(q_bias, "shard", axis=0, tiled=True),
        lax.all_gather(v_bias, "shard", axis=0, tiled=True),
        lax.all_gather(w_out, "shard", axis=0, tiled=True),
        lax.all_gather(out_bias, "shard", axis=0, tiled=True),
        lax.all_gather(norm1_gain, "shard", axis=0, tiled=True),
        lax.all_gather(norm1_bias, "shard", axis=0, tiled=True),
        lax.all_gather(scale1, "shard", axis=0, tiled=True),
        lax.all_gather(norm2_gain, "shard", axis=0, tiled=True),
        lax.all_gather(norm2_bias, "shard", axis=0, tiled=True),
        lax.all_gather(w_up, "shard", axis=0, tiled=True),
        lax.all_gather(up_bias, "shard", axis=0, tiled=True),
        lax.all_gather(w_down, "shard", axis=0, tiled=True),
        lax.all_gather(down_bias, "shard", axis=0, tiled=True),
        lax.all_gather(scale2, "shard", axis=0, tiled=True),
    )
    (qkv_mat, out_mat, up_mat, down_mat), (
        qbias_vec,
        vbias_vec,
        obias_vec,
        gain_one,
        shift_one,
        layer_one,
        gain_two,
        shift_two,
        ubias_vec,
        dbias_vec,
        layer_two,
    ) = unpack_weights(gathered)
    images, tok_dev, width = inputs.shape
    rows = images * tok_dev
    seq_pos = lax.axis_index("seq")
    live_full = (token_valid * image_real[:, None]).astype(jnp.float32)
    live_mine = lax.dynamic_slice_in_dim(live_full, seq_pos * tok_dev, tok_dev, 1).reshape(rows, 1)
    x_rows = inputs.reshape(rows, width).astype(jnp.float32)
    normed1 = layer_norm(x_rows, gain_one, shift_one).astype(jnp.bfloat16)
    qkv_out = jnp.dot(normed1, qkv_mat, preferred_element_type=jnp.float32)
    queries = (qkv_out[:, 0:width] + qbias_vec).astype(jnp.bfloat16).reshape(images, tok_dev, width)
    key_rows = qkv_out[:, width : 2 * width].astype(jnp.bfloat16).reshape(images, tok_dev, width)
    value_rows = (
        (qkv_out[:, 2 * width : 3 * width] + vbias_vec)
        .astype(jnp.bfloat16)
        .reshape(images, tok_dev, width)
    )
    query_heads, key_heads, value_heads = (
        lax.all_to_all(queries, "seq", split_axis=2, concat_axis=1, tiled=True),
        lax.all_to_all(key_rows, "seq", split_axis=2, concat_axis=1, tiled=True),
        lax.all_to_all(value_rows, "seq", split_axis=2, concat_axis=1, tiled=True),
    )
    mixed_heads, lse_all = lax.map(attend_forward, (query_heads, key_heads, value_heads, live_full))
    mixed_tok = jax.tree.map(
        lambda part, own: part.astype(own.dtype),
        lax.all_to_all(as_sent(mixed_heads), "seq", split_axis=1, concat_axis=2, tiled=True),
        mixed_heads,
    ).reshape(rows, width)
    attn_out = jnp.dot(mixed_tok, out_mat, preferred_element_type=jnp.float32) + obias_vec
    resid_one = x_rows + layer_one * attn_out
    normed2 = layer_norm(resid_one, gain_two, shift_two).astype(jnp.bfloat16)
    hidden_pre = jnp.dot(normed2, up_mat, preferred_element_type=jnp.float32) + ubias_vec
    hidden_act = gelu_exact(hidden_pre).astype(jnp.bfloat16)
    branch_out = jnp.dot(hidden_act, down_mat, preferred_element_type=jnp.float32) + dbias_vec
    resid_two = resid_one + layer_two * branch_out
    out_rows = jnp.where(live_mine > 0, resid_two, x_rows)
    diff_rows = (out_rows - teacher.reshape(rows, width).astype(jnp.float32)) * live_mine
    err_total, live_total = lax.psum(
        (jnp.sum(diff_rows * diff_rows), jnp.sum(live_mine)), ("shard", "seq")
    )
    loss = err_total / (live_total * width)
    regathered = (
        lax.all_gather(w_qkv, "shard", axis=0, tiled=True),
        lax.all_gather(q_bias, "shard", axis=0, tiled=True),
        lax.all_gather(v_bias, "shard", axis=0, tiled=True),
        lax.all_gather(w_out, "shard", axis=0, tiled=True),
        lax.all_gather(out_bias, "shard", axis=0, tiled=True),
        lax.all_gather(norm1_gain, "shard", axis=0, tiled=True),
        lax.all_gather(norm1_bias, "shard", axis=0, tiled=True),
        lax.all_gather(scale1, "shard", axis=0, tiled=True),
        lax.all_gather(norm2_gain, "shard", axis=0, tiled=True),
        lax.all_gather(norm2_bias, "shard", axis=0, tiled=True),
        lax.all_gather(w_up, "shard", axis=0, tiled=True),
        lax.all_gather(up_bias, "shard", axis=0, tiled=True),
        lax.all_gather(w_down, "shard", axis=0, tiled=True),
        lax.all_gather(down_bias, "shard", axis=0, tiled=True),
        lax.all_gather(scale2, "shard", axis=0, tiled=True),
    )
    (qkv_mat, out_mat, up_mat, down_mat), (
        qbias_vec,
        vbias_vec,
        obias_vec,
        gain_one,
        shift_one,
        layer_one,
        gain_two,
        shift_two,
        ubias_vec,
        dbias_vec,
        layer_two,
    ) = unpack_weights(regathered)
    grad_out = cotangent.reshape(rows, width).astype(jnp.float32) + 2.0 * diff_rows / (
        live_total * width
    )
    grad_keep = jnp.where(live_mine > 0, grad_out, 0.0)
    grad_pass = grad_out - grad_keep
    d_scale2 = jnp.sum(grad_keep * branch_out, axis=0)
    grad_branch = (grad_keep * layer_two).astype(jnp.bfloat16)
    d_down_bias = jnp.sum(grad_branch.astype(jnp.float32), axis=0)
    d_w_down = jnp.einsum("rf,rd->fd", hidden_act, grad_branch, preferred_element_type=jnp.float32)
    grad_hidden = jnp.einsum("rd,fd->rf", grad_branch, down_mat, preferred_element_type=jnp.float32)
    _, gelu_pull = jax.vjp(gelu_exact, hidden_pre)
    grad_pre = gelu_pull(grad_hidden)[0].astype(jnp.bfloat16)
    d_up_bias = jnp.sum(grad_pre.astype(jnp.float32), axis=0)
    d_w_up = jnp.einsum("rd,rf->df", normed2, grad_pre, preferred_element_type=jnp.float32)
    grad_norm2 = jnp.einsum("rf,df->rd", grad_pre, up_mat, preferred_element_type=jnp.float32)
    grad_res_ln, d_norm2_gain, d_norm2_bias = norm_back(resid_one, gain_two, shift_two, grad_norm2)
    grad_resid = grad_keep + grad_res_ln
    d_scale1 = jnp.sum(grad_resid * attn_out, axis=0)
    grad_attn = (grad_resid * layer_one).astype(jnp.bfloat16)
    d_out_bias = jnp.sum(grad_attn.astype(jnp.float32), axis=0)
    d_w_out = jnp.einsum("rc,rd->cd", mixed_tok, grad_attn, preferred_element_type=jnp.float32)
    grad_mixed = jnp.einsum("rd,cd->rc", grad_attn, out_mat, preferred_element_type=jnp.float32)
    grad_mixed = grad_mixed.astype(jnp.bfloat16).reshape(images, tok_dev, width)
    grad_heads = lax.all_to_all(grad_mixed, "seq", split_axis=2, concat_axis=1, tiled=True)
    query_grad, key_grad, value_grad = lax.map(
        attend_backward, (query_heads, key_heads, value_heads, live_full, lse_all, grad_heads)
    )
    query_grad, key_grad, value_grad = (
        lax.all_to_all(as_sent(query_grad), "seq", split_axis=1, concat_axis=2, tiled=True).astype(
            query_grad.dtype
        ),
        lax.all_to_all(as_sent(key_grad), "seq", split_axis=1, concat_axis=2, tiled=True).astype(
            key_grad.dtype
        ),
        lax.all_to_all(as_sent(value_grad), "seq", split_axis=1, concat_axis=2, tiled=True).astype(
            value_grad.dtype
        ),
    )
    grad_qkv = jnp.concatenate([query_grad, key_grad, value_grad], axis=2).reshape(rows, 3 * width)
    d_q_bias = jnp.sum(query_grad.reshape(rows, width).astype(jnp.float32), axis=0)
    d_v_bias = jnp.sum(value_grad.reshape(rows, width).astype(jnp.float32), axis=0)
    d_w_qkv = jnp.einsum("rd,re->de", normed1, grad_qkv, preferred_element_type=jnp.float32)
    grad_norm1 = jnp.einsum("re,de->rd", grad_qkv, qkv_mat, preferred_element_type=jnp.float32)
    grad_in_ln, d_norm1_gain, d_norm1_bias = norm_back(x_rows, gain_one, shift_one, grad_norm1)
    grad_inputs = (grad_pass + grad_resid + grad_in_ln).reshape(images, tok_dev, width)
    grad_parts = (
        lax.psum_scatter(d_w_qkv, "shard", scatter_dimension=0, tiled=True),
        lax.psum_scatter(d_q_bias, "shard", scatter_dimension=0, tiled=True),
        lax.psum_scatter(d_v_bias, "shard", scatter_dimension=0, tiled=True),
        lax.psum_scatter(d_w_out, "shard", scatter_dimension=0, tiled=True),
        lax.psum_scatter(d_out_bias, "shard", scatter_dimension=0, tiled=True),
        lax.psum_scatter(d_norm1_gain, "shard", scatter_dimension=0, tiled=True),
        lax.psum_scatter(d_norm1_bias, "shard", scatter_dimension=0, tiled=True),
        lax.psum_scatter(d_scale1, "shard", scatter_dimension=0, tiled=True),
        lax.psum_scatter(d_norm2_gain, "shard", scatter_dimension=0, tiled=True),
        lax.psum_scatter(d_norm2_bias, "shard", scatter_dimension=0, tiled=True),
        lax.psum_scatter(d_w_up, "shard", scatter_dimension=0, tiled=True),
        lax.psum_scatter(d_up_bias, "shard", scatter_dimension=0, tiled=True),
        lax.psum_scatter(d_w_down, "shard", scatter_dimension=0, tiled=True),
        lax.psum_scatter(d_down_bias, "shard", scatter_dimension=0, tiled=True),
        lax.psum_scatter(d_scale2, "shard", scatter_dimension=0, tiled=True),
    )
    grad_final = tuple(lax.psum(tuple(grad_parts), "seq"))
    result = out_rows.astype(jnp.bfloat16).reshape(images, tok_dev, width)
    return (result, loss, grad_inputs) + tuple(grad_final)


def solution(mesh):
    in_specs = (
        P("shard", "seq", None),
        P("shard", "seq", None),
        P("shard", "seq", None),
        P("shard", None),
        P("shard"),
        P("shard", None),
        P("shard"),
        P("shard"),
        P("shard", None),
        P("shard"),
        P("shard"),
        P("shard"),
        P("shard"),
        P("shard"),
        P("shard"),
        P("shard", None),
        P("shard"),
        P("shard", None),
        P("shard"),
        P("shard"),
    )
    out_specs = (
        P("shard", "seq", None),
        P(),
        P("shard", "seq", None),
        P("shard", None),
        P("shard"),
        P("shard"),
        P("shard", None),
        P("shard"),
        P("shard"),
        P("shard"),
        P("shard"),
        P("shard"),
        P("shard"),
        P("shard", None),
        P("shard"),
        P("shard", None),
        P("shard"),
        P("shard"),
    )
    return jax.shard_map(
        on_device, mesh=mesh, in_specs=in_specs, out_specs=out_specs, check_vma=False
    )
```

profile of v0, /device:TPU:0, one launch (start us, length us, event | category | flops | bytes accessed | tf_op | source)
XLA Modules:
  0.0 1489.0 jit_solution(15059101976948463380)
XLA Ops:
  10.4 10.3 all-gather.1
  20.7 9.0 all-gather.2
  30.4 27.7 %all-gather.16.cloned.1.call-done = bf16[1024,3072]{1,0:T(8,128)(2,1)} async-done(((bf16[128,3072]{1,0:T(8,128)(2,1)}), bf16[1024,3072]{1,0:T(8,128)(2,1)}) %all-gather.16.cloned.1.call-update) | async-done | bytes 6291472 | tf_op jit(solution)/shard_map/all_gather | solution.py:158
  75.9 8.9 all-gather.4
  84.7 7.8 all-gather.3
  100.1 13.1 all-to-all-done.2
  121.9 31.4 %all-to-all-done = bf16[2,344,1024]{1,0,2:T(2,128)(2,1)S(1)} async-done(((bf16[2,344,1024]{1,0,2:T(2,128)(2,1)}), bf16[2,344,1024]{1,0,2:T(2,128)(2,1)S(1)}, u32[]{:S(2)}, u32[]{:S(2)}) %all-to-all-start) | async-done | bytes 1409056 | tf_op jit(solution)/shard_map/all_to_all | solution.py:205
  170.0 24.2 %all-to-all-done.1 = bf16[2,344,1024]{1,0,2:T(2,128)(2,1)} async-done(((bf16[2,344,1024]{1,0,2:T(2,128)(2,1)}), bf16[2,344,1024]{1,0,2:T(2,128)(2,1)}, u32[]{:S(2)}, u32[]{:S(2)}) %all-to-all-start.1) | async-done | bytes 1409056 | tf_op jit(solution)/shard_map/all_to_all | solution.py:203
  200.6 66.3 %while.26 = (s32[]{:T(128)}, bf16[2,1376,256]{1,2,0:T(8,128)(2,1)S(1)}, f32[2,4,1376]{2,1,0:T(4,128)S(1)}, bf16[2,1376,256]{1,2,0:T(8,128)(2,1)}, f32[2,1376]{1,...) while((s32[]{:T(128)}, ...), condition=%wide.region_7.8_spmd, body=%wide.region_2.7_spmd.sunk | while | flops 2031461760 | bytes 161668704 | solution.py:207
  206.1 8.6 fusion.193
  219.2 8.3 fusion.194
  239.2 8.6 fusion.193
  252.3 8.3 fusion.194
  273.5 8.7 all-gather.5
  282.3 7.8 all-gather
  290.1 8.7 all-gather.7
  298.9 7.8 all-gather.8
  306.7 8.7 all-gather.10
  315.5 8.3 all-gather.6
  324.5 8.9 all-gather.9
  341.9 35.4 %multiply_convert_fusion = (bf16[688,4096]{1,0:T(8,128)(2,1)}, f32[688,4096]{1,0:T(8,128)}, f32[688,4096]{1,0:T(8,128)}) fusion(f32[4096]{0:T(1024)S(1)} %bitcast.331, bf16[1024,4096]{1,0:T(8,128)(2,1)} %all-gather.20.cloned.1.call-done, f32[688,1024]{1,0:T(8,128)S(1)} %get-tuple-element.272, f32[1024]{0:T(1024)S(1)} %bitcast.311, f32[1024]{0:T(1024)S(1)} %bitcast.307, ...), kind=kOutput, calls=%fused_computation.80 | convolution fusion | flops 5960876032 | bytes 39417216 | tf_op jit(solution)/shard_map/dot_general | solution.py:216
  377.4 13.8 multiply_reduce_fusion.7
  391.2 40.1 %all-reduce.11 = (f32[]{:T(128)}, f32[]{:T(128)}) all-reduce(f32[]{:T(128)} %get-tuple-element.249, f32[]{:T(128)} %get-tuple-element.247), channel_id=1, replica_groups=mesh['shard'=8,'seq'=4] {'shard','seq'}, use_global_device_ids=true, to_apply=%region_11.12 | all-reduce | flops 2 | bytes 16 | tf_op jit(solution)/shard_map/psum | solution.py:222
  439.1 19.4 %convert_reduce_fusion = (f32[4096]{0:T(1024)}, bf16[688,4096]{1,0:T(8,128)(2,1)}) fusion(f32[688,4096]{1,0:T(8,128)} %get-tuple-element.252, f32[688,4096]{1,0:T(8,128)} %get-tuple-element.274, f32[4096]{0:T(1024)S(1)} %bitcast.332, bf16[688,1024]{1,0:T(8,128)(2,1)} %get-tuple-element.239, bf16[4096,1024]{1,0:T(8,128)(2,1)} %all-gather.22.cloned.1.call-done), kind=kOutput, calls=%fused_computation.78 | convolution fusion | flops 5819265024 | bytes 38010880 | tf_op jit(solution)/shard_map/rd,fd->rf/dot_general | solution.py:265
  458.5 11.4 multiply_reduce_fusion.2
  481.7 36.5 %all-to-all-done.4 = bf16[2,344,1024]{1,0,2:T(2,128)(2,1)S(1)} async-done(((bf16[2,344,1024]{1,0,2:T(2,128)(2,1)}), bf16[2,344,1024]{1,0,2:T(2,128)(2,1)S(1)}, u32[]{:S(2)}, u32[]{:S(2)}) %all-to-all-start.4) | async-done | bytes 1409056 | tf_op jit(solution)/shard_map/all_to_all | solution.py:279
  526.2 262.4 %while.27 = (s32[]{:T(128)}, bf16[2,1376,256]{1,2,0:T(8,128)(2,1)}, bf16[2,1376,256]{1,2,0:T(8,128)(2,1)}, bf16[2,1376,256]{1,2,0:T(8,128)(2,1)}, bf16[2,1376,25...) while((s32[]{:T(128)}, bf16[2,1376,256]{1,2,0:T(8,128)(2,1)}, ...), condition=%wide.region_19.20_spmd, body=%wide.region_16.19_spmd.sunk | while | flops 4956964352 | bytes 300296704 | solution.py:280
  564.0 20.5 %fusion.223 = bf16[4,64,688]{2,1,0:T(8,128)(2,1)S(1)} fusion(bf16[1376,4,64]{0,2,1:T(8,128)(2,1)S(1)} %bitcast.262, f32[4,688,1376]{2,1,0:T(8,128)} %subtract_exponential_fusion.7, f32[4,688,1376]{2,1,0:T(8,128)} %fusion.222, pred[1376]{0:T(1024)(128)(4,1)S(1)} %compare_reduce_fusion.5), kind=kOutput, calls=%fused_computation.58.clone.1 | convolution fusion | flops 503994400 | bytes 31352160 | tf_op jit(solution)/shard_map/while/body/eval_jaxpr/hqk,khd->qhd/dot_general | solution.py:103
  584.5 21.6 %fusion.227 = f32[4,64,1376]{2,1,0:T(8,128)} fusion(bf16[688,4,64]{0,2,1:T(8,128)(2,1)} %bitcast.279, f32[4,688,1376]{2,1,0:T(8,128)} %subtract_exponential_fusion.7, f32[4,688,1376]{2,1,0:T(8,128)} %fusion.222, pred[1376]{0:T(1024)(128)(4,1)S(1)} %compare_reduce_fusion.5), kind=kOutput, calls=%fused_computation.43.clone.1 | convolution fusion | flops 503642144 | bytes 32056672 | tf_op jit(solution)/shard_map/while/body/eval_jaxpr/hqk,qhd->khd/dot_general | solution.py:111
  613.8 20.9 %fusion.228 = bf16[4,64,1376]{2,1,0:T(8,128)(2,1)S(1)} fusion(f32[4,64,1376]{2,1,0:T(8,128)} %fusion.227, bf16[688,4,64]{0,2,1:T(8,128)(2,1)S(1)} %bitcast.275, f32[4,688,1376]{2,1,0:T(8,128)} %copy-done.1, f32[4,688,1376]{2,1,0:T(8,128)} %fusion.220, pred[1376]{0:T(1024)(128)(4,1)S(1)} %compare_reduce_fusion.5), kind=kOutput, calls=%fused_computation.55.clone.1 | convolution fusion | flops 504698912 | bytes 32761184 | tf_op jit(solution)/shard_map/while/body/eval_jaxpr/hqk,qhd->khd/dot_general | solution.py:111
  634.7 20.6 %fusion.221 = bf16[4,64,688]{2,1,0:T(8,128)(2,1)S(1)} fusion(bf16[1376,4,64]{0,2,1:T(8,128)(2,1)S(1)} %bitcast.263, f32[4,688,1376]{2,1,0:T(8,128)} %copy-done.1, f32[4,688,1376]{2,1,0:T(8,128)} %fusion.220, pred[1376]{0:T(1024)(128)(4,1)S(1)} %compare_reduce_fusion.5), kind=kOutput, calls=%fused_computation.59.clone.1 | convolution fusion | flops 503994400 | bytes 31352160 | tf_op jit(solution)/shard_map/while/body/eval_jaxpr/hqk,khd->qhd/dot_general | solution.py:103
  694.9 20.5 %fusion.223 = bf16[4,64,688]{2,1,0:T(8,128)(2,1)S(1)} fusion(bf16[1376,4,64]{0,2,1:T(8,128)(2,1)S(1)} %bitcast.262, f32[4,688,1376]{2,1,0:T(8,128)} %subtract_exponential_fusion.7, f32[4,688,1376]{2,1,0:T(8,128)} %fusion.222, pred[1376]{0:T(1024)(128)(4,1)S(1)} %compare_reduce_fusion.5), kind=kOutput, calls=%fused_computation.58.clone.1 | convolution fusion | flops 503994400 | bytes 31352160 | tf_op jit(solution)/shard_map/while/body/eval_jaxpr/hqk,khd->qhd/dot_general | solution.py:103
  715.4 21.6 %fusion.227 = f32[4,64,1376]{2,1,0:T(8,128)} fusion(bf16[688,4,64]{0,2,1:T(8,128)(2,1)} %bitcast.279, f32[4,688,1376]{2,1,0:T(8,128)} %subtract_exponential_fusion.7, f32[4,688,1376]{2,1,0:T(8,128)} %fusion.222, pred[1376]{0:T(1024)(128)(4,1)S(1)} %compare_reduce_fusion.5), kind=kOutput, calls=%fused_computation.43.clone.1 | convolution fusion | flops 503642144 | bytes 32056672 | tf_op jit(solution)/shard_map/while/body/eval_jaxpr/hqk,qhd->khd/dot_general | solution.py:111
  744.7 20.9 %fusion.228 = bf16[4,64,1376]{2,1,0:T(8,128)(2,1)S(1)} fusion(f32[4,64,1376]{2,1,0:T(8,128)} %fusion.227, bf16[688,4,64]{0,2,1:T(8,128)(2,1)S(1)} %bitcast.275, f32[4,688,1376]{2,1,0:T(8,128)} %copy-done.1, f32[4,688,1376]{2,1,0:T(8,128)} %fusion.220, pred[1376]{0:T(1024)(128)(4,1)S(1)} %compare_reduce_fusion.5), kind=kOutput, calls=%fused_computation.55.clone.1 | convolution fusion | flops 504698912 | bytes 32761184 | tf_op jit(solution)/shard_map/while/body/eval_jaxpr/hqk,qhd->khd/dot_general | solution.py:111
  765.6 20.6 %fusion.221 = bf16[4,64,688]{2,1,0:T(8,128)(2,1)S(1)} fusion(bf16[1376,4,64]{0,2,1:T(8,128)(2,1)S(1)} %bitcast.263, f32[4,688,1376]{2,1,0:T(8,128)} %copy-done.1, f32[4,688,1376]{2,1,0:T(8,128)} %fusion.220, pred[1376]{0:T(1024)(128)(4,1)S(1)} %compare_reduce_fusion.5), kind=kOutput, calls=%fused_computation.59.clone.1 | convolution fusion | flops 503994400 | bytes 31352160 | tf_op jit(solution)/shard_map/while/body/eval_jaxpr/hqk,khd->qhd/dot_general | solution.py:103
  806.0 24.9 %all-to-all-done.7 = bf16[2,1376,256]{2,0,1:T(2,128)(2,1)} async-done(((bf16[2,1376,256]{2,0,1:T(2,128)(2,1)}), bf16[2,1376,256]{2,0,1:T(2,128)(2,1)}, u32[]{:S(2)}, u32[]{:S(2)}) %all-to-all-start.7) | async-done | bytes 1409056 | tf_op jit(solution)/shard_map/all_to_all | solution.py:290
  837.4 30.1 %all-to-all-done.5 = bf16[2,1376,256]{2,0,1:T(2,128)(2,1)S(1)} async-done(((bf16[2,1376,256]{2,0,1:T(2,128)(2,1)}), bf16[2,1376,256]{2,0,1:T(2,128)(2,1)S(1)}, u32[]{:S(2)}, u32[]{:S(2)}) %all-to-all-start.5) | async-done | bytes 1409056 | tf_op jit(solution)/shard_map/all_to_all | solution.py:284
  876.6 28.3 %all-to-all-done.6 = bf16[2,1376,256]{2,0,1:T(2,128)(2,1)} async-done(((bf16[2,1376,256]{2,0,1:T(2,128)(2,1)}), bf16[2,1376,256]{2,0,1:T(2,128)(2,1)}, u32[]{:S(2)}, u32[]{:S(2)}) %all-to-all-start.6) | async-done | bytes 1409056 | tf_op jit(solution)/shard_map/all_to_all | solution.py:287
  909.7 8.1 fusion.98
  919.7 16.4 %fusion.88 = f32[1024,4096]{1,0:T(8,128)} fusion(bf16[688,4096]{1,0:T(8,128)(2,1)} %get-tuple-element.242, f32[688,1024]{1,0:T(8,128)S(1)} %copy-done.3, f32[1024]{0:T(1024)S(1)} %bitcast.312, f32[1024]{0:T(1024)S(1)} %bitcast.310, f32[688]{0:T(1024)S(1)} %copy-done.33, f32[688]{0:T(1024)S(1)} %copy-done.27), kind=kOutput, calls=%fused_computation.146 | convolution fusion | flops 5774884864 | bytes 25245056 | tf_op jit(solution)/shard_map/rd,rf->df/dot_general | solution.py:269
  937.5 12.9 fusion.100
  950.5 58.7 %reduce-scatter.5.cloned.1.call-done = f32[128,3072]{1,0:T(8,128)} async-done(((f32[1024,3072]{1,0:T(8,128)}), f32[128,3072]{1,0:T(8,128)}) %reduce-scatter.5.cloned.1.call-update) | async-done | bytes 1572880 | tf_op jit(solution)/shard_map/reduce_scatter | solution.py:302
  1009.3 119.8 %reduce-scatter.9.cloned.1.call-done = f32[128,4096]{1,0:T(8,128)} async-done(((f32[1024,4096]{1,0:T(8,128)}), f32[128,4096]{1,0:T(8,128)}) %reduce-scatter.9.cloned.1.call-update) | async-done | bytes 2097168 | tf_op jit(solution)/shard_map/reduce_scatter | solution.py:312
  1129.0 119.8 %reduce-scatter.11.cloned.1.call-done = f32[512,1024]{1,0:T(8,128)} async-done(((f32[4096,1024]{1,0:T(8,128)}), f32[512,1024]{1,0:T(8,128)}) %reduce-scatter.11.cloned.1.call-update) | async-done | bytes 2097168 | tf_op jit(solution)/shard_map/reduce_scatter | solution.py:314
  1253.8 8.8 multiply_reduce_fusion.4
  1274.1 24.9 %all-reduce.12 = (f32[1024]{0:T(1024)S(1)}, f32[1024]{0:T(1024)S(1)}, f32[1024]{0:T(1024)S(1)}, f32[1024]{0:T(1024)S(1)}, f32[1024]{0:T(1024)S(1)}, /*index=5*/f...) all-reduce(f32[1024]{0:T(1024)S(1)} %bitcast.330, ...), channel_id=3, replica_groups=mesh['shard'=8,'seq'=4] {'shard'}, use_global_device_ids=true, to_apply=%region_25.26.clone | all-reduce | flops 14336 | bytes 114688
  1299.8 15.5 %all-reduce.13 = (f32[128]{0:T(128)}, f32[128]{0:T(128)}, f32[128]{0:T(128)}, f32[128]{0:T(128)}, f32[128]{0:T(128)}, /*index=5*/f32[128]{0:T(128)}, f32[128]{0:...) all-reduce(f32[128]{0:T(128)S(1)} %dynamic-slice.1, ...), channel_id=1, replica_groups=mesh['shard'=8,'seq'=4] {'seq'}, use_global_device_ids=true, to_apply=%region_26.27 | all-reduce | flops 1792 | bytes 14336 | tf_op jit(solution)/shard_map/psum | solution.py:318
  1315.3 159.5 %all-reduce.17.cloned.1.call-done = (f32[128,3072]{1,0:T(8,128)}, f32[128,1024]{1,0:T(8,128)}, f32[128,4096]{1,0:T(8,128)}, f32[512,1024]{1,0:T(8,128)}) async-done(((f32[128,3072]{1,0:T(8,128)}, f32[128,1024]{1,0:T(8,128)}, f32[128,4096]{1,0:T(8,128)}, f32[512,1024]{1,0:T(8,128)}), (f32[128,3072]{1,0:T(8,128)}, f32[128,1024]{1,0:T(8,128)}, f32[128,4096]{1,0:T(8,128)}, ...) | async-done | bytes 6291472 | tf_op jit(solution)/shard_map/psum | solution.py:318
  (342 shorter events, 292.2 us)
Async XLA Ops:
  7.2 13.5 copy-start.62
  7.2 50.9 %all-gather.16.cloned.1.call-start = ((), (), s32[]{:S(2)}) async-start(), calls=%async_computation.12 | async-start | bytes 7077888 | tf_op jit(solution)/shard_map/all_gather | solution.py:158
  8.0 327.6 %all-gather.18.cloned.1.call-start = ((), (), s32[]{:S(2)}) async-start(), calls=%async_computation.13 | async-start | bytes 2359296 | tf_op jit(solution)/shard_map/all_gather | solution.py:161
  8.7 333.2 %all-gather.20.cloned.1.call-start = ((), (), s32[]{:S(2)}) async-start(), calls=%async_computation.14 | async-start | bytes 9437184 | tf_op jit(solution)/shard_map/all_gather | solution.py:168
  9.8 54.9 %copy-start.38 = (f32[688]{0:T(1024)}, f32[688]{0:T(1024)S(1)}, u32[]{:S(2)}) copy-start(f32[688]{0:T(1024)S(1)} %div.68) | copy-start | bytes 8260
  10.4 19.4 %copy-start.46 = (f32[688]{0:T(1024)}, f32[688]{0:T(1024)S(1)}, u32[]{:S(2)}) copy-start(f32[688]{0:T(1024)S(1)} %add.195) | copy-start | bytes 8260
  10.4 19.4 %copy-start.40 = (f32[688]{0:T(1024)}, f32[688]{0:T(1024)S(1)}, u32[]{:S(2)}) copy-start(f32[688]{0:T(1024)S(1)} %rsqrt.22) | copy-start | bytes 8260
  20.7 9.1 copy-start.42
  30.4 34.3 %copy-start.17 = (bf16[688,1024]{1,0:T(8,128)(2,1)}, bf16[688,1024]{1,0:T(8,128)(2,1)S(1)}, u32[]{:S(2)}) copy-start(bf16[688,1024]{1,0:T(8,128)(2,1)S(1)} %add_convert_fusion.2) | copy-start | bytes 4227076
  68.3 7.6 copy-start.63
  68.3 16.5 %copy-start.64 = (bf16[128]{0:T(256)(128)(2,1)S(1)}, bf16[128]{0:T(256)(128)(2,1)}, u32[]{:S(2)}) copy-start(bf16[128]{0:T(256)(128)(2,1)} %param.31) | copy-start | bytes 772
  71.3 42.0 %all-to-all-start.2 = ((bf16[2,344,1024]{1,0,2:T(2,128)(2,1)}), bf16[2,344,1024]{1,0,2:T(2,128)(2,1)S(1)}, u32[]{:S(2)}, u32[]{:S(2)}) async-start(bf16[2,344,1024]{1,0,2:T(2,128)(2,1)} %copy.82), calls=%async_computation.2 | async-start | bytes 3145728 | tf_op jit(solution)/shard_map/all_to_all | solution.py:204
  113.2 40.1 %all-to-all-start = ((bf16[2,344,1024]{1,0,2:T(2,128)(2,1)}), bf16[2,344,1024]{1,0,2:T(2,128)(2,1)S(1)}, u32[]{:S(2)}, u32[]{:S(2)}) async-start(bf16[2,344,1024]{1,0,2:T(2,128)(2,1)} %copy.76), calls=%async_computation | async-start | bytes 3145728 | tf_op jit(solution)/shard_map/all_to_all | solution.py:205
  121.9 36.4 %copy-start.57 = (s32[2,1376]{1,0:T(2,128)S(1)}, s32[2,1376]{1,0:T(2,128)}, u32[]{:S(2)}) copy-start(s32[2,1376]{1,0:T(2,128)} %param.27) | copy-start | bytes 33028
  121.9 36.4 %copy-start.65 = (s32[2]{0:T(128)S(1)}, s32[2]{0:T(128)}, u32[]{:S(2)}) copy-start(s32[2]{0:T(128)} %param.28) | copy-start | bytes 28
  153.3 40.9 %all-to-all-start.1 = ((bf16[2,344,1024]{1,0,2:T(2,128)(2,1)}), bf16[2,344,1024]{1,0,2:T(2,128)(2,1)}, u32[]{:S(2)}, u32[]{:S(2)}) async-start(bf16[2,344,1024]{1,0,2:T(2,128)(2,1)} %copy.79), calls=%async_computation.1 | async-start | bytes 3145728 | tf_op jit(solution)/shard_map/all_to_all | solution.py:203
  157.7 219.7 %all-gather.22.cloned.1.call-start = ((), (), s32[]{:S(2)}) async-start(), calls=%async_computation.15 | async-start | bytes 9437184 | tf_op jit(solution)/shard_map/all_gather | solution.py:170
  219.2 9.9 copy-start
  252.3 9.9 copy-start
  267.0 56.8 %copy-start.28 = (f32[2,1376]{1,0:T(2,128)}, f32[2,1376]{1,0:T(2,128)S(1)}, u32[]{:S(2)}) copy-start(f32[2,1376]{1,0:T(2,128)S(1)} %get-tuple-element.560) | copy-start | bytes 33028
  267.0 15.3 %copy-start.67 = (bf16[128]{0:T(256)(128)(2,1)S(1)}, bf16[128]{0:T(256)(128)(2,1)}, u32[]{:S(2)}) copy-start(bf16[128]{0:T(256)(128)(2,1)} %param.36) | copy-start | bytes 772
  267.0 23.1 %copy-start.68 = (bf16[128]{0:T(256)(128)(2,1)S(1)}, bf16[128]{0:T(256)(128)(2,1)}, u32[]{:S(2)}) copy-start(bf16[128]{0:T(256)(128)(2,1)} %param.37) | copy-start | bytes 772
  267.0 31.9 %copy-start.69 = (bf16[128]{0:T(256)(128)(2,1)S(1)}, bf16[128]{0:T(256)(128)(2,1)}, u32[]{:S(2)}) copy-start(bf16[128]{0:T(256)(128)(2,1)} %param.38) | copy-start | bytes 772
  267.0 39.7 %copy-start.70 = (bf16[128]{0:T(256)(128)(2,1)S(1)}, bf16[128]{0:T(256)(128)(2,1)}, u32[]{:S(2)}) copy-start(bf16[128]{0:T(256)(128)(2,1)} %param.42) | copy-start | bytes 772
  267.0 48.5 %copy-start.71 = (bf16[128]{0:T(256)(128)(2,1)S(1)}, bf16[128]{0:T(256)(128)(2,1)}, u32[]{:S(2)}) copy-start(bf16[128]{0:T(256)(128)(2,1)} %param.43) | copy-start | bytes 772
  269.9 63.5 %all-to-all-start.3 = ((bf16[2,1376,256]{2,0,1:T(2,128)(2,1)}), bf16[2,1376,256]{2,0,1:T(2,128)(2,1)S(1)}, u32[]{:S(2)}, u32[]{:S(2)}) async-start(bf16[2,1376,256]{2,0,1:T(2,128)(2,1)} %copy.88), calls=%async_computation.3 | async-start | bytes 2818048 | tf_op jit(solution)/shard_map/all_to_all | solution.py:210
  282.3 53.3 %copy-start.52 = (f32[8,1,128]{2,1,0:T(1,128)}, f32[8,1,128]{2,1,0:T(1,128)S(1)}, u32[]{:S(2)}) copy-start(f32[8,1,128]{2,1,0:T(1,128)S(1)} %convert_element_type.238) | copy-start | bytes 12292
  298.9 171.1 %copy-start.30 = (f32[8,1,128]{2,1,0:T(1,128)}, f32[8,1,128]{2,1,0:T(1,128)S(1)}, u32[]{:S(2)}) copy-start(f32[8,1,128]{2,1,0:T(1,128)S(1)} %convert_element_type.240) | copy-start | bytes 12292
  306.7 35.2 %copy-start.34 = (f32[8,1,128]{2,1,0:T(1,128)}, f32[8,1,128]{2,1,0:T(1,128)S(1)}, u32[]{:S(2)}) copy-start(f32[8,1,128]{2,1,0:T(1,128)S(1)} %convert_element_type.241) | copy-start | bytes 12292
  315.5 61.9 %copy-start.54 = (f32[8,1,128]{2,1,0:T(1,128)}, f32[8,1,128]{2,1,0:T(1,128)S(1)}, u32[]{:S(2)}) copy-start(f32[8,1,128]{2,1,0:T(1,128)S(1)} %convert_element_type.243) | copy-start | bytes 12292
  333.4 137.4 %copy-start.49 = (pred[688]{0:T(1024)(128)(4,1)}, pred[688]{0:T(1024)(128)(4,1)S(1)}, u32[]{:S(2)}) copy-start(pred[688]{0:T(1024)(128)(4,1)S(1)} %broadcast_compare_fusion) | copy-start | bytes 2068
  341.2 128.7 %copy-start.2 = (f32[688,1024]{1,0:T(8,128)}, f32[688,1024]{1,0:T(8,128)S(1)}, u32[]{:S(2)}) copy-start(f32[688,1024]{1,0:T(8,128)S(1)} %get-tuple-element.272) | copy-start | bytes 8454148
  341.4 128.5 %copy-start.26 = (f32[688]{0:T(1024)}, f32[688]{0:T(1024)S(1)}, u32[]{:S(2)}) copy-start(f32[688]{0:T(1024)S(1)} %broadcast_multiply_fusion) | copy-start | bytes 8260
  341.9 128.1 %copy-start.32 = (f32[688]{0:T(1024)}, f32[688]{0:T(1024)S(1)}, u32[]{:S(2)}) copy-start(f32[688]{0:T(1024)S(1)} %fusion.87) | copy-start | bytes 8260
  478.0 40.1 %all-to-all-start.4 = ((bf16[2,344,1024]{1,0,2:T(2,128)(2,1)}), bf16[2,344,1024]{1,0,2:T(2,128)(2,1)S(1)}, u32[]{:S(2)}, u32[]{:S(2)}) async-start(bf16[2,344,1024]{1,0,2:T(2,128)(2,1)} %copy.91), calls=%async_computation.4 | async-start | bytes 3145728 | tf_op jit(solution)/shard_map/all_to_all | solution.py:279
  662.8 7.2 copy-start.12
  788.6 9.3 copy-start.22
  788.6 9.3 copy-start.24
  793.5 37.4 %all-to-all-start.7 = ((bf16[2,1376,256]{2,0,1:T(2,128)(2,1)}), bf16[2,1376,256]{2,0,1:T(2,128)(2,1)}, u32[]{:S(2)}, u32[]{:S(2)}) async-start(bf16[2,1376,256]{2,0,1:T(2,128)(2,1)} %copy.104), calls=%async_computation.7 | async-start | bytes 2818048 | tf_op jit(solution)/shard_map/all_to_all | solution.py:290
  797.9 152.7 %reduce-scatter.7.cloned.1.call-start = ((), (), s32[]{:S(2)}) async-start(), calls=%async_computation.17 | async-start | bytes 4718592 | tf_op jit(solution)/shard_map/reduce_scatter | solution.py:305
  803.1 31.4 %copy-start.15 = (bf16[2,1376,256]{1,2,0:T(8,128)(2,1)S(1)}, bf16[2,1376,256]{1,2,0:T(8,128)(2,1)}, u32[]{:S(2)}) copy-start(bf16[2,1376,256]{1,2,0:T(8,128)(2,1)} %get-tuple-element.113) | copy-start | bytes 4227076
  830.9 36.5 %all-to-all-start.5 = ((bf16[2,1376,256]{2,0,1:T(2,128)(2,1)}), bf16[2,1376,256]{2,0,1:T(2,128)(2,1)S(1)}, u32[]{:S(2)}, u32[]{:S(2)}) async-start(bf16[2,1376,256]{2,0,1:T(2,128)(2,1)} %copy.98), calls=%async_computation.5 | async-start | bytes 2818048 | tf_op jit(solution)/shard_map/all_to_all | solution.py:284
  867.4 37.4 %all-to-all-start.6 = ((bf16[2,1376,256]{2,0,1:T(2,128)(2,1)}), bf16[2,1376,256]{2,0,1:T(2,128)(2,1)}, u32[]{:S(2)}, u32[]{:S(2)}) async-start(bf16[2,1376,256]{2,0,1:T(2,128)(2,1)} %copy.101), calls=%async_computation.6 | async-start | bytes 2818048 | tf_op jit(solution)/shard_map/all_to_all | solution.py:287
  871.8 137.5 %reduce-scatter.5.cloned.1.call-start = ((), (), s32[]{:S(2)}) async-start(), calls=%async_computation.16 | async-start | bytes 14155776 | tf_op jit(solution)/shard_map/reduce_scatter | solution.py:302
  917.9 211.2 %reduce-scatter.9.cloned.1.call-start = ((), (), s32[]{:S(2)}) async-start(), calls=%async_computation.18 | async-start | bytes 18874368 | tf_op jit(solution)/shard_map/reduce_scatter | solution.py:312
  936.1 312.7 %reduce-scatter.11.cloned.1.call-start = ((), (), s32[]{:S(2)}) async-start(), calls=%async_computation.19 | async-start | bytes 18874368 | tf_op jit(solution)/shard_map/reduce_scatter | solution.py:314
  950.5 524.4 %all-reduce.17.cloned.1.call-start = ((), (), s32[]{:S(2)}) async-start(), calls=%async_computation.20 | async-start | bytes 12582912 | tf_op jit(solution)/shard_map/psum | solution.py:318
  1253.8 8.8 copy-start.47
  (46 other events, 155.3 us)
Sparse Core Ops, SparseCore 0:
  9.9 48.1 all-gather.15
  60.0 27.7 all-gather.17
  89.7 54.2 all-gather.19
  160.0 54.6 all-gather.21
  801.9 52.3 reduce-scatter.6
  918.0 91.2 reduce-scatter.4
  1012.8 116.1 reduce-scatter.8
  1132.6 116.1 reduce-scatter.10
  1251.4 223.3 all-reduce.16
where the time goes:
time: 1500 us; the launch traced here: 1490 us
  waiting for transfers between devices  677 us (45%)
  matrix products  420 us (28%)
  blocking collectives  176 us (12%)
  local copies, waits for them, and re-layouts  115 us (8%)
  other arithmetic  49.2 us (3%)
  starting transfers between devices  32.5 us (2%)
  between operations  18.9 us (1%)
    psum x1, waiting for transfers between devices, on_device(): grad_final = tuple(lax.psum(tuple(grad_parts), 'seq'))  160 us
    reduce_scatter x1, waiting for transfers between devices, on_device(): lax.psum_scatter(d_w_up, 'shard', scatter_dimension=0, tiled=True)  120 us
    reduce_scatter x1, waiting for transfers between devices, on_device(): lax.psum_scatter(d_w_down, 'shard', scatter_dimension=0, tiled=True)  120 us
    dot_general x4, matrix products, attend_backward(): jnp.einsum('hqk,qhd->khd', grad_scores, query_block, preferred_element_ty...  85.2 us
    dot_general x4, matrix products, attend_backward(): jnp.einsum('hqk,khd->qhd', grad_scores, key_heads, preferred_element_type...  82.2 us
    reduce_scatter x1, waiting for transfers between devices, on_device(): lax.psum_scatter(d_w_qkv, 'shard', scatter_dimension=0, tiled=True)  58.7 us
    psum x1, blocking collectives, on_device(): lax.psum((jnp.sum(diff_rows * diff_rows), jnp.sum(live_mine)), ('shard',...  40.1 us
    all_to_all x1, waiting for transfers between devices, on_device(): lax.all_to_all(grad_mixed, 'seq', split_axis=2, concat_axis=1, tiled=True)  36.5 us
  transfers between devices with their start and end apart: 17, of which 12 were waited for; matrix products, arithmetic and copies ran while one was open for 15% of the time, Pallas kernels for 0%

commit v1 on v0

v1 whole, which is shorter than its diff:
```python
import jax
import jax.numpy as jnp
from jax import lax
from jax.experimental import pallas as pl
from jax.experimental.pallas import tpu as pltpu
from jax.sharding import PartitionSpec as P

HEAD_DIM = 64
DEAD = -1000000000.0
SPAN = 352
F32 = jnp.float32
BF16 = jnp.bfloat16
NT = (((1,), (1,)), ((), ()))


def lane_masks(dtype):
    lane = lax.broadcasted_iota(jnp.int32, (1, 2 * HEAD_DIM), 1)
    low = jnp.where(lane < HEAD_DIM, 1.0, 0.0).astype(F32)
    return low.astype(dtype), (1.0 - low).astype(dtype)


def forward_kernel(
    q_own, k_own, v_own, q_rec, k_rec, v_rec, bias_ref, o_own, o_rec, lse_ref, q_s, k_s, v_s, o_s, lse_s
):
    half = q_own.shape[0]
    for all_ref, own, rec in ((q_s, q_own, q_rec), (k_s, k_own, k_rec), (v_s, v_own, v_rec)):
        all_ref[:half, :] = own[...]
        all_ref[half:, :] = rec[...]
    masks = lane_masks(BF16)
    low, high = lane_masks(F32)
    bias = bias_ref[...]

    def block(idx, carry):
        row = pl.multiple_of(idx * SPAN, 16)
        query = q_s[pl.ds(row, SPAN), :]
        outs = []
        sums = []
        for mask in masks:
            scores = lax.dot_general(query * mask, k_s[...], NT, preferred_element_type=F32) + bias
            peak = jnp.max(scores, axis=-1, keepdims=True)
            weight = jnp.exp(scores - peak)
            total = jnp.sum(weight, axis=-1, keepdims=True)
            mixed = jnp.dot(weight.astype(BF16), v_s[...], preferred_element_type=F32)
            outs.append(mixed / total)
            sums.append(peak + jnp.log(total))
        o_s[pl.ds(row, SPAN), :] = (outs[0] * low + outs[1] * high).astype(BF16)
        lse_s[pl.ds(row, SPAN), :] = sums[0] * low + sums[1] * high
        return carry

    lax.fori_loop(0, 2 * half // SPAN, block, 0)
    o_own[...] = o_s[:half, :]
    o_rec[...] = o_s[half:, :]
    turned = jnp.transpose(lse_s[...])
    lse_ref[0, 0:8, :] = turned[0:8, :]
    lse_ref[0, 8:16, :] = turned[HEAD_DIM : HEAD_DIM + 8, :]


def backward_kernel(
    q_own,
    k_own,
    v_own,
    q_rec,
    k_rec,
    v_rec,
    g_own,
    g_rec,
    o_own,
    o_rec,
    lse_ref,
    bias_ref,
    dq_own,
    dk_own,
    dv_own,
    dq_rec,
    dk_rec,
    dv_rec,
    q_s,
    k_s,
    v_s,
    g_s,
    dqt_s,
    dk_s,
    dv_s,
):
    half = q_own.shape[0]
    low, high = lane_masks(BF16)
    for all_ref, own, rec in ((k_s, k_own, k_rec), (v_s, v_own, v_rec)):
        all_ref[:half, :] = own[...]
        all_ref[half:, :] = rec[...]
    for all_ref, own, rec in ((q_s, q_own, q_rec), (g_s, g_own, g_rec)):
        for head, mask in enumerate((low, high)):
            all_ref[head, :half, :] = own[...] * mask
            all_ref[head, half:, :] = rec[...] * mask
    dots_own = jnp.transpose(g_own[...].astype(F32) * o_own[...].astype(F32))
    dots_rec = jnp.transpose(g_rec[...].astype(F32) * o_rec[...].astype(F32))
    dots = jnp.concatenate([dots_own, dots_rec], axis=1)
    inner = (
        jnp.sum(dots[:HEAD_DIM], axis=0, keepdims=True),
        jnp.sum(dots[HEAD_DIM:], axis=0, keepdims=True),
    )
    dqt_s[...] = jnp.zeros_like(dqt_s)

    def block(idx, carry):
        row = pl.multiple_of(idx * SPAN, 16)
        key = k_s[pl.ds(row, SPAN), :]
        value = v_s[pl.ds(row, SPAN), :]
        bias = bias_ref[pl.ds(row, SPAN), :]
        key_t = jnp.transpose(key.astype(F32)).astype(BF16)
        dk = jnp.zeros((SPAN, 2 * HEAD_DIM), F32)
        dv = jnp.zeros((SPAN, 2 * HEAD_DIM), F32)
        for head in range(2):
            query = q_s[head]
            grad = g_s[head]
            lse = lse_ref[0, 8 * head : 8 * head + 1, :]
            prob = jnp.exp(
                lax.dot_general(key, query, NT, preferred_element_type=F32) + bias - lse
            )
            g_prob = lax.dot_general(value, grad, NT, preferred_element_type=F32)
            g_score = (prob * (g_prob - inner[head])).astype(BF16)
            dv = dv + jnp.dot(prob.astype(BF16), grad, preferred_element_type=F32)
            dk = dk + jnp.dot(g_score, query, preferred_element_type=F32)
            rows = slice(HEAD_DIM * head, HEAD_DIM * (head + 1))
            dqt_s[rows, :] += jnp.dot(key_t[rows, :], g_score, preferred_element_type=F32)
        dk_s[pl.ds(row, SPAN), :] = dk.astype(BF16)
        dv_s[pl.ds(row, SPAN), :] = dv.astype(BF16)
        return carry

    lax.fori_loop(0, 2 * half // SPAN, block, 0)
    dq = (jnp.transpose(dqt_s[...]) * HEAD_DIM ** (-0.5)).astype(BF16)
    dq_own[...] = dq[:half, :]
    dq_rec[...] = dq[half:, :]
    for all_ref, own, rec in ((dk_s, dk_own, dk_rec), (dv_s, dv_own, dv_rec)):
        own[...] = all_ref[:half, :]
        rec[...] = all_ref[half:, :]


def pair_blocks(half, pairs):
    wide = 2 * HEAD_DIM
    return [
        pl.BlockSpec((half, wide), lambda pair, part=part: (0, part * pairs + pair))
        for part in range(3)
    ]


def attention(own, rec, bias):
    half = own.shape[0]
    width = own.shape[1] // 3
    wide = 2 * HEAD_DIM
    pairs = width // wide
    full = 2 * half
    col = pl.BlockSpec((half, wide), lambda pair: (0, pair))
    ops = pairs * 2 * full * full
    return pl.pallas_call(
        forward_kernel,
        grid=(pairs,),
        in_specs=pair_blocks(half, pairs)
        + pair_blocks(half, pairs)
        + [pl.BlockSpec((1, full), lambda pair: (0, 0))],
        out_specs=[col, col, pl.BlockSpec((1, 16, full), lambda pair: (pair, 0, 0))],
        out_shape=[
            jax.ShapeDtypeStruct((half, width), BF16),
            jax.ShapeDtypeStruct((half, width), BF16),
            jax.ShapeDtypeStruct((pairs, 16, full), F32),
        ],
        scratch_shapes=[pltpu.VMEM((full, wide), BF16)] * 4 + [pltpu.VMEM((full, wide), F32)],
        cost_estimate=pl.CostEstimate(
            flops=ops * 4 * 256, transcendentals=ops, bytes_accessed=own.size * 6
        ),
        compiler_params=pltpu.CompilerParams(vmem_limit_bytes=56 * 1024 * 1024),
        name="attend",
    )(own, own, own, rec, rec, rec, bias.reshape(1, full))


def attention_back(own, rec, g_own, g_rec, o_own, o_rec, lse, bias):
    half = own.shape[0]
    width = own.shape[1] // 3
    wide = 2 * HEAD_DIM
    pairs = width // wide
    full = 2 * half
    col = pl.BlockSpec((half, wide), lambda pair: (0, pair))
    ops = pairs * 2 * full * full
    return pl.pallas_call(
        backward_kernel,
        grid=(pairs,),
        in_specs=pair_blocks(half, pairs)
        + pair_blocks(half, pairs)
        + [
            col,
            col,
            col,
            col,
            pl.BlockSpec((1, 16, full), lambda pair: (pair, 0, 0)),
            pl.BlockSpec((full, 1), lambda pair: (0, 0)),
        ],
        out_specs=[col] * 6,
        out_shape=[jax.ShapeDtypeStruct((half, width), BF16)] * 6,
        scratch_shapes=[
            pltpu.VMEM((2, full, wide), BF16),
            pltpu.VMEM((full, wide), BF16),
            pltpu.VMEM((full, wide), BF16),
            pltpu.VMEM((2, full, wide), BF16),
            pltpu.VMEM((wide, full), F32),
            pltpu.VMEM((full, wide), BF16),
            pltpu.VMEM((full, wide), BF16),
        ],
        cost_estimate=pl.CostEstimate(
            flops=ops * 10 * 256, transcendentals=ops, bytes_accessed=own.size * 12
        ),
        compiler_params=pltpu.CompilerParams(vmem_limit_bytes=56 * 1024 * 1024),
        name="attend_back",
    )(own, own, own, rec, rec, rec, g_own, g_rec, o_own, o_rec, lse, bias.reshape(full, 1))


def gelu_parts(values):
    phi_sum = 0.5 * (1.0 + lax.erf(values * 0.7071067811865476))
    phi = jnp.exp(-0.5 * values * values) * 0.3989422804014327
    return phi_sum, phi


def norm_parts(values):
    center = values - jnp.mean(values, axis=-1, keepdims=True)
    spread = jnp.mean(center * center, axis=-1, keepdims=True)
    scale = lax.rsqrt(spread + 1e-06)
    return center * scale, scale


def norm_back(values, gain, grad):
    unit, scale = norm_parts(values)
    scaled = grad * gain
    drift = jnp.mean(scaled, axis=-1, keepdims=True)
    slope = jnp.mean(scaled * unit, axis=-1, keepdims=True)
    back = scale * (scaled - drift - unit * slope)
    return back, jnp.sum(grad * unit, axis=0), jnp.sum(grad, axis=0)


def make_step(n_shard, n_seq):
    def place(shard, seq):
        return shard * n_seq + seq

    def route(turn):
        moves = []
        for shard in range(n_shard):
            for seq in range(n_seq):
                src = place(shard, seq)
                dst = place(
                    shard // 2 * 2 + seq % 2, 2 * (shard % 2) + (turn + seq // 2) % 2
                )
                moves.append((src, dst))
        return moves

    there = (route(0), route(1))
    back = tuple([(dst, src) for src, dst in moves] for moves in there)
    swap = [
        (place(shard, seq), place(shard ^ 1, seq))
        for shard in range(n_shard)
        for seq in range(n_seq)
    ]
    axes = ("shard", "seq")

    def on_device(
        inputs,
        teacher,
        cotangent,
        token_valid,
        image_real,
        w_qkv,
        q_bias,
        v_bias,
        w_out,
        out_bias,
        norm1_gain,
        norm1_bias,
        scale1,
        norm2_gain,
        norm2_bias,
        w_up,
        up_bias,
        w_down,
        down_bias,
        scale2,
    ):
        images, tok_dev, width = inputs.shape
        dl = q_bias.shape[0]
        ups = up_bias.shape[0] // dl
        ff = ups * width
        shard_pos = lax.axis_index("shard")
        seq_pos = lax.axis_index("seq")
        core = shard_pos % 2
        turn_out = seq_pos // 2
        turn_in = seq_pos % 2
        pad = SPAN - tok_dev
        rows = 2 * SPAN

        def bring(array):
            got = [
                lax.ppermute(
                    lax.dynamic_index_in_dim(array, (turn + turn_out) % 2, 0, keepdims=False),
                    axes,
                    there[turn],
                )
                for turn in range(2)
            ]
            first = jnp.where(turn_in == 0, got[0], got[1])
            second = jnp.where(turn_in == 0, got[1], got[0])
            both = jnp.stack([first, second])
            return jnp.pad(both, ((0, 0), (0, pad), (0, 0))).reshape(rows, array.shape[-1])

        def give(array):
            parts = array.reshape(2, SPAN, array.shape[-1])[:, :tok_dev]
            got = [
                lax.ppermute(
                    lax.dynamic_index_in_dim(parts, (turn + seq_pos) % 2, 0, keepdims=False),
                    axes,
                    back[turn],
                )
                for turn in range(2)
            ]
            first = jnp.where(turn_out == 0, got[0], got[1])
            second = jnp.where(turn_out == 0, got[1], got[0])
            return jnp.stack([first, second])

        def exchange(array):
            return lax.ppermute(array, axes, swap)

        lengths = jnp.sum(token_valid, axis=1) * image_real
        sizes = jnp.stack([lengths // 64, lengths % 64], axis=1).reshape(1, 2 * images)
        sizes = jnp.pad(sizes.astype(BF16), ((0, 0), (0, dl - 2 * images)))
        small = jnp.concatenate(
            [
                jnp.stack(
                    [
                        q_bias,
                        v_bias,
                        out_bias,
                        norm1_gain,
                        norm1_bias,
                        scale1,
                        norm2_gain,
                        norm2_bias,
                        down_bias,
                        scale2,
                    ]
                ),
                up_bias.reshape(ups, dl),
                sizes,
            ],
            axis=0,
        )
        vecs = lax.all_gather(small, "shard", axis=1, tiled=True).astype(F32)
        qbias, vbias, obias, gain1, shift1, layer1, gain2, shift2, dbias, layer2 = (
            vecs[i] for i in range(10)
        )
        ubias = (
            vecs[10 : 10 + ups].reshape(ups, n_shard, dl).transpose(1, 0, 2).reshape(ff)
        )
        tails = vecs[10 + ups].reshape(n_shard, dl)[:, : 2 * images].reshape(n_shard, images, 2)
        all_len = tails[:, :, 0] * 64.0 + tails[:, :, 1]
        count = jnp.sum(all_len)
        my_len = all_len.reshape(-1)[
            (shard_pos // 2 * 2 + seq_pos // 2) * images + seq_pos % 2
        ]

        slot = jnp.arange(rows)
        offset = slot % SPAN

        def live_of(which):
            token = (which + 2 * (slot // SPAN)) * tok_dev + offset
            return (offset < tok_dev) & (token.astype(F32) < my_len)

        live = live_of(core)
        live_all = jnp.concatenate([live, live_of(1 - core)])
        key_bias = jnp.where(live_all, 0.0, DEAD).astype(F32)
        live = live[:, None]

        qkv_mat = lax.all_gather(w_qkv, "shard", axis=0, tiled=True)
        out_mat = lax.all_gather(w_out, "shard", axis=0, tiled=True)
        up_mat = lax.all_gather(w_up, "shard", axis=0, tiled=True)
        down_mat = lax.all_gather(w_down, "shard", axis=0, tiled=True)

        x_rows = bring(inputs).astype(F32)
        normed1 = (norm_parts(x_rows)[0] * gain1 + shift1).astype(BF16)
        qkv_bias = jnp.concatenate([qbias, jnp.zeros_like(qbias), vbias])
        qkv = (jnp.dot(normed1, qkv_mat, preferred_element_type=F32) + qkv_bias).astype(BF16)
        teacher, cotangent, qkv = lax.optimization_barrier((teacher, cotangent, qkv))
        teach_rows = bring(teacher).astype(F32)
        cot_rows = bring(cotangent).astype(F32)
        head_cols = width // 2

        def parted(array, parts):
            array = array.reshape(rows, parts, 2, head_cols)
            left = array[:, :, 0].reshape(rows, parts * head_cols)
            right = array[:, :, 1].reshape(rows, parts * head_cols)
            return jnp.where(core == 0, left, right), jnp.where(core == 0, right, left)

        def joined(mine, other):
            return jnp.where(core == 0, mine, other), jnp.where(core == 0, other, mine)

        scale = jnp.concatenate(
            [jnp.full((width,), HEAD_DIM ** (-0.5), BF16), jnp.ones((2 * width,), BF16)]
        )
        own, away = parted(qkv * scale, 3)
        rec = exchange(away)
        o_own, o_rec, lse = attention(own, rec, key_bias)
        mixed = jnp.concatenate(joined(o_own, exchange(o_rec)), axis=1)
        attn_out = jnp.dot(mixed, out_mat, preferred_element_type=F32) + obias
        resid1 = x_rows + layer1 * attn_out
        normed2 = (norm_parts(resid1)[0] * gain2 + shift2).astype(BF16)
        pre = jnp.dot(normed2, up_mat, preferred_element_type=F32) + ubias
        act = (pre * gelu_parts(pre)[0]).astype(BF16)
        branch = jnp.dot(act, down_mat, preferred_element_type=F32) + dbias
        resid2 = resid1 + layer2 * branch
        out_rows = jnp.where(live, resid2, x_rows)
        diff = jnp.where(live, out_rows - teach_rows, 0.0)
        err = jnp.sum(diff * diff)
        result = give(out_rows.astype(BF16))

        g_out = cot_rows + 2.0 * diff / (count * width)
        g_keep = jnp.where(live, g_out, 0.0)
        g_pass = g_out - g_keep
        d_scale2 = jnp.sum(g_keep * branch, axis=0)
        g_branch = (g_keep * layer2).astype(BF16)
        d_down_bias = jnp.sum(g_branch.astype(F32), axis=0)

        def weight_grad(left, right):
            return jnp.einsum("ra,rb->ab", left, right, preferred_element_type=F32).astype(BF16)

        def scatter(array):
            return lax.psum_scatter(array, "shard", scatter_dimension=0, tiled=True)

        p_down = scatter(weight_grad(act, g_branch))
        g_hidden = jnp.einsum("rd,fd->rf", g_branch, down_mat, preferred_element_type=F32)
        phi_sum, phi = gelu_parts(pre)
        g_pre = (g_hidden * (phi_sum + pre * phi)).astype(BF16)
        d_up_bias = jnp.sum(g_pre.astype(F32), axis=0)
        p_up = scatter(weight_grad(normed2, g_pre))
        g_norm2 = jnp.einsum("rf,df->rd", g_pre, up_mat, preferred_element_type=F32)
        g_ln2, d_gain2, d_shift2 = norm_back(resid1, gain2, g_norm2)
        g_resid1 = g_keep + g_ln2
        d_scale1 = jnp.sum(g_resid1 * attn_out, axis=0)
        g_attn = (g_resid1 * layer1).astype(BF16)
        d_out_bias = jnp.sum(g_attn.astype(F32), axis=0)
        g_mixed = jnp.einsum("rd,cd->rc", g_attn, out_mat, preferred_element_type=F32).astype(BF16)
        g_mine, g_away = parted(g_mixed, 1)
        g_rec = exchange(g_away)
        p_out = scatter(weight_grad(mixed, g_attn))
        grads = attention_back(own, rec, g_mine, g_rec, o_own, o_rec, lse, key_bias)
        pieces = []
        for part in range(3):
            pieces.extend(joined(grads[part], exchange(grads[3 + part])))
        g_qkv = jnp.concatenate(pieces, axis=1)
        p_qkv = scatter(weight_grad(normed1, g_qkv))
        d_qkv_bias = jnp.sum(g_qkv.astype(F32), axis=0)
        g_norm1 = jnp.einsum("re,de->rd", g_qkv, qkv_mat, preferred_element_type=F32)
        g_ln1, d_gain1, d_shift1 = norm_back(x_rows, gain1, g_norm1)
        g_in = give((g_pass + g_resid1 + g_ln1).astype(BF16)).astype(F32)

        p_down, p_up, p_out = lax.psum((p_down, p_up, p_out), "seq")
        p_qkv = lax.psum(p_qkv, "seq")
        sums = jnp.concatenate(
            [
                jnp.stack(
                    [
                        d_qkv_bias[:width],
                        d_qkv_bias[2 * width :],
                        d_out_bias,
                        d_gain1,
                        d_shift1,
                        d_scale1,
                        d_gain2,
                        d_shift2,
                        d_down_bias,
                        d_scale2,
                    ]
                ),
                d_up_bias.reshape(n_shard, ups, dl).transpose(1, 0, 2).reshape(ups, width),
                jnp.full((1, width), err),
            ],
            axis=0,
        )
        sums = lax.psum(sums, axes)
        loss = sums[10 + ups, 0] / (count * width)
        mine = lax.dynamic_slice_in_dim(sums, shard_pos * dl, dl, 1)
        (
            s_qb, s_vb, s_ob, s_g1, s_b1, s_l1, s_g2, s_b2, s_db, s_l2
        ) = (mine[i] for i in range(10))
        s_ub = mine[10 : 10 + ups].reshape(ups * dl)
        return (
            result,
            loss,
            g_in,
            p_qkv.astype(F32),
            s_qb,
            s_vb,
            p_out.astype(F32),
            s_ob,
            s_g1,
            s_b1,
            s_l1,
            s_g2,
            s_b2,
            p_up.astype(F32),
            s_ub,
            p_down.astype(F32),
            s_db,
            s_l2,
        )

    return on_device


def solution(mesh):
    tokens = P("shard", "seq", None)
    matrix = P("shard", None)
    vector = P("shard")
    in_specs = (
        tokens,
        tokens,
        tokens,
        matrix,
        vector,
        matrix,
        vector,
        vector,
        matrix,
        vector,
        vector,
        vector,
        vector,
        vector,
        vector,
        matrix,
        vector,
        matrix,
        vector,
        vector,
    )
    out_specs = (
        tokens,
        P(),
        tokens,
        matrix,
        vector,
        vector,
        matrix,
        vector,
        vector,
        vector,
        vector,
        vector,
        vector,
        matrix,
        vector,
        matrix,
        vector,
        vector,
    )
    return jax.shard_map(
        make_step(mesh.shape["shard"], mesh.shape["seq"]),
        mesh=mesh,
        in_specs=in_specs,
        out_specs=out_specs,
        check_vma=False,
    )
```

time: 1500 us -> 772 us (0.51)
  waiting for transfers between devices: 677 us -> 280 us
  matrix products: 420 us -> 114 us
  Pallas kernels: 0 us -> 88.5 us
  blocking collectives: 176 us -> 98.1 us
  local copies, waits for them, and re-layouts: 115 us -> 78.4 us
    dot_general x40 -> x12, matrix products: 420 us -> 114 us  [the longest x4 34.3 us: weight_grad(): jnp.einsum('ra,rb->ab', left, right, preferred_element_type=F32)]
    all_to_all x8 -> x0, waiting for transfers between devices: 189 us -> none  [the longest x1 36.5 us: on_device(): lax.all_to_all(grad_mixed, 'seq', split_axis=2, concat_axis=1, tiled=True)]
    psum x1, waiting for transfers between devices: 160 us -> 43.2 us  [on_device(): p_qkv = lax.psum(p_qkv, 'seq')]
    reduce_scatter x4, waiting for transfers between devices: 298 us -> 193 us  [scatter(): return lax.psum_scatter(array, 'shard', scatter_dimension=0, tiled=True)]
    pallas_call x0 -> x2, Pallas kernels: none -> 88.5 us  [the longest x1 49.8 us: attention_back(): pl.pallas_call(backward_kernel, grid=(pairs,), in_specs=pair_blocks(half,...]
    all_gather x11 -> x1, blocking collectives: 95.1 us -> 10.7 us  [on_device(): vecs = lax.all_gather(small, 'shard', axis=1, tiled=True).astype(F32)]
    ppermute x0 -> x16, waiting for transfers between devices: none -> 37.7 us  [the longest x6 20.3 us: bring(): lax.ppermute(lax.dynamic_index_in_dim(array, (turn + turn_out) % 2, 0, ke...]
    ppermute x0 -> x16, starting transfers between devices: none -> 34.5 us  [the longest x6 18.8 us: bring(): lax.ppermute(lax.dynamic_index_in_dim(array, (turn + turn_out) % 2, 0, ke...]
  transfers between devices with their start and end apart: 17 -> 25, of which waited for: 12 -> 9; matrix products, arithmetic and copies ran while one was open for 15% -> 22% of each run, Pallas kernels for 0% -> 5%
where the time goes in v1:
time: 772 us; the launch traced here: 762 us
  waiting for transfers between devices  280 us (36%)
  matrix products  114 us (15%)
  blocking collectives  98.1 us (13%)
  Pallas kernels  88.5 us (11%)
  local copies, waits for them, and re-layouts  78.4 us (10%)
  other arithmetic  50.6 us (7%)
  starting transfers between devices  34.8 us (5%)
  between operations  17.7 us (2%)
    reduce_scatter x4, waiting for transfers between devices, scatter(): return lax.psum_scatter(array, 'shard', scatter_dimension=0, tiled=True)  193 us
    psum x1, blocking collectives, on_device(): sums = lax.psum(sums, axes)  87.4 us
    pallas_call x1, Pallas kernels, attention_back(): pl.pallas_call(backward_kernel, grid=(pairs,), in_specs=pair_blocks(half,...  49.8 us
    psum x1, waiting for transfers between devices, on_device(): p_qkv = lax.psum(p_qkv, 'seq')  43.2 us
    pallas_call x1, Pallas kernels, attention(): pl.pallas_call(forward_kernel, grid=(pairs,), in_specs=pair_blocks(half,...  38.7 us
    dot_general x4, matrix products, weight_grad(): jnp.einsum('ra,rb->ab', left, right, preferred_element_type=F32)  34.3 us
    unnamed x112, local copies, waits for them, and re-layouts  32.4 us
    ppermute x6, waiting for transfers between devices, bring(): lax.ppermute(lax.dynamic_index_in_dim(array, (turn + turn_out) % 2, 0, ke...  20.3 us
  transfers between devices with their start and end apart: 25, of which 9 were waited for; matrix products, arithmetic and copies ran while one was open for 22% of the time, Pallas kernels for 5%

profile of v1, /device:TPU:0, one launch (start us, length us, event | category | flops | bytes accessed | tf_op | source)
XLA Modules:
  0.0 762.0 jit_solution(13229530777064006958)
XLA Ops:
  11.0 4.3 collective-permute-start.1
  17.2 10.7 %all_gather.15 = bf16[15,1024]{1,0:T(8,128)(2,1)S(1)} all-gather(bf16[15,128]{1,0:T(8,128)(2,1)S(1)} %concatenate.42), channel_id=1, replica_groups=mesh['shard'=8,'seq'=4] {'shard'}, dimensions={1}, use_global_device_ids=true | all-gather | bytes 34560 | tf_op jit(solution)/shard_map/all_gather | solution.py:349
  29.1 19.4 %collective-permute-done.1 = bf16[344,1024]{1,0:T(8,128)(2,1)} collective-permute-done((bf16[344,1024]{1,0:T(8,128)(2,1)S(1)}, bf16[344,1024]{1,0:T(8,128)(2,1)}, u32[]{:S(2)}, u32[]{:S(2)}) %collective-permute-start.1) | collective-permute-done | bytes 704544 | tf_op jit(solution)/shard_map/ppermute | solution.py:296
  52.7 2.0 add_convert_fusion.2
  54.7 3.5 all-gather.5.cloned.1.call-done
  58.2 7.9 %add_convert_fusion = bf16[704,3072]{1,0:T(8,128)(2,1)S(1)} fusion(bf16[704,1024]{1,0:T(8,128)(2,1)} %add_convert_fusion.2, bf16[1024,3072]{1,0:T(8,128)(2,1)} %all-gather.5.cloned.1.call-done, f32[3072]{0:T(1024)S(1)} %copy-done.39), kind=kOutput, calls=%fused_computation.11 | convolution fusion | flops 4433510400 | bytes 12070912 | tf_op jit(solution)/shard_map/dot_general | solution.py:383
  66.1 2.3 broadcast_multiply_fusion
  68.4 7.9 %reshape.243 = bf16[704,3,2,512]{3,2,1,0:T(2,128)(2,1)} reshape(bf16[704,3072]{1,0:T(8,128)(2,1)} %broadcast_multiply_fusion) | data formatting | bytes 8650752 | tf_op jit(solution)/shard_map/reshape | solution.py:390
  76.3 10.1 %fusion.41 = (bf16[704,3,1,512]{3,2,1,0:T(2,128)(2,1)}, bf16[704,3,1,512]{3,2,1,0:T(2,128)(2,1)}) fusion(bf16[704,3,2,512]{3,2,1,0:T(2,128)(2,1)} %reshape.243), kind=kLoop, calls=%fused_computation.152 | loop fusion | bytes 8650752 | tf_op jit(solution)/shard_map/slice | solution.py:392
  86.4 11.7 %copy.74 = bf16[704,3,1,512]{0,3,1,2:T(8,128)(2,1)} copy(bf16[704,3,1,512]{3,2,1,0:T(2,128)(2,1)} %get-tuple-element.70) | data formatting | bytes 4325376
  98.0 11.7 %copy.73 = bf16[704,3,1,512]{0,3,1,2:T(8,128)(2,1)} copy(bf16[704,3,1,512]{3,2,1,0:T(2,128)(2,1)} %get-tuple-element.71) | data formatting | bytes 4325376
  109.8 4.8 broadcast_select_fusion
  114.6 4.3 copy.63
  122.6 2.5 dynamic-slice_bitcast_fusion.3
  125.1 6.8 collective-permute-start.8
  133.1 7.0 collective-permute-start.6
  140.1 4.2 copy.64.q_own.k_own.v_own
  144.3 38.7 %attend.1 = (bf16[704,512]{1,0:T(8,128)(2,1)}, bf16[704,512]{1,0:T(8,128)(2,1)}, f32[4,16,1408]{2,1,0:T(8,128)}) custom-call(bf16[704,1536]{1,0:T(8,128)(2,1)} %copy.64.q_own.k_own.v_own, bf16[704,1536]{1,0:T(8,128)(2,1)} %copy.64.q_own.k_own.v_own, bf16[704,1536]{1,0:T(8,128)(2,1)} %copy.64.q_own.k_own.v_own, ...), custom_call_target="tpu_custom_call" | custom-call | flops 16240345088 | bytes 6488064 | tf_op jit(solution)/shard_map/attend/pallas_call | solution.py:153
  184.7 2.0 select_bitcast_fusion.5
  189.1 2.4 broadcast_select_fusion.3
  191.5 6.2 multiply_add_fusion
  197.7 2.1 reduce_sum.208
  199.8 2.2 multiply_reduce_fusion.6
  202.1 13.8 %multiply_convert_fusion = (bf16[704,4096]{1,0:T(8,128)(2,1)}, f32[704,4096]{1,0:T(8,128)}) fusion(f32[4096]{0:T(1024)S(1)} %bitcast.181, bf16[1024,4096]{1,0:T(8,128)(2,1)} %all-gather.9.cloned.1.call-done, f32[704,1024]{1,0:T(8,128)} %get-tuple-element.121, f32[1024]{0:T(1024)S(1)} %bitcast.193, f32[1024]{0:T(1024)S(1)} %bitcast.168, ...), kind=kOutput, calls=%fused_computation.8 | convolution fusion | flops 5926486016 | bytes 28603904 | tf_op jit(solution)/shard_map/dot_general | solution.py:408
  215.9 14.0 %multiply_reduce_fusion.1 = (f32[]{:T(128)}, f32[1024]{0:T(1024)}, f32[704,1024]{1,0:T(8,128)S(1)}, bf16[704,1024]{1,0:T(8,128)(2,1)}) fusion(bf16[2,352,1024]{2,1,0:T(8,128)(2,1)} %fusion.21, pred[704]{0:T(1024)(128)(4,1)S(1)} %fusion.30, f32[1024]{0:T(1024)S(1)} %bitcast.198, f32[]{:T(128)S(6)} %mul.314, bf16[2,352,1024]{2,1,0:T(8,128)(2,1)} %fusion.20, ...), kind=kOutput, calls=%fused_computation.35 | convolution fusion | flops 5917834240 | bytes 27144904 | tf_op jit(solution)/shard_map/dot_general | solution.py:410
  231.0 16.8 %convert_reduce_fusion = (f32[4096]{0:T(1024)S(1)}, bf16[704,4096]{1,0:T(8,128)(2,1)}) fusion(f32[704,4096]{1,0:T(8,128)} %get-tuple-element.124, f32[4096]{0:T(1024)S(1)} %bitcast.182, bf16[704,1024]{1,0:T(8,128)(2,1)S(1)} %get-tuple-element.59, bf16[4096,1024]{1,0:T(8,128)(2,1)} %all-gather.11.cloned.1.call-done), kind=kOutput, calls=%fused_computation.7 | convolution fusion | flops 5943062528 | bytes 27164672 | tf_op jit(solution)/shard_map/rd,fd->rf/dot_general | solution.py:431
  247.9 9.5 %multiply_reduce_fusion.2 = (f32[1024]{0:T(1024)S(1)}, f32[704]{0:T(1024)S(1)}, f32[704]{0:T(1024)S(1)}, f32[1024]{0:T(1024)S(1)}, f32[704,1024]{1,0:T(8,128)S(1)}) fusion(f32[704,1024]{1,0:T(8,128)S(1)} %copy-done.2, f32[704]{0:T(1024)S(1)} %add_rsqrt_fusion, f32[704]{0:T(1024)S(1)} %broadcast_multiply_fusion.5, f32[1024]{0:T(1024)S(1)} %bitcast.169, ...), kind=kOutput, calls=%fused_computation.37 | convolution fusion | flops 5912065024 | bytes 19946496 | tf_op jit(solution)/shard_map/rf,df->rd/dot_general | solution.py:436
  262.1 2.8 convolution_convert_fusion.4
  265.0 4.9 reshape.246
  269.8 4.3 fusion.42
  277.9 49.8 %attend_back.1 = (bf16[704,512]{1,0:T(8,128)(2,1)}, bf16[704,512]{1,0:T(8,128)(2,1)}, bf16[704,512]{1,0:T(8,128)(2,1)}, bf16[704,512]{1,0:T(8,128)(2,1)}, bf16[7...) custom-call(bf16[704,1536]{1,0:T(8,128)(2,1)} %copy.64.q_own.k_own.v_own, bf16[704,1536]{1,0:T(8,128)(2,1)} %copy.64.q_own.k_own.v_own, ...), custom_call_target="tpu_custom_call" | custom-call | flops 40600862720 | bytes 12976128 | tf_op jit(solution)/shard_map/attend_back/pallas_call | solution.py:182
  328.0 3.2 convolution_convert_fusion.3
  335.4 2.1 copy-done.9
  337.5 7.3 convolution_convert_fusion.2
  344.8 12.2 %convolution_convert_fusion.1 = bf16[1024,4096]{1,0:T(8,128)(2,1)} fusion(bf16[704,4096]{1,0:T(8,128)(2,1)} %get-tuple-element.127, f32[704,1024]{1,0:T(8,128)S(1)} %copy-done.2, f32[1024]{0:T(1024)S(1)} %bitcast.194, f32[1024]{0:T(1024)S(1)} %bitcast.171, f32[704]{0:T(1024)S(1)} %add_rsqrt_fusion, f32[704]{0:T(1024)S(1)} %broadcast_multiply_fusion.5), kind=kOutput, calls=%fused_computation.13 | convolution fusion | flops 5913378816 | bytes 17053184 | tf_op jit(solution)/shard_map/ra,rb->ab/dot_general | solution.py:425
  358.5 11.7 %convolution_convert_fusion = bf16[4096,1024]{1,0:T(8,128)(2,1)} fusion(bf16[704,4096]{1,0:T(8,128)(2,1)} %get-tuple-element.123, bf16[704,1024]{1,0:T(8,128)(2,1)S(1)} %copy-done.14), kind=kOutput, calls=%fused_computation.12 | convolution fusion | flops 5909774336 | bytes 15597568 | tf_op jit(solution)/shard_map/ra,rb->ab/dot_general | solution.py:425
  372.4 9.4 %collective-permute-start.5 = (bf16[344,1024]{1,0:T(8,128)(2,1)S(1)}, bf16[344,1024]{1,0:T(8,128)(2,1)S(1)}, u32[]{:S(2)}, u32[]{:S(2)}) collective-permute-start(bf16[344,1024]{1,0:T(8,128)(2,1)S(1)} %get-tuple-element.85), channel_id=1, source_target_pairs={{1,0},{5,1},{0,2},{4,3},{3,4},{7,5},{2,6},{6,7},{9,8},{13,9},{8,10... | collective-permute-start | bytes 2113544 | tf_op jit(solution)/shard_map/ppermute | solution.py:311
  381.8 16.2 %collective-permute-done.5 = bf16[344,1024]{1,0:T(8,128)(2,1)S(1)} collective-permute-done((bf16[344,1024]{1,0:T(8,128)(2,1)S(1)}, bf16[344,1024]{1,0:T(8,128)(2,1)S(1)}, u32[]{:S(2)}, u32[]{:S(2)}) %collective-permute-start.5) | collective-permute-done | bytes 704544 | tf_op jit(solution)/shard_map/ppermute | solution.py:311
  399.4 43.0 %reduce-scatter.5.cloned.1.call-done = bf16[128,3072]{1,0:T(8,128)(2,1)} async-done(((bf16[1024,3072]{1,0:T(8,128)(2,1)}), bf16[128,3072]{1,0:T(8,128)(2,1)}) %reduce-scatter.5.cloned.1.call-update) | async-done | bytes 786448 | tf_op jit(solution)/shard_map/reduce_scatter | solution.py:428
  442.4 75.0 %reduce-scatter.9.cloned.1.call-done = bf16[128,4096]{1,0:T(8,128)(2,1)} async-done(((bf16[1024,4096]{1,0:T(8,128)(2,1)}), bf16[128,4096]{1,0:T(8,128)(2,1)}) %reduce-scatter.9.cloned.1.call-update) | async-done | bytes 1048592 | tf_op jit(solution)/shard_map/reduce_scatter | solution.py:428
  517.4 75.0 %reduce-scatter.11.cloned.1.call-done = bf16[512,1024]{1,0:T(8,128)(2,1)} async-done(((bf16[4096,1024]{1,0:T(8,128)(2,1)}), bf16[512,1024]{1,0:T(8,128)(2,1)}) %reduce-scatter.11.cloned.1.call-update) | async-done | bytes 1048592 | tf_op jit(solution)/shard_map/reduce_scatter | solution.py:428
  592.5 8.5 %fusion.45 = f32[704,1024]{1,0:T(8,128)S(1)} fusion(bf16[704,3072]{1,0:T(8,128)(2,1)} %copy-done.9, bf16[1024,3072]{1,0:T(8,128)(2,1)} %all-gather.5.cloned.1.call-done), kind=kOutput, calls=%fused_computation.156 | convolution fusion | flops 4429185024 | bytes 13500416 | tf_op jit(solution)/shard_map/re,de->rd/dot_general | solution.py:453
  606.1 3.8 collective-permute-start.15
  611.5 87.4 %psum.35 = f32[15,1024]{1,0:T(8,128)S(1)} all-reduce(f32[15,1024]{1,0:T(8,128)S(1)} %concatenate.52), channel_id=1, replica_groups=mesh['shard'=8,'seq'=4] {'shard','seq'}, use_global_device_ids=true, to_apply=%region_19.20 | all-reduce | flops 15360 | bytes 122880 | tf_op jit(solution)/shard_map/psum | solution.py:480
  701.5 1.7 maximum_convert_fusion
  703.2 43.2 %all-reduce.7.cloned.1.call-done = (bf16[128,3072]{1,0:T(8,128)(2,1)}, bf16[128,1024]{1,0:T(8,128)(2,1)}, bf16[128,4096]{1,0:T(8,128)(2,1)}, bf16[512,1024]{1,0:T(8,128)(2,1)}) async-done(((bf16[128,3072]{1,0:T(8,128)(2,1)}, bf16[128,1024]{1,0:T(8,128)(2,1)}, bf16[128,4096]{1,0:T(8,128)(2,1)}, bf16[512,1024]{1,0:T(8,128)(2,1)}), (bf16[128,3072]{1,0:T(8,128)(2,1)}, bf16[128,1024]{1,0:T(8,128)(2,1)}, ...) | async-done | bytes 3145744 | tf_op jit(solution)/shard_map/psum | solution.py:458
  746.4 2.6 convert_element_type.173
  749.0 1.8 convert_element_type.175
  (231 shorter events, 49.7 us)
Async XLA Ops:
  7.2 8.2 %copy-start.46 = (s32[2]{0:T(128)S(1)}, s32[2]{0:T(128)}, u32[]{:S(2)}) copy-start(s32[2]{0:T(128)} %param.24) | copy-start | bytes 28
  7.2 8.5 %copy-start.47 = (bf16[128]{0:T(256)(128)(2,1)S(1)}, bf16[128]{0:T(256)(128)(2,1)}, u32[]{:S(2)}) copy-start(bf16[128]{0:T(256)(128)(2,1)} %param.26) | copy-start | bytes 772
  7.2 8.5 %copy-start.48 = (bf16[128]{0:T(256)(128)(2,1)S(1)}, bf16[128]{0:T(256)(128)(2,1)}, u32[]{:S(2)}) copy-start(bf16[128]{0:T(256)(128)(2,1)} %param.27) | copy-start | bytes 772
  7.2 8.5 %copy-start.49 = (bf16[128]{0:T(256)(128)(2,1)S(1)}, bf16[128]{0:T(256)(128)(2,1)}, u32[]{:S(2)}) copy-start(bf16[128]{0:T(256)(128)(2,1)} %param.29) | copy-start | bytes 772
  7.3 8.5 %copy-start.45 = (bf16[512]{0:T(512)(128)(2,1)S(1)}, bf16[512]{0:T(512)(128)(2,1)}, u32[]{:S(2)}) copy-start(bf16[512]{0:T(512)(128)(2,1)} %param.36) | copy-start | bytes 3076
  7.3 50.9 %all-gather.5.cloned.1.call-start = ((), (), s32[]{:S(2)}) async-start(), calls=%async_computation.4 | async-start | bytes 7077888 | tf_op jit(solution)/shard_map/all_gather | solution.py:375
  8.0 183.5 %all-gather.7.cloned.1.call-start = ((), (), s32[]{:S(2)}) async-start(), calls=%async_computation.5 | async-start | bytes 2359296 | tf_op jit(solution)/shard_map/all_gather | solution.py:376
  8.7 193.3 %all-gather.9.cloned.1.call-start = ((), (), s32[]{:S(2)}) async-start(), calls=%async_computation.6 | async-start | bytes 9437184 | tf_op jit(solution)/shard_map/all_gather | solution.py:377
  9.5 206.4 %all-gather.11.cloned.1.call-start = ((), (), s32[]{:S(2)}) async-start(), calls=%async_computation.7 | async-start | bytes 9437184 | tf_op jit(solution)/shard_map/all_gather | solution.py:378
  10.1 389.3 %reduce-scatter.7.cloned.1.call-start = ((), (), s32[]{:S(2)}) async-start(), calls=%async_computation.9 | async-start | bytes 2359296 | tf_op jit(solution)/shard_map/reduce_scatter | solution.py:428
  10.3 18.8 %collective-permute-start = (bf16[344,1024]{1,0:T(8,128)(2,1)S(1)}, bf16[344,1024]{1,0:T(8,128)(2,1)S(1)}, u32[]{:S(2)}, u32[]{:S(2)}) collective-permute-start(bf16[344,1024]{1,0:T(8,128)(2,1)S(1)} %get-tuple-element.96), channel_id=1, source_target_pairs={{0,0},{1,4},{2,1},{3,5},{4,2},{5,6},{6,3},{7,7},{8,8},{9,12},{10,9... | collective-permute-start | bytes 2113544 | tf_op jit(solution)/shard_map/ppermute | solution.py:296
  11.0 37.5 %collective-permute-start.1 = (bf16[344,1024]{1,0:T(8,128)(2,1)S(1)}, bf16[344,1024]{1,0:T(8,128)(2,1)}, u32[]{:S(2)}, u32[]{:S(2)}) collective-permute-start(bf16[344,1024]{1,0:T(8,128)(2,1)S(1)} %get-tuple-element.97), channel_id=1, source_target_pairs={{0,1},{1,5},{2,0},{3,4},{4,3},{5,7},{6,2},{7,6},{8,9},{9,13},{10,8... | collective-permute-start | bytes 2113544 | tf_op jit(solution)/shard_map/ppermute | solution.py:296
  52.7 163.2 %copy-start = (f32[2,352,1024]{2,1,0:T(8,128)}, f32[2,352,1024]{2,1,0:T(8,128)S(1)}, u32[]{:S(2)}) copy-start(f32[2,352,1024]{2,1,0:T(8,128)S(1)} %fusion.19) | copy-start | bytes 8650756
  54.7 11.3 %copy-start.41 = (bf16[3072]{0:T(1024)(128)(2,1)S(1)}, bf16[3072]{0:T(1024)(128)(2,1)}, u32[]{:S(2)}) copy-start(bf16[3072]{0:T(1024)(128)(2,1)} %constant.178.clone.1) | copy-start | bytes 18436
  118.9 25.4 %collective-permute-start.2 = (bf16[704,1536]{1,0:T(8,128)(2,1)}, bf16[704,1536]{1,0:T(8,128)(2,1)}, u32[]{:S(2)}, u32[]{:S(2)}) collective-permute-start(bf16[704,1536]{1,0:T(8,128)(2,1)} %copy.63), channel_id=1, source_target_pairs={{0,4},{1,5},{2,6},{3,7},{4,0},{5,1},{6,2},{7,3},{8,12},{9,13},{10,... | collective-permute-start | bytes 6488072 | tf_op jit(solution)/shard_map/ppermute | solution.py:323
  120.0 11.9 %copy-start.19 = (bf16[2,344,1024]{2,1,0:T(8,128)(2,1)S(1)}, bf16[2,344,1024]{2,1,0:T(8,128)(2,1)}, u32[]{:S(2)}) copy-start(bf16[2,344,1024]{2,1,0:T(8,128)(2,1)} %param.22) | copy-start | bytes 4227076
  125.1 58.6 %collective-permute-start.8 = (bf16[344,1024]{1,0:T(8,128)(2,1)}, bf16[344,1024]{1,0:T(8,128)(2,1)}, u32[]{:S(2)}, u32[]{:S(2)}) collective-permute-start(bf16[344,1024]{1,0:T(8,128)(2,1)} %get-tuple-element.92), channel_id=1, source_target_pairs={{0,0},{1,4},{2,1},{3,5},{4,2},{5,6},{6,3},{7,7},{8,8},{9,12},{10,9... | collective-permute-start | bytes 2113544 | tf_op jit(solution)/shard_map/ppermute | solution.py:296
  131.9 51.9 %collective-permute-start.9 = (bf16[344,1024]{1,0:T(8,128)(2,1)}, bf16[344,1024]{1,0:T(8,128)(2,1)}, u32[]{:S(2)}, u32[]{:S(2)}) collective-permute-start(bf16[344,1024]{1,0:T(8,128)(2,1)} %get-tuple-element.93), channel_id=1, source_target_pairs={{0,1},{1,5},{2,0},{3,4},{4,3},{5,7},{6,2},{7,6},{8,9},{9,13},{10,8... | collective-permute-start | bytes 2113544 | tf_op jit(solution)/shard_map/ppermute | solution.py:296
  133.1 51.6 %collective-permute-start.7 = (bf16[344,1024]{1,0:T(8,128)(2,1)}, bf16[344,1024]{1,0:T(8,128)(2,1)}, u32[]{:S(2)}, u32[]{:S(2)}) collective-permute-start(bf16[344,1024]{1,0:T(8,128)(2,1)} %get-tuple-element.89), channel_id=1, source_target_pairs={{0,1},{1,5},{2,0},{3,4},{4,3},{5,7},{6,2},{7,6},{8,9},{9,13},{10,8... | collective-permute-start | bytes 2113544 | tf_op jit(solution)/shard_map/ppermute | solution.py:296
  133.1 51.6 %collective-permute-start.6 = (bf16[344,1024]{1,0:T(8,128)(2,1)}, bf16[344,1024]{1,0:T(8,128)(2,1)}, u32[]{:S(2)}, u32[]{:S(2)}) collective-permute-start(bf16[344,1024]{1,0:T(8,128)(2,1)} %get-tuple-element.88), channel_id=1, source_target_pairs={{0,0},{1,4},{2,1},{3,5},{4,2},{5,6},{6,3},{7,7},{8,8},{9,12},{10,9... | collective-permute-start | bytes 2113544 | tf_op jit(solution)/shard_map/ppermute | solution.py:296
  183.0 6.1 collective-permute-start.3
  202.1 13.8 %copy-start.35 = (f32[1,1024]{1,0:T(1,128)S(1)}, f32[1,1024]{1,0:T(1,128)}, u32[]{:S(2)}) copy-start(f32[1,1024]{1,0:T(1,128)} %get-tuple-element.108) | copy-start | bytes 12292
  202.1 13.8 %copy-start.44 = (f32[1,1024]{1,0:T(1,128)S(1)}, f32[1,1024]{1,0:T(1,128)}, u32[]{:S(2)}) copy-start(f32[1,1024]{1,0:T(1,128)} %get-tuple-element.109) | copy-start | bytes 12292
  229.9 27.4 %copy-start.3 = (f32[704,1024]{1,0:T(8,128)}, f32[704,1024]{1,0:T(8,128)S(1)}, u32[]{:S(2)}) copy-start(f32[704,1024]{1,0:T(8,128)S(1)} %get-tuple-element.56) | copy-start | bytes 8650756
  229.9 17.9 %slice-start.2 = ((s8[8388608]{0:T(1024)(128)(4,1)}), s8[4194304]{0:T(1024)(128)(4,1)S(1)}, s32[]{:S(2)}) async-start(s8[8388608]{0:T(1024)(128)(4,1)} %bitcast.210), calls=%async_computation.15 | async-start | bytes 8388608
  231.0 16.9 %copy-start.13 = (bf16[704,1024]{1,0:T(8,128)(2,1)}, bf16[704,1024]{1,0:T(8,128)(2,1)S(1)}, u32[]{:S(2)}) copy-start(bf16[704,1024]{1,0:T(8,128)(2,1)S(1)} %get-tuple-element.59) | copy-start | bytes 4325380
  231.0 16.9 %copy-start.2 = (f32[704,1024]{1,0:T(8,128)S(1)}, f32[704,1024]{1,0:T(8,128)}, u32[]{:S(2)}) copy-start(f32[704,1024]{1,0:T(8,128)} %get-tuple-element.121) | copy-start | bytes 8650756
  231.0 16.9 %slice-start.3 = ((s8[8388608]{0:T(1024)(128)(4,1)}), s8[4194304]{0:T(1024)(128)(4,1)S(1)}, s32[]{:S(2)}) async-start(s8[8388608]{0:T(1024)(128)(4,1)} %bitcast.210), calls=%async_computation.16 | async-start | bytes 8388608
  247.8 9.5 %copy-start.12 = (f32[704,1024]{1,0:T(8,128)S(1)}, f32[704,1024]{1,0:T(8,128)}, u32[]{:S(2)}) copy-start(f32[704,1024]{1,0:T(8,128)} %get-tuple-element.122) | copy-start | bytes 8650756
  275.4 2.5 collective-permute-start.10
  277.9 50.0 %copy-start.17 = (bf16[704,1024]{1,0:T(8,128)(2,1)S(1)}, bf16[704,1024]{1,0:T(8,128)(2,1)}, u32[]{:S(2)}) copy-start(bf16[704,1024]{1,0:T(8,128)(2,1)} %copy-done.16) | copy-start | bytes 4325380
  277.9 50.0 %copy-start.24 = (bf16[704,512]{1,0:T(8,128)(2,1)S(1)}, bf16[704,512]{1,0:T(8,128)(2,1)}, u32[]{:S(2)}) copy-start(bf16[704,512]{1,0:T(8,128)(2,1)} %get-tuple-element.76) | copy-start | bytes 2162692
  277.9 50.0 %copy-start.25 = (bf16[704,512]{1,0:T(8,128)(2,1)S(1)}, bf16[704,512]{1,0:T(8,128)(2,1)}, u32[]{:S(2)}) copy-start(bf16[704,512]{1,0:T(8,128)(2,1)} %get-tuple-element.77) | copy-start | bytes 2162692
  327.7 4.0 collective-permute-start.11
  331.1 111.3 %reduce-scatter.5.cloned.1.call-start = ((), (), s32[]{:S(2)}) async-start(), calls=%async_computation.8 | async-start | bytes 7077888 | tf_op jit(solution)/shard_map/reduce_scatter | solution.py:428
  331.2 3.3 collective-permute-start.12
  331.6 3.3 collective-permute-start.13
  344.8 172.6 %reduce-scatter.9.cloned.1.call-start = ((), (), s32[]{:S(2)}) async-start(), calls=%async_computation.10 | async-start | bytes 9437184 | tf_op jit(solution)/shard_map/reduce_scatter | solution.py:428
  357.1 235.3 %reduce-scatter.11.cloned.1.call-start = ((), (), s32[]{:S(2)}) async-start(), calls=%async_computation.11 | async-start | bytes 9437184 | tf_op jit(solution)/shard_map/reduce_scatter | solution.py:428
  370.1 376.3 %all-reduce.7.cloned.1.call-start = ((), (), s32[]{:S(2)}) async-start(), calls=%async_computation.12 | async-start | bytes 6291456 | tf_op jit(solution)/shard_map/psum | solution.py:458
  371.7 10.1 %collective-permute-start.4 = (bf16[344,1024]{1,0:T(8,128)(2,1)S(1)}, bf16[344,1024]{1,0:T(8,128)(2,1)S(1)}, u32[]{:S(2)}, u32[]{:S(2)}) collective-permute-start(bf16[344,1024]{1,0:T(8,128)(2,1)S(1)} %get-tuple-element.84), channel_id=1, source_target_pairs={{0,0},{4,1},{1,2},{5,3},{2,4},{6,5},{3,6},{7,7},{8,8},{12,9},{9,10... | collective-permute-start | bytes 2113544 | tf_op jit(solution)/shard_map/ppermute | solution.py:311
  372.4 25.6 %collective-permute-start.5 = (bf16[344,1024]{1,0:T(8,128)(2,1)S(1)}, bf16[344,1024]{1,0:T(8,128)(2,1)S(1)}, u32[]{:S(2)}, u32[]{:S(2)}) collective-permute-start(bf16[344,1024]{1,0:T(8,128)(2,1)S(1)} %get-tuple-element.85), channel_id=1, source_target_pairs={{1,0},{5,1},{0,2},{4,3},{3,4},{7,5},{2,6},{6,7},{9,8},{13,9},{8,10... | collective-permute-start | bytes 2113544 | tf_op jit(solution)/shard_map/ppermute | solution.py:311
  592.4 8.5 %copy-start.1 = (f32[2,352,1024]{2,1,0:T(8,128)S(1)}, f32[2,352,1024]{2,1,0:T(8,128)}, u32[]{:S(2)}) copy-start(f32[2,352,1024]{2,1,0:T(8,128)} %copy-done) | copy-start | bytes 8650756
  592.4 8.5 %copy-start.27 = (f32[1,1024]{1,0:T(1,128)S(1)}, f32[1,1024]{1,0:T(1,128)}, u32[]{:S(2)}) copy-start(f32[1,1024]{1,0:T(1,128)} %get-tuple-element.117) | copy-start | bytes 12292
  592.4 8.5 %copy-start.29 = (f32[704]{0:T(1024)S(1)}, f32[704]{0:T(1024)}, u32[]{:S(2)}) copy-start(f32[704]{0:T(1024)} %copy-done.28) | copy-start | bytes 8452
  592.4 8.5 %copy-start.31 = (f32[704]{0:T(1024)S(1)}, f32[704]{0:T(1024)}, u32[]{:S(2)}) copy-start(f32[704]{0:T(1024)} %copy-done.30) | copy-start | bytes 8452
  605.4 96.0 %collective-permute-start.14 = (bf16[344,1024]{1,0:T(8,128)(2,1)S(1)}, bf16[344,1024]{1,0:T(8,128)(2,1)S(1)}, u32[]{:S(2)}, u32[]{:S(2)}) collective-permute-start(bf16[344,1024]{1,0:T(8,128)(2,1)S(1)} %get-tuple-element.80), channel_id=1, source_target_pairs={{0,0},{4,1},{1,2},{5,3},{2,4},{6,5},{3,6},{7,7},{8,8},{12,9},{9,10... | collective-permute-start | bytes 2113544 | tf_op jit(solution)/shard_map/ppermute | solution.py:311
  606.1 95.3 %collective-permute-start.15 = (bf16[344,1024]{1,0:T(8,128)(2,1)S(1)}, bf16[344,1024]{1,0:T(8,128)(2,1)S(1)}, u32[]{:S(2)}, u32[]{:S(2)}) collective-permute-start(bf16[344,1024]{1,0:T(8,128)(2,1)S(1)} %get-tuple-element.81), channel_id=1, source_target_pairs={{1,0},{5,1},{0,2},{4,3},{3,4},{7,5},{2,6},{6,7},{9,8},{13,9},{8,10... | collective-permute-start | bytes 2113544 | tf_op jit(solution)/shard_map/ppermute | solution.py:311
  (32 other events, 114.2 us)
Sparse Core Ops, SparseCore 0:
  10.0 48.2 all-gather.4
  60.1 27.7 all-gather.6
  89.8 54.2 all-gather.8
  145.8 54.2 all-gather.10
  331.3 46.0 reduce-scatter.6
  380.6 61.7 reduce-scatter.4
  445.9 71.4 reduce-scatter.8
  520.8 71.5 reduce-scatter.10
  595.0 151.3 all-reduce.6

commit v2 on v1

--- a/solution.py
+++ b/solution.py
@@ -1,3 +1,5 @@
+import functools
+
 import jax
 import jax.numpy as jnp
 from jax import lax
@@ -11,6 +13,7 @@
 F32 = jnp.float32
 BF16 = jnp.bfloat16
 NT = (((1,), (1,)), ((), ()))
+TN = (((0,), (0,)), ((), ()))
 
 
 def lane_masks(dtype):
@@ -20,7 +23,7 @@
 
 
 def forward_kernel(
-    q_own, k_own, v_own, q_rec, k_rec, v_rec, bias_ref, o_own, o_rec, lse_ref, q_s, k_s, v_s, o_s, lse_s
+    core_ref, q_own, k_own, v_own, q_rec, k_rec, v_rec, bias_ref, o_ref, lse_ref, q_s, k_s, v_s, lse_s
 ):
     half = q_own.shape[0]
     for all_ref, own, rec in ((q_s, q_own, q_rec), (k_s, k_own, k_rec), (v_s, v_own, v_rec)):
@@ -43,19 +46,18 @@
             mixed = jnp.dot(weight.astype(BF16), v_s[...], preferred_element_type=F32)
             outs.append(mixed / total)
             sums.append(peak + jnp.log(total))
-        o_s[pl.ds(row, SPAN), :] = (outs[0] * low + outs[1] * high).astype(BF16)
+        o_ref[pl.ds(row, SPAN), :] = (outs[0] * low + outs[1] * high).astype(BF16)
         lse_s[pl.ds(row, SPAN), :] = sums[0] * low + sums[1] * high
         return carry
 
     lax.fori_loop(0, 2 * half // SPAN, block, 0)
-    o_own[...] = o_s[:half, :]
-    o_rec[...] = o_s[half:, :]
     turned = jnp.transpose(lse_s[...])
     lse_ref[0, 0:8, :] = turned[0:8, :]
     lse_ref[0, 8:16, :] = turned[HEAD_DIM : HEAD_DIM + 8, :]
 
 
 def backward_kernel(
+    core_ref,
     q_own,
     k_own,
     v_own,
@@ -64,25 +66,16 @@
     v_rec,
     g_own,
     g_rec,
-    o_own,
-    o_rec,
+    o_ref,
     lse_ref,
     bias_ref,
-    dq_own,
-    dk_own,
-    dv_own,
-    dq_rec,
-    dk_rec,
-    dv_rec,
-    q_s,
-    k_s,
-    v_s,
-    g_s,
-    dqt_s,
-    dk_s,
-    dv_s,
+    *rest,
 ):
+    d_ref, q_s, k_s, v_s, g_s, dqt_s = rest[-6:]
     half = q_own.shape[0]
+    width = d_ref.shape[1] // 3
+    pair = pl.program_id(0)
+    cols = [pl.multiple_of(part * width + pair * 2 * HEAD_DIM, 128) for part in range(3)]
     low, high = lane_masks(BF16)
     for all_ref, own, rec in ((k_s, k_own, k_rec), (v_s, v_own, v_rec)):
         all_ref[:half, :] = own[...]
@@ -91,8 +84,8 @@
         for head, mask in enumerate((low, high)):
             all_ref[head, :half, :] = own[...] * mask
             all_ref[head, half:, :] = rec[...] * mask
-    dots_own = jnp.transpose(g_own[...].astype(F32) * o_own[...].astype(F32))
-    dots_rec = jnp.transpose(g_rec[...].astype(F32) * o_rec[...].astype(F32))
+    dots_own = jnp.transpose(g_own[...].astype(F32) * o_ref[:half, :].astype(F32))
+    dots_rec = jnp.transpose(g_rec[...].astype(F32) * o_ref[half:, :].astype(F32))
     dots = jnp.concatenate([dots_own, dots_rec], axis=1)
     inner = (
         jnp.sum(dots[:HEAD_DIM], axis=0, keepdims=True),
@@ -121,94 +114,192 @@
             dk = dk + jnp.dot(g_score, query, preferred_element_type=F32)
             rows = slice(HEAD_DIM * head, HEAD_DIM * (head + 1))
             dqt_s[rows, :] += jnp.dot(key_t[rows, :], g_score, preferred_element_type=F32)
-        dk_s[pl.ds(row, SPAN), :] = dk.astype(BF16)
-        dv_s[pl.ds(row, SPAN), :] = dv.astype(BF16)
+        d_ref[pl.ds(row, SPAN), pl.ds(cols[1], 2 * HEAD_DIM)] = dk.astype(BF16)
+        d_ref[pl.ds(row, SPAN), pl.ds(cols[2], 2 * HEAD_DIM)] = dv.astype(BF16)
         return carry
 
     lax.fori_loop(0, 2 * half // SPAN, block, 0)
     dq = (jnp.transpose(dqt_s[...]) * HEAD_DIM ** (-0.5)).astype(BF16)
-    dq_own[...] = dq[:half, :]
-    dq_rec[...] = dq[half:, :]
-    for all_ref, own, rec in ((dk_s, dk_own, dk_rec), (dv_s, dv_own, dv_rec)):
-        own[...] = all_ref[:half, :]
-        rec[...] = all_ref[half:, :]
-
-
-def pair_blocks(half, pairs):
+    d_ref[:, pl.ds(cols[0], 2 * HEAD_DIM)] = dq
+
+
+def call(kernel, core, args, grid, in_specs, out_specs, out_shape, scratch, flops, trans):
+    moved = sum(arg.size * arg.dtype.itemsize for arg in args)
+    return pl.pallas_call(
+        kernel,
+        grid_spec=pltpu.PrefetchScalarGridSpec(
+            num_scalar_prefetch=1,
+            grid=grid,
+            in_specs=in_specs,
+            out_specs=out_specs,
+            scratch_shapes=scratch,
+        ),
+        out_shape=out_shape,
+        cost_estimate=pl.CostEstimate(flops=flops, transcendentals=trans, bytes_accessed=moved),
+        compiler_params=pltpu.CompilerParams(vmem_limit_bytes=56 * 1024 * 1024),
+    )(core, *args)
+
+
+def head_blocks(half, pairs):
     wide = 2 * HEAD_DIM
-    return [
-        pl.BlockSpec((half, wide), lambda pair, part=part: (0, part * pairs + pair))
+    own = [
+        pl.BlockSpec((half, wide), lambda pair, core, part=part: (0, 2 * (part * pairs + pair) + core[0]))
         for part in range(3)
     ]
-
-
-def attention(own, rec, bias):
-    half = own.shape[0]
-    width = own.shape[1] // 3
+    rec = [
+        pl.BlockSpec((half, wide), lambda pair, core, part=part: (0, part * pairs + pair))
+        for part in range(3)
+    ]
+    return own + rec
+
+
+def attention(core, qkv, rec, bias):
+    half = rec.shape[0]
+    width = rec.shape[1] // 3
     wide = 2 * HEAD_DIM
     pairs = width // wide
     full = 2 * half
-    col = pl.BlockSpec((half, wide), lambda pair: (0, pair))
     ops = pairs * 2 * full * full
-    return pl.pallas_call(
+    return call(
         forward_kernel,
-        grid=(pairs,),
-        in_specs=pair_blocks(half, pairs)
-        + pair_blocks(half, pairs)
-        + [pl.BlockSpec((1, full), lambda pair: (0, 0))],
-        out_specs=[col, col, pl.BlockSpec((1, 16, full), lambda pair: (pair, 0, 0))],
-        out_shape=[
-            jax.ShapeDtypeStruct((half, width), BF16),
-            jax.ShapeDtypeStruct((half, width), BF16),
+        core,
+        (qkv, qkv, qkv, rec, rec, rec, bias.reshape(1, full)),
+        (pairs,),
+        head_blocks(half, pairs) + [pl.BlockSpec((1, full), lambda pair, core: (0, 0))],
+        [
+            pl.BlockSpec((full, wide), lambda pair, core: (0, pair)),
+            pl.BlockSpec((1, 16, full), lambda pair, core: (pair, 0, 0)),
+        ],
+        [
+            jax.ShapeDtypeStruct((full, width), BF16),
             jax.ShapeDtypeStruct((pairs, 16, full), F32),
         ],
-        scratch_shapes=[pltpu.VMEM((full, wide), BF16)] * 4 + [pltpu.VMEM((full, wide), F32)],
-        cost_estimate=pl.CostEstimate(
-            flops=ops * 4 * 256, transcendentals=ops, bytes_accessed=own.size * 6
-        ),
-        compiler_params=pltpu.CompilerParams(vmem_limit_bytes=56 * 1024 * 1024),
-        name="attend",
-    )(own, own, own, rec, rec, rec, bias.reshape(1, full))
-
-
-def attention_back(own, rec, g_own, g_rec, o_own, o_rec, lse, bias):
-    half = own.shape[0]
-    width = own.shape[1] // 3
+        [pltpu.VMEM((full, wide), BF16)] * 3 + [pltpu.VMEM((full, wide), F32)],
+        ops * 4 * 256,
+        ops,
+    )
+
+
+def attention_back(core, qkv, rec, g_own, g_rec, mixed, lse, bias, after):
+    half = rec.shape[0]
+    width = rec.shape[1] // 3
     wide = 2 * HEAD_DIM
     pairs = width // wide
     full = 2 * half
-    col = pl.BlockSpec((half, wide), lambda pair: (0, pair))
+    col = pl.BlockSpec((half, wide), lambda pair, core: (0, pair))
     ops = pairs * 2 * full * full
-    return pl.pallas_call(
+    return call(
         backward_kernel,
-        grid=(pairs,),
-        in_specs=pair_blocks(half, pairs)
-        + pair_blocks(half, pairs)
+        core,
+        (qkv, qkv, qkv, rec, rec, rec, g_own, g_rec, mixed, lse, bias.reshape(full, 1)) + tuple(after),
+        (pairs,),
+        head_blocks(half, pairs)
         + [
             col,
             col,
-            col,
-            col,
-            pl.BlockSpec((1, 16, full), lambda pair: (pair, 0, 0)),
-            pl.BlockSpec((full, 1), lambda pair: (0, 0)),
-        ],
-        out_specs=[col] * 6,
-        out_shape=[jax.ShapeDtypeStruct((half, width), BF16)] * 6,
-        scratch_shapes=[
+            pl.BlockSpec((full, wide), lambda pair, core: (0, pair)),
+            pl.BlockSpec((1, 16, full), lambda pair, core: (pair, 0, 0)),
+            pl.BlockSpec((full, 1), lambda pair, core: (0, 0)),
+        ]
+        + [pl.BlockSpec(memory_space=pl.ANY)] * len(after),
+        pl.BlockSpec((full, 3 * width), lambda pair, core: (0, 0)),
+        jax.ShapeDtypeStruct((full, 3 * width), BF16),
+        [
             pltpu.VMEM((2, full, wide), BF16),
             pltpu.VMEM((full, wide), BF16),
             pltpu.VMEM((full, wide), BF16),
             pltpu.VMEM((2, full, wide), BF16),
             pltpu.VMEM((wide, full), F32),
-            pltpu.VMEM((full, wide), BF16),
-            pltpu.VMEM((full, wide), BF16),
         ],
-        cost_estimate=pl.CostEstimate(
-            flops=ops * 10 * 256, transcendentals=ops, bytes_accessed=own.size * 12
-        ),
-        compiler_params=pltpu.CompilerParams(vmem_limit_bytes=56 * 1024 * 1024),
-        name="attend_back",
-    )(own, own, own, rec, rec, rec, g_own, g_rec, o_own, o_rec, lse, bias.reshape(full, 1))
+        ops * 10 * 256,
+        ops,
+    )
+
+
+def grad_kernel(core_ref, *refs):
+    a_own, a_rec = refs[:2]
+    b_rec, out = refs[-2:]
+    start = 0
+    for b_own in refs[2:-2]:
+        cols = slice(start, start + b_own.shape[1])
+        total = lax.dot_general(a_own[...], b_own[...], TN, preferred_element_type=F32)
+        total += lax.dot_general(a_rec[...], b_rec[:, cols], TN, preferred_element_type=F32)
+        out[:, cols] = total.astype(BF16)
+        start += b_own.shape[1]
+
+
+def weight_grad(core, a_own, a_rec, b_owns, b_rec, specs, shape, tile):
+    args = (a_own, a_rec) + tuple(b_owns) + (b_rec,)
+    rows = 4 * SPAN
+    return call(
+        grad_kernel,
+        core,
+        args,
+        (shape[0] // tile,),
+        specs,
+        pl.BlockSpec((tile, shape[1]), lambda i, core: (i, 0)),
+        jax.ShapeDtypeStruct(shape, BF16),
+        [],
+        2 * rows * shape[0] * shape[1],
+        0,
+    )
+
+
+def pick_kernel(unit, core_ref, src, dst):
+    for parity in range(2):
+
+        @pl.when(core_ref[0] == parity)
+        def _():
+            for idx in range(dst.shape[1] // unit):
+                low = (2 * idx + 1 - parity) * unit
+                dst[:, idx * unit : (idx + 1) * unit] = src[:, low : low + unit]
+
+
+def pick_other(core, array, unit):
+    rows, width = array.shape
+    wide = 1024
+    return call(
+        functools.partial(pick_kernel, unit),
+        core,
+        (array,),
+        (width // wide,),
+        [pl.BlockSpec((rows, wide), lambda i, core: (0, i))],
+        pl.BlockSpec((rows, wide // 2), lambda i, core: (0, i)),
+        jax.ShapeDtypeStruct((rows, width // 2), array.dtype),
+        [],
+        0,
+        0,
+    )
+
+
+def merge_kernel(unit, core_ref, own, rec, dst):
+    for parity in range(2):
+
+        @pl.when(core_ref[0] == parity)
+        def _():
+            for idx in range(own.shape[1] // unit):
+                cols = slice(idx * unit, (idx + 1) * unit)
+                for side, src in enumerate((own, rec)):
+                    low = (2 * idx + (parity + side) % 2) * unit
+                    dst[:, low : low + unit] = src[:, cols]
+
+
+def merge(core, own, rec, rows, unit):
+    width = rec.shape[1]
+    wide = 512
+    spec = pl.BlockSpec((rows, wide), lambda i, core: (0, i))
+    return call(
+        functools.partial(merge_kernel, unit),
+        core,
+        (own, rec),
+        (width // wide,),
+        [spec, spec],
+        pl.BlockSpec((rows, 2 * wide), lambda i, core: (0, i)),
+        jax.ShapeDtypeStruct((rows, 2 * width), rec.dtype),
+        [],
+        0,
+        0,
+    )
 
 
 def gelu_parts(values):
@@ -256,8 +347,9 @@
         for seq in range(n_seq)
     ]
     axes = ("shard", "seq")
-
-    def on_device(
+    chips = [list(range(core, n_shard, 2)) for core in range(2)]
+
+    def inner(
         inputs,
         teacher,
         cotangent,
@@ -322,6 +414,42 @@
         def exchange(array):
             return lax.ppermute(array, axes, swap)
 
+        halves = dl % (2 * HEAD_DIM) == 0
+
+        def interleave(own, other, part, axis):
+            own = jnp.split(own, own.shape[axis] // part, axis)
+            other = jnp.split(other, len(own), axis)
+            blocks = []
+            for mine, his in zip(own, other):
+                blocks.append(jnp.where(core == 0, mine, his))
+                blocks.append(jnp.where(core == 0, his, mine))
+            return jnp.concatenate(blocks, axis)
+
+        def scatter(array, part, axis):
+            if halves:
+                return lax.psum_scatter(
+                    array, "shard", scatter_dimension=0, axis_index_groups=chips, tiled=True
+                )
+            array = interleave(array, jnp.zeros_like(array), part, axis)
+            return lax.psum_scatter(array, "shard", scatter_dimension=0, tiled=True)
+
+        def z_reduce(array):
+            split = (n_seq, array.shape[0] // n_seq, array.shape[1])
+            got = lax.all_to_all(array.reshape(split), "seq", 0, 0, tiled=True)
+            total = jnp.sum(got.astype(F32), axis=0).astype(BF16)
+            got = lax.all_to_all(
+                jnp.broadcast_to(total[None], split), "seq", 0, 0, tiled=True
+            )
+            return got.reshape(array.shape)
+
+        def spread(array, part):
+            if not halves:
+                return array
+            array = array.reshape(2, dl, array.shape[1])
+            keep = lax.dynamic_index_in_dim(array, core, 0, keepdims=False)
+            away = lax.dynamic_index_in_dim(array, 1 - core, 0, keepdims=False)
+            return interleave(keep, exchange(away), part, 1)
+
         lengths = jnp.sum(token_valid, axis=1) * image_real
         sizes = jnp.stack([lengths // 64, lengths % 64], axis=1).reshape(1, 2 * images)
         sizes = jnp.pad(sizes.astype(BF16), ((0, 0), (0, dl - 2 * images)))
@@ -373,40 +501,36 @@
         live = live[:, None]
 
         qkv_mat = lax.all_gather(w_qkv, "shard", axis=0, tiled=True)
-        out_mat = lax.all_gather(w_out, "shard", axis=0, tiled=True)
+        out_mat = lax.all_to_all(
+            jnp.broadcast_to(w_out[None], (n_shard, dl, width)), "shard", 0, 0, tiled=True
+        ).reshape(width, width)
         up_mat = lax.all_gather(w_up, "shard", axis=0, tiled=True)
         down_mat = lax.all_gather(w_down, "shard", axis=0, tiled=True)
 
+        unit = 2 * HEAD_DIM
+        ff_unit = max(ff // n_shard, 4 * unit)
+        core_arr = core.astype(jnp.int32).reshape(1)
         x_rows = bring(inputs).astype(F32)
         normed1 = (norm_parts(x_rows)[0] * gain1 + shift1).astype(BF16)
+        normed1_rec = exchange(normed1)
         qkv_bias = jnp.concatenate([qbias, jnp.zeros_like(qbias), vbias])
-        qkv = (jnp.dot(normed1, qkv_mat, preferred_element_type=F32) + qkv_bias).astype(BF16)
-        teacher, cotangent, qkv = lax.optimization_barrier((teacher, cotangent, qkv))
-        teach_rows = bring(teacher).astype(F32)
-        cot_rows = bring(cotangent).astype(F32)
-        head_cols = width // 2
-
-        def parted(array, parts):
-            array = array.reshape(rows, parts, 2, head_cols)
-            left = array[:, :, 0].reshape(rows, parts * head_cols)
-            right = array[:, :, 1].reshape(rows, parts * head_cols)
-            return jnp.where(core == 0, left, right), jnp.where(core == 0, right, left)
-
-        def joined(mine, other):
-            return jnp.where(core == 0, mine, other), jnp.where(core == 0, other, mine)
-
         scale = jnp.concatenate(
             [jnp.full((width,), HEAD_DIM ** (-0.5), BF16), jnp.ones((2 * width,), BF16)]
         )
-        own, away = parted(qkv * scale, 3)
-        rec = exchange(away)
-        o_own, o_rec, lse = attention(own, rec, key_bias)
-        mixed = jnp.concatenate(joined(o_own, exchange(o_rec)), axis=1)
+        qkv = (jnp.dot(normed1, qkv_mat, preferred_element_type=F32) + qkv_bias).astype(BF16) * scale
+        rec = exchange(pick_other(core_arr, qkv, unit))
+        mixed_mine, lse = attention(core_arr, qkv, rec, key_bias)
+        both = bring(jnp.concatenate([teacher, cotangent], axis=-1))
+        teach_rows = both[:, :width].astype(F32)
+        cot_rows = both[:, width:].astype(F32)
+        mixed = merge(core_arr, mixed_mine, exchange(mixed_mine[rows:]), rows, unit)
         attn_out = jnp.dot(mixed, out_mat, preferred_element_type=F32) + obias
         resid1 = x_rows + layer1 * attn_out
         normed2 = (norm_parts(resid1)[0] * gain2 + shift2).astype(BF16)
+        normed2_rec = exchange(normed2)
         pre = jnp.dot(normed2, up_mat, preferred_element_type=F32) + ubias
         act = (pre * gelu_parts(pre)[0]).astype(BF16)
+        act_rec = exchange(pick_other(core_arr, act, ff_unit))
         branch = jnp.dot(act, down_mat, preferred_element_type=F32) + dbias
         resid2 = resid1 + layer2 * branch
         out_rows = jnp.where(live, resid2, x_rows)
@@ -420,42 +544,116 @@
         d_scale2 = jnp.sum(g_keep * branch, axis=0)
         g_branch = (g_keep * layer2).astype(BF16)
         d_down_bias = jnp.sum(g_branch.astype(F32), axis=0)
-
-        def weight_grad(left, right):
-            return jnp.einsum("ra,rb->ab", left, right, preferred_element_type=F32).astype(BF16)
-
-        def scatter(array):
-            return lax.psum_scatter(array, "shard", scatter_dimension=0, tiled=True)
-
-        p_down = scatter(weight_grad(act, g_branch))
+        g_branch_rec = exchange(g_branch)
+
+        tile = 2 * unit
+        whole = pl.BlockSpec((rows, width), lambda i, core: (0, 0))
+        strip = pl.BlockSpec((rows, tile), lambda i, core: (0, i))
+        per = ff_unit // tile
+        w_down_part = weight_grad(
+            core_arr,
+            act,
+            act_rec,
+            (g_branch,),
+            g_branch_rec,
+            [
+                pl.BlockSpec(
+                    (rows, tile), lambda i, core: (0, (2 * (i // per) + core[0]) * per + i % per)
+                ),
+                strip,
+                whole,
+                whole,
+            ],
+            (ff // 2, width),
+            tile,
+        )
+        p_down = scatter(w_down_part, ff_unit, 0)
         g_hidden = jnp.einsum("rd,fd->rf", g_branch, down_mat, preferred_element_type=F32)
         phi_sum, phi = gelu_parts(pre)
         g_pre = (g_hidden * (phi_sum + pre * phi)).astype(BF16)
         d_up_bias = jnp.sum(g_pre.astype(F32), axis=0)
-        p_up = scatter(weight_grad(normed2, g_pre))
+        g_pre_rec = exchange(pick_other(core_arr, g_pre, ff_unit))
+        n_units = ff // ff_unit // 2
+        w_up_part = weight_grad(
+            core_arr,
+            normed2,
+            normed2_rec,
+            (g_pre,) * n_units,
+            g_pre_rec,
+            [strip, strip]
+            + [
+                pl.BlockSpec((rows, ff_unit), lambda i, core, j=j: (0, 2 * j + core[0]))
+                for j in range(n_units)
+            ]
+            + [pl.BlockSpec((rows, ff // 2), lambda i, core: (0, 0))],
+            (width, ff // 2),
+            tile,
+        )
+        p_up = scatter(w_up_part, ff_unit, 1)
         g_norm2 = jnp.einsum("rf,df->rd", g_pre, up_mat, preferred_element_type=F32)
         g_ln2, d_gain2, d_shift2 = norm_back(resid1, gain2, g_norm2)
         g_resid1 = g_keep + g_ln2
         d_scale1 = jnp.sum(g_resid1 * attn_out, axis=0)
         g_attn = (g_resid1 * layer1).astype(BF16)
         d_out_bias = jnp.sum(g_attn.astype(F32), axis=0)
-        g_mixed = jnp.einsum("rd,cd->rc", g_attn, out_mat, preferred_element_type=F32).astype(BF16)
-        g_mine, g_away = parted(g_mixed, 1)
-        g_rec = exchange(g_away)
-        p_out = scatter(weight_grad(mixed, g_attn))
-        grads = attention_back(own, rec, g_mine, g_rec, o_own, o_rec, lse, key_bias)
-        pieces = []
-        for part in range(3):
-            pieces.extend(joined(grads[part], exchange(grads[3 + part])))
-        g_qkv = jnp.concatenate(pieces, axis=1)
-        p_qkv = scatter(weight_grad(normed1, g_qkv))
+        g_attn_rec = exchange(g_attn)
+        out_mine = lax.dynamic_index_in_dim(
+            out_mat.reshape(width // unit // 2, 2, unit, width), core, 1, keepdims=False
+        ).reshape(width // 2, width)
+
+        def mixed_grad(array):
+            return jnp.einsum("rd,cd->rc", array, out_mine, preferred_element_type=F32).astype(BF16)
+
+        w_out_part = weight_grad(
+            core_arr,
+            mixed_mine,
+            mixed_mine,
+            (g_attn,),
+            g_attn_rec,
+            [strip, pl.BlockSpec((rows, tile), lambda i, core: (1, i)), whole, whole],
+            (width // 2, width),
+            tile,
+        )
+        p_out = scatter(w_out_part, unit, 0)
+        g_all = attention_back(
+            core_arr,
+            qkv,
+            rec,
+            mixed_grad(g_attn),
+            mixed_grad(g_attn_rec),
+            mixed_mine,
+            lse,
+            key_bias,
+            (),
+        )
+        g_rec = exchange(g_all[rows:])
+        w_qkv_part = weight_grad(
+            core_arr,
+            normed1,
+            normed1_rec,
+            (g_all,),
+            g_all,
+            [
+                strip,
+                strip,
+                pl.BlockSpec((rows, 3 * width // 2), lambda i, core: (0, 0)),
+                pl.BlockSpec((rows, 3 * width // 2), lambda i, core: (1, 0)),
+            ],
+            (width, 3 * width // 2),
+            tile,
+        )
+        p_qkv = scatter(w_qkv_part, unit, 1)
+        g_qkv = merge(core_arr, g_all, g_rec, rows, unit)
         d_qkv_bias = jnp.sum(g_qkv.astype(F32), axis=0)
         g_norm1 = jnp.einsum("re,de->rd", g_qkv, qkv_mat, preferred_element_type=F32)
         g_ln1, d_gain1, d_shift1 = norm_back(x_rows, gain1, g_norm1)
         g_in = give((g_pass + g_resid1 + g_ln1).astype(BF16)).astype(F32)
 
-        p_down, p_up, p_out = lax.psum((p_down, p_up, p_out), "seq")
-        p_qkv = lax.psum(p_qkv, "seq")
+        p_down = z_reduce(p_down)
+        p_up = z_reduce(p_up)
+        p_out, p_qkv = lax.psum((p_out, p_qkv), "seq")
+        p_up = spread(p_up, ff_unit)
+        p_qkv = spread(p_qkv, unit)
         sums = jnp.concatenate(
             [
                 jnp.stack(
@@ -477,9 +675,14 @@
             ],
             axis=0,
         )
-        sums = lax.psum(sums, axes)
-        loss = sums[10 + ups, 0] / (count * width)
-        mine = lax.dynamic_slice_in_dim(sums, shard_pos * dl, dl, 1)
+        kinds = sums.shape[0]
+        sums = sums.reshape(kinds, n_shard, 1, dl).transpose(1, 2, 0, 3)
+        sums = jnp.broadcast_to(sums, (n_shard, n_seq, kinds, dl))
+        sums = lax.all_to_all(
+            sums.reshape(n_shard * n_seq, kinds, dl), axes, 0, 0, tiled=True
+        )
+        mine = jnp.sum(sums, axis=0)
+        loss = mine[10 + ups, 0] / (count * width)
         (
             s_qb, s_vb, s_ob, s_g1, s_b1, s_l1, s_g2, s_b2, s_db, s_l2
         ) = (mine[i] for i in range(10))
@@ -505,7 +708,7 @@
             s_l2,
         )
 
-    return on_device
+    return inner
 
 
 def solution(mesh):

time: 772 us -> 646 us (0.84)
  blocking collectives: 98.1 us -> 10.7 us
  waiting for transfers between devices: 280 us -> 213 us
  Pallas kernels: 88.5 us -> 150 us
  local copies, waits for them, and re-layouts: 78.4 us -> 32.8 us
  matrix products: 114 us -> 81.7 us
  starting transfers between devices: 34.8 us -> 57.2 us
  other arithmetic: 50.6 us -> 70.4 us
    psum x1 -> x0, blocking collectives: 87.4 us -> none  [on_device(): sums = lax.psum(sums, axes)]
    reduce_scatter x4, waiting for transfers between devices: 193 us -> 112 us  [scatter(): lax.psum_scatter(array, 'shard', scatter_dimension=0, axis_index_groups=c...]
    pallas_call x2 -> x11, Pallas kernels: 88.5 us -> 150 us  [call(): pl.pallas_call(kernel, grid_spec=pltpu.PrefetchScalarGridSpec(num_scalar_...]
    all_to_all x0 -> x6, waiting for transfers between devices: none -> 55.3 us  [the longest x2 29 us: z_reduce(): lax.all_to_all(jnp.broadcast_to(total[None], split), 'seq', 0, 0, tiled=T...]
    psum x1, waiting for transfers between devices: 43.2 us -> 0.01 us  [inner(): p_out, p_qkv = lax.psum((p_out, p_qkv), 'seq')]
    dot_general x12 -> x9, matrix products: 114 us -> 81.7 us  [the longest x1 14.1 us: inner(): branch = jnp.dot(act, down_mat, preferred_element_type=F32) + dbias]
    unnamed x112 -> x93, local copies, waits for them, and re-layouts: 32.4 us -> 8.84 us
    all_to_all x0 -> x6, starting transfers between devices: none -> 23.2 us  [the longest x2 9.24 us: z_reduce(): got = lax.all_to_all(array.reshape(split), 'seq', 0, 0, tiled=True)]
  transfers between devices with their start and end apart: 25 -> 33, of which waited for: 9 -> 12; matrix products, arithmetic and copies ran while one was open for 22% -> 21% of each run, Pallas kernels for 5% -> 24%
where the time goes in v2:
time: 646 us; the launch traced here: 634 us
  waiting for transfers between devices  213 us (33%)
  Pallas kernels  150 us (23%)
  matrix products  81.7 us (13%)
  other arithmetic  70.4 us (11%)
  starting transfers between devices  57.2 us (9%)
  local copies, waits for them, and re-layouts  32.8 us (5%)
  between operations  17.7 us (3%)
  blocking collectives  10.7 us (2%)
    pallas_call x11, Pallas kernels, call(): pl.pallas_call(kernel, grid_spec=pltpu.PrefetchScalarGridSpec(num_scalar_...  150 us
    reduce_scatter x4, waiting for transfers between devices, scatter(): lax.psum_scatter(array, 'shard', scatter_dimension=0, axis_index_groups=c...  112 us
    ppermute x4, waiting for transfers between devices, bring(): lax.ppermute(lax.dynamic_index_in_dim(array, (turn + turn_out) % 2, 0, ke...  30.2 us
    all_to_all x2, waiting for transfers between devices, z_reduce(): lax.all_to_all(jnp.broadcast_to(total[None], split), 'seq', 0, 0, tiled=T...  29 us
    unnamed x30, other arithmetic  23.8 us
    all_to_all x2, waiting for transfers between devices, z_reduce(): got = lax.all_to_all(array.reshape(split), 'seq', 0, 0, tiled=True)  21 us
    ppermute x4, starting transfers between devices, bring(): lax.ppermute(lax.dynamic_index_in_dim(array, (turn + turn_out) % 2, 0, ke...  17.4 us
    dot_general x1, matrix products, inner(): branch = jnp.dot(act, down_mat, preferred_element_type=F32) + dbias  14.1 us
  transfers between devices with their start and end apart: 33, of which 12 were waited for; matrix products, arithmetic and copies ran while one was open for 21% of the time, Pallas kernels for 24%

profile of v2, /device:TPU:0, one launch (start us, length us, event | category | flops | bytes accessed | tf_op | source)
XLA Modules:
  0.0 633.8 jit_solution(1177722235166549007)
XLA Ops:
  10.4 4.3 collective-permute-start.1
  16.6 10.7 %all_gather.12 = bf16[15,1024]{1,0:T(8,128)(2,1)S(1)} all-gather(bf16[15,128]{1,0:T(8,128)(2,1)S(1)} %concatenate.64), channel_id=1, replica_groups=mesh['shard'=8,'seq'=4] {'shard'}, dimensions={1}, use_global_device_ids=true | all-gather | bytes 34560 | tf_op jit(solution)/shard_map/all_gather | solution.py:477
  28.5 19.4 %collective-permute-done.1 = bf16[344,1024]{1,0:T(8,128)(2,1)} collective-permute-done((bf16[344,1024]{1,0:T(8,128)(2,1)S(1)}, bf16[344,1024]{1,0:T(8,128)(2,1)}, u32[]{:S(2)}, u32[]{:S(2)}) %collective-permute-start.1) | collective-permute-done | bytes 704544 | tf_op jit(solution)/shard_map/ppermute | solution.py:388
  53.6 4.6 all-gather.4.cloned.1.call-done
  58.2 9.9 %fusion.8.src.q_own.k_own.v_own = bf16[704,3072]{1,0:T(8,128)(2,1)} fusion(bf16[704,1024]{1,0:T(8,128)(2,1)} %add_convert_fusion.2.refs_0_, bf16[1024,3072]{1,0:T(8,128)(2,1)} %all-gather.4.cloned.1.call-done, f32[3072]{0:T(1024)S(1)} %copy-done.33, bf16[3072]{0:T(1024)(128)(2,1)S(1)} %copy-done.45), kind=kOutput, calls=%fused_computation.15 | convolution fusion | flops 4435673088 | bytes 12077056 | tf_op jit(solution)/shard_map/dot_general | solution.py:520
  68.1 4.4 shard_map.331
  74.3 4.3 all-to-all-start
  82.4 12.4 %collective-permute-start.6 = (bf16[344,2048]{1,0:T(8,128)(2,1)}, bf16[344,2048]{1,0:T(8,128)(2,1)}, u32[]{:S(2)}, u32[]{:S(2)}) collective-permute-start(bf16[344,2048]{1,0:T(8,128)(2,1)} %get-tuple-element.48), channel_id=1, source_target_pairs={{0,0},{1,4},{2,1},{3,5},{4,2},{5,6},{6,3},{7,7},{8,8},{9,12},{10,9... | collective-permute-start | bytes 4227080 | tf_op jit(solution)/shard_map/ppermute | solution.py:388
  98.9 38.7 %shard_map.332 = (bf16[1408,512]{1,0:T(8,128)(2,1)}, f32[4,16,1408]{2,1,0:T(8,128)}) custom-call(s32[1]{0:T(128)} %bitcast.22.core_ref, bf16[704,3072]{1,0:T(8,128)(2,1)} %fusion.8.src.q_own.k_own.v_own, bf16[704,3072]{1,0:T(8,128)(2,1)} %fusion.8.src.q_own.k_own.v_own, bf16[704,3072]{1,0:T(8,128)(2,1)} %fusion.8.src.q_own.k_own.v_own, ...), custom_call_target="tpu_custom_call" | custom-call | flops 16240345088 | bytes 19469824 | tf_op jit(solution)/shard_map/pallas_call | solution.py:128
  139.0 10.8 %collective-permute-done.7 = bf16[344,2048]{1,0:T(8,128)(2,1)} collective-permute-done((bf16[344,2048]{1,0:T(8,128)(2,1)}, bf16[344,2048]{1,0:T(8,128)(2,1)}, u32[]{:S(2)}, u32[]{:S(2)}) %collective-permute-start.7) | collective-permute-done | bytes 1409056 | tf_op jit(solution)/shard_map/ppermute | solution.py:388
  154.4 3.0 shard_map.333
  157.4 6.5 %multiply_add_fusion = (f32[704,1024]{1,0:T(8,128)}, f32[704,1024]{1,0:T(8,128)}) fusion(f32[1024]{0:T(1024)S(1)} %bitcast.176, f32[1024]{0:T(1024)S(1)} %bitcast.191, f32[2,352,1024]{2,1,0:T(8,128)S(1)} %fusion.18, bf16[704,1024]{1,0:T(8,128)(2,1)} %shard_map.333, bf16[1024,1024]{1,0:T(8,128)(2,1)} %bitcast.27), kind=kOutput, calls=%fused_computation.43 | convolution fusion | flops 1478557696 | bytes 12197888 | tf_op jit(solution)/shard_map/dot_general | solution.py:527
  166.0 2.4 multiply_reduce_fusion.6
  170.4 13.3 %multiply_convert_fusion = (bf16[704,4096]{1,0:T(8,128)(2,1)}, f32[704,4096]{1,0:T(8,128)}) fusion(f32[4096]{0:T(1024)S(1)} %bitcast.183, bf16[704,1024]{1,0:T(8,128)(2,1)} %add_convert_fusion.1.refs_0_, bf16[1024,4096]{1,0:T(8,128)(2,1)} %all-gather.6.cloned.1.call-done), kind=kOutput, calls=%fused_computation.8 | convolution fusion | flops 5922881536 | bytes 27148288 | tf_op jit(solution)/shard_map/dot_general | solution.py:531
  185.5 14.1 %multiply_reduce_fusion.1 = (f32[]{:T(128)}, f32[1024]{0:T(1024)}, f32[704,1024]{1,0:T(8,128)S(1)}, bf16[704,1024]{1,0:T(8,128)(2,1)}) fusion(pred[704]{0:T(1024)(128)(4,1)S(1)} %fusion.26, bf16[704,2048]{1,0:T(8,128)(2,1)} %bitcast.160, f32[1024]{0:T(1024)S(1)} %bitcast.199, f32[]{:T(128)S(6)} %mul.311, f32[2,352,1024]{2,1,0:T(8,128)S(1)} %fusion.18, ...), kind=kOutput, calls=%fused_computation.30 | convolution fusion | flops 5917834240 | bytes 27144904 | tf_op jit(solution)/shard_map/dot_general | solution.py:534
  200.9 12.7 %convert_reduce_fusion = (f32[4096]{0:T(1024)S(1)}, bf16[704,4096]{1,0:T(8,128)(2,1)S(1)}) fusion(f32[704,4096]{1,0:T(8,128)} %get-tuple-element.92, f32[4096]{0:T(1024)S(1)} %bitcast.184, bf16[704,1024]{1,0:T(8,128)(2,1)S(1)} %get-tuple-element.37.refs_2_, bf16[4096,1024]{1,0:T(8,128)(2,1)S(1)} %copy-done.42), kind=kOutput, calls=%fused_computation.7 | convolution fusion | flops 5943062528 | bytes 27164672 | tf_op jit(solution)/shard_map/rd,fd->rf/dot_general | solution.py:571
  213.7 11.5 %multiply_reduce_fusion.2 = (f32[1024]{0:T(1024)S(1)}, f32[704]{0:T(1024)S(1)}, f32[704]{0:T(1024)S(1)}, f32[1024]{0:T(1024)S(1)}, f32[704,1024]{1,0:T(8,128)S(1)}) fusion(f32[704,1024]{1,0:T(8,128)S(1)} %copy-done.2, f32[704]{0:T(1024)S(1)} %add_rsqrt_fusion, f32[704]{0:T(1024)S(1)} %broadcast_multiply_fusion.4, f32[1024]{0:T(1024)S(1)} %bitcast.172, ...), kind=kOutput, calls=%fused_computation.32 | convolution fusion | flops 5912065024 | bytes 19946496 | tf_op jit(solution)/shard_map/rf,df->rd/dot_general | solution.py:593
  234.6 3.2 convolution_convert_fusion.1.g_own
  237.7 4.9 shard_map.337
  242.7 3.5 convolution_convert_fusion.g_rec
  246.1 50.8 %shard_map.334.own.refs_2_.refs_3_ = bf16[1408,1536]{1,0:T(8,128)(2,1)} custom-call(s32[1]{0:T(128)} %bitcast.22.core_ref, bf16[704,3072]{1,0:T(8,128)(2,1)} %fusion.8.src.q_own.k_own.v_own, bf16[704,3072]{1,0:T(8,128)(2,1)} %fusion.8.src.q_own.k_own.v_own, bf16[704,3072]{1,0:T(8,128)(2,1)} %fusion.8.src.q_own.k_own.v_own, ...), custom_call_target="tpu_custom_call" | custom-call | flops 40600862720 | bytes 22713856 | tf_op jit(solution)/shard_map/pallas_call | solution.py:128
  297.0 9.1 %shard_map.336 = bf16[1024,1536]{1,0:T(8,128)(2,1)} custom-call(s32[1]{0:T(128)} %bitcast.22.core_ref, bf16[704,1024]{1,0:T(8,128)(2,1)} %add_convert_fusion.2.refs_0_, bf16[704,1024]{1,0:T(8,128)(2,1)} %collective-permute-done.12.refs_1_, bf16[1408,1536]{1,0:T(8,128)(2,1)} %shard_map.334.own.refs_2_.refs_3_, bf16[1408,1536]{1,0:T(8,128)(2,1)} %shard_map.334.own.refs_2_.refs_3_), custom_call_target="tpu_custom_call" | custom-call | flops 4429185024 | bytes 11534336 | tf_op jit(solution)/shard_map/pallas_call | solution.py:128
  306.1 4.8 shard_map.338
  311.5 38.6 %reduce-scatter.5.cloned.1.call-done = bf16[256,1536]{1,0:T(8,128)(2,1)} async-done(((bf16[1024,1536]{1,0:T(8,128)(2,1)}), bf16[256,1536]{1,0:T(8,128)(2,1)}) %reduce-scatter.5.cloned.1.call-update) | async-done | bytes 786448 | tf_op jit(solution)/shard_map/reduce_scatter | solution.py:430
  350.2 11.5 %shard_map.339 = bf16[1024,2048]{1,0:T(8,128)(2,1)} custom-call(s32[1]{0:T(128)} %bitcast.22.core_ref, bf16[704,1024]{1,0:T(8,128)(2,1)} %add_convert_fusion.1.refs_0_, bf16[704,1024]{1,0:T(8,128)(2,1)} %collective-permute-done.14.refs_1_, bf16[704,4096]{1,0:T(8,128)(2,1)} %copy-done, bf16[704,4096]{1,0:T(8,128)(2,1)} %copy-done, bf16[704,4096]{1,0:T(8,128)(2,1)} %copy-done, ...), custom_call_target="tpu_custom_call" | custom-call | flops 5905580032 | bytes 28835840 | tf_op jit(solution)/shard_map/pallas_call | solution.py:128
  361.8 5.0 shard_map.340
  367.2 7.0 %collective-permute-done.18.refs_3_ = bf16[704,1024]{1,0:T(8,128)(2,1)S(1)} collective-permute-done((bf16[704,1024]{1,0:T(8,128)(2,1)S(1)}, bf16[704,1024]{1,0:T(8,128)(2,1)S(1)}, u32[]{:S(2)}, u32[]{:S(2)}) %collective-permute-start.18) | collective-permute-done | bytes 1441824 | tf_op jit(solution)/shard_map/ppermute | solution.py:415
  377.0 12.0 %shard_map.341 = bf16[2048,1024]{1,0:T(8,128)(2,1)} custom-call(s32[1]{0:T(128)} %bitcast.22.core_ref, bf16[704,4096]{1,0:T(8,128)(2,1)} %get-tuple-element.91.src.refs_0_, bf16[704,2048]{1,0:T(8,128)(2,1)} %copy-done.43, bf16[704,1024]{1,0:T(8,128)(2,1)} %copy-done.11, bf16[704,1024]{1,0:T(8,128)(2,1)} %copy-done.44), custom_call_target="tpu_custom_call" | custom-call | flops 5905580032 | bytes 11534336 | tf_op jit(solution)/shard_map/pallas_call | solution.py:128
  389.0 3.1 slice.175
  394.9 2.6 collective-permute-start.5
  397.5 6.8 %collective-permute-start.4 = (bf16[344,1024]{1,0:T(8,128)(2,1)}, bf16[344,1024]{1,0:T(8,128)(2,1)}, u32[]{:S(2)}, u32[]{:S(2)}) collective-permute-start(bf16[344,1024]{1,0:T(8,128)(2,1)} %get-tuple-element.56), channel_id=1, source_target_pairs={{0,0},{4,1},{1,2},{5,3},{2,4},{6,5},{3,6},{7,7},{8,8},{12,9},{9,10... | collective-permute-start | bytes 2113544 | tf_op jit(solution)/shard_map/ppermute | solution.py:403
  404.3 5.7 shard_map.335
  410.0 3.2 convert_reduce_fusion.1
  413.5 7.0 %fusion.35 = f32[704,1024]{1,0:T(8,128)S(1)} fusion(bf16[704,3072]{1,0:T(8,128)(2,1)S(1)} %copy-done.5, bf16[1024,3072]{1,0:T(8,128)(2,1)} %all-gather.4.cloned.1.call-done), kind=kOutput, calls=%fused_computation.166 | convolution fusion | flops 4429185024 | bytes 13500416 | tf_op jit(solution)/shard_map/re,de->rd/dot_general | solution.py:648
  423.6 2.6 all-to-all-start.1
  426.2 4.4 fusion.13
  432.4 3.0 collective-permute-start.11
  435.4 5.4 all-to-all-done.1
  445.6 31.0 %reduce-scatter.9.cloned.1.call-done = bf16[256,2048]{1,0:T(8,128)(2,1)} async-done(((bf16[1024,2048]{1,0:T(8,128)(2,1)}), bf16[256,2048]{1,0:T(8,128)(2,1)}) %reduce-scatter.9.cloned.1.call-update) | async-done | bytes 1048592 | tf_op jit(solution)/shard_map/reduce_scatter | solution.py:430
  476.6 4.6 all-to-all-start.2
  489.5 42.6 %reduce-scatter.11.cloned.1.call-done = bf16[512,1024]{1,0:T(8,128)(2,1)} async-done(((bf16[2048,1024]{1,0:T(8,128)(2,1)}), bf16[512,1024]{1,0:T(8,128)(2,1)}) %reduce-scatter.11.cloned.1.call-update) | async-done | bytes 1048592 | tf_op jit(solution)/shard_map/reduce_scatter | solution.py:430
  532.2 4.6 all-to-all-start.4
  541.4 21.0 %all-to-all-done.4 = bf16[4,128,1024]{2,1,0:T(8,128)(2,1)S(1)} async-done(((bf16[4,128,1024]{2,1,0:T(8,128)(2,1)}), bf16[4,128,1024]{2,1,0:T(8,128)(2,1)S(1)}, u32[]{:S(2)}, u32[]{:S(2)}) %all-to-all-start.4) | async-done | bytes 1048608 | tf_op jit(solution)/shard_map/all_to_all | solution.py:438
  563.4 3.5 all-to-all-start.3
  576.8 15.4 %all-to-all-done.3 = bf16[4,64,2048]{2,1,0:T(8,128)(2,1)S(1)} async-done(((bf16[4,64,2048]{2,1,0:T(8,128)(2,1)}), bf16[4,64,2048]{2,1,0:T(8,128)(2,1)S(1)}, u32[]{:S(2)}, u32[]{:S(2)}) %all-to-all-start.3) | async-done | bytes 1048608 | tf_op jit(solution)/shard_map/all_to_all | solution.py:440
  593.3 3.5 all-to-all-start.5
  606.0 2.4 convert_element_type.163
  608.5 13.6 %all-to-all-done.5 = bf16[4,128,1024]{2,1,0:T(8,128)(2,1)S(1)} async-done(((bf16[4,128,1024]{2,1,0:T(8,128)(2,1)}), bf16[4,128,1024]{2,1,0:T(8,128)(2,1)S(1)}, u32[]{:S(2)}, u32[]{:S(2)}) %all-to-all-start.5) | async-done | bytes 1048608 | tf_op jit(solution)/shard_map/all_to_all | solution.py:440
  (257 shorter events, 96.6 us)
Async XLA Ops:
  7.2 7.6 %copy-start.38 = (s32[2]{0:T(128)S(1)}, s32[2]{0:T(128)}, u32[]{:S(2)}) copy-start(s32[2]{0:T(128)} %param.24) | copy-start | bytes 28
  7.2 7.9 %copy-start.39 = (bf16[128]{0:T(256)(128)(2,1)S(1)}, bf16[128]{0:T(256)(128)(2,1)}, u32[]{:S(2)}) copy-start(bf16[128]{0:T(256)(128)(2,1)} %param.26) | copy-start | bytes 772
  7.2 7.9 %copy-start.40 = (bf16[128]{0:T(256)(128)(2,1)S(1)}, bf16[128]{0:T(256)(128)(2,1)}, u32[]{:S(2)}) copy-start(bf16[128]{0:T(256)(128)(2,1)} %param.27) | copy-start | bytes 772
  7.2 7.9 %copy-start.41 = (bf16[128]{0:T(256)(128)(2,1)S(1)}, bf16[128]{0:T(256)(128)(2,1)}, u32[]{:S(2)}) copy-start(bf16[128]{0:T(256)(128)(2,1)} %param.29) | copy-start | bytes 772
  7.3 7.9 %copy-start.37 = (bf16[512]{0:T(512)(128)(2,1)S(1)}, bf16[512]{0:T(512)(128)(2,1)}, u32[]{:S(2)}) copy-start(bf16[512]{0:T(512)(128)(2,1)} %param.36) | copy-start | bytes 3076
  7.3 50.9 %all-gather.4.cloned.1.call-start = ((), (), s32[]{:S(2)}) async-start(), calls=%async_computation.10 | async-start | bytes 7077888 | tf_op jit(solution)/shard_map/all_gather | solution.py:503
  8.0 162.4 %all-gather.6.cloned.1.call-start = ((), (), s32[]{:S(2)}) async-start(), calls=%async_computation.11 | async-start | bytes 9437184 | tf_op jit(solution)/shard_map/all_gather | solution.py:507
  8.7 176.7 %all-gather.8.cloned.1.call-start = ((), (), s32[]{:S(2)}) async-start(), calls=%async_computation.12 | async-start | bytes 9437184 | tf_op jit(solution)/shard_map/all_gather | solution.py:508
  9.7 18.8 %collective-permute-start = (bf16[344,1024]{1,0:T(8,128)(2,1)S(1)}, bf16[344,1024]{1,0:T(8,128)(2,1)S(1)}, u32[]{:S(2)}, u32[]{:S(2)}) collective-permute-start(bf16[344,1024]{1,0:T(8,128)(2,1)S(1)} %get-tuple-element.60), channel_id=1, source_target_pairs={{0,0},{1,4},{2,1},{3,5},{4,2},{5,6},{6,3},{7,7},{8,8},{9,12},{10,9... | collective-permute-start | bytes 2113544 | tf_op jit(solution)/shard_map/ppermute | solution.py:388
  10.4 37.5 %collective-permute-start.1 = (bf16[344,1024]{1,0:T(8,128)(2,1)S(1)}, bf16[344,1024]{1,0:T(8,128)(2,1)}, u32[]{:S(2)}, u32[]{:S(2)}) collective-permute-start(bf16[344,1024]{1,0:T(8,128)(2,1)S(1)} %get-tuple-element.61), channel_id=1, source_target_pairs={{0,1},{1,5},{2,0},{3,4},{4,3},{5,7},{6,2},{7,6},{8,9},{9,13},{10,8... | collective-permute-start | bytes 2113544 | tf_op jit(solution)/shard_map/ppermute | solution.py:388
  72.5 26.4 %collective-permute-start.2 = (bf16[704,1536]{1,0:T(8,128)(2,1)}, bf16[704,1536]{1,0:T(8,128)(2,1)}, u32[]{:S(2)}, u32[]{:S(2)}) collective-permute-start(bf16[704,1536]{1,0:T(8,128)(2,1)} %shard_map.331), channel_id=1, source_target_pairs={{0,4},{1,5},{2,6},{3,7},{4,0},{5,1},{6,2},{7,3},{8,12},{9,13},{10,... | collective-permute-start | bytes 6488072 | tf_op jit(solution)/shard_map/ppermute | solution.py:415
  74.3 83.1 %all-to-all-start = ((bf16[8,128,1024]{2,1,0:T(8,128)(2,1)}), bf16[8,128,1024]{2,1,0:T(8,128)(2,1)}, u32[]{:S(2)}, u32[]{:S(2)}) async-start(bf16[8,128,1024]{2,1,0:T(8,128)(2,1)} %broadcast_in_dim.83), calls=%async_computation | async-start | bytes 4194304 | tf_op jit(solution)/shard_map/all_to_all | solution.py:504
  78.7 232.8 %reduce-scatter.7.cloned.1.call-start = ((), (), s32[]{:S(2)}) async-start(), calls=%async_computation.14 | async-start | bytes 1310720 | tf_op jit(solution)/shard_map/reduce_scatter | solution.py:430
  80.6 14.2 %copy-start.29 = (f32[1,1024]{1,0:T(1,128)S(1)}, f32[1,1024]{1,0:T(1,128)}, u32[]{:S(2)}) copy-start(f32[1,1024]{1,0:T(1,128)} %get-tuple-element.72) | copy-start | bytes 12292
  82.4 56.6 %collective-permute-start.6 = (bf16[344,2048]{1,0:T(8,128)(2,1)}, bf16[344,2048]{1,0:T(8,128)(2,1)}, u32[]{:S(2)}, u32[]{:S(2)}) collective-permute-start(bf16[344,2048]{1,0:T(8,128)(2,1)} %get-tuple-element.48), channel_id=1, source_target_pairs={{0,0},{1,4},{2,1},{3,5},{4,2},{5,6},{6,3},{7,7},{8,8},{9,12},{10,9... | collective-permute-start | bytes 4227080 | tf_op jit(solution)/shard_map/ppermute | solution.py:388
  94.7 55.0 %collective-permute-start.7 = (bf16[344,2048]{1,0:T(8,128)(2,1)}, bf16[344,2048]{1,0:T(8,128)(2,1)}, u32[]{:S(2)}, u32[]{:S(2)}) collective-permute-start(bf16[344,2048]{1,0:T(8,128)(2,1)} %get-tuple-element.49), channel_id=1, source_target_pairs={{0,1},{1,5},{2,0},{3,4},{4,3},{5,7},{6,2},{7,6},{8,9},{9,13},{10,8... | collective-permute-start | bytes 4227080 | tf_op jit(solution)/shard_map/ppermute | solution.py:388
  138.9 14.6 %collective-permute-start.3 = (bf16[704,512]{1,0:T(8,128)(2,1)S(1)}, bf16[704,512]{1,0:T(8,128)(2,1)S(1)}, u32[]{:S(2)}, u32[]{:S(2)}) collective-permute-start(bf16[704,512]{1,0:T(8,128)(2,1)S(1)} %slice.130), channel_id=1, source_target_pairs={{0,4},{1,5},{2,6},{3,7},{4,0},{5,1},{6,2},{7,3},{8,12},{9,13},{10,... | collective-permute-start | bytes 2162696 | tf_op jit(solution)/shard_map/ppermute | solution.py:415
  170.4 15.1 %copy-start.28 = (f32[1,1024]{1,0:T(1,128)S(1)}, f32[1,1024]{1,0:T(1,128)}, u32[]{:S(2)}) copy-start(f32[1,1024]{1,0:T(1,128)} %get-tuple-element.66) | copy-start | bytes 12292
  170.4 15.1 %copy-start.36 = (f32[1,1024]{1,0:T(1,128)S(1)}, f32[1,1024]{1,0:T(1,128)}, u32[]{:S(2)}) copy-start(f32[1,1024]{1,0:T(1,128)} %get-tuple-element.67) | copy-start | bytes 12292
  185.5 15.4 %copy-start.42 = (bf16[4096,1024]{1,0:T(8,128)(2,1)S(1)}, bf16[4096,1024]{1,0:T(8,128)(2,1)}, u32[]{:S(2)}) copy-start(bf16[4096,1024]{1,0:T(8,128)(2,1)} %all-gather.8.cloned.1.call-done) | copy-start | bytes 25165828
  199.6 25.6 %copy-start.3 = (f32[704,1024]{1,0:T(8,128)}, f32[704,1024]{1,0:T(8,128)S(1)}, u32[]{:S(2)}) copy-start(f32[704,1024]{1,0:T(8,128)S(1)} %get-tuple-element.34) | copy-start | bytes 8650756
  200.9 12.7 %copy-start.11 = (bf16[704,1024]{1,0:T(8,128)(2,1)}, bf16[704,1024]{1,0:T(8,128)(2,1)S(1)}, u32[]{:S(2)}) copy-start(bf16[704,1024]{1,0:T(8,128)(2,1)S(1)} %get-tuple-element.37.refs_2_) | copy-start | bytes 4325380
  200.9 12.7 %copy-start.2 = (f32[704,1024]{1,0:T(8,128)S(1)}, f32[704,1024]{1,0:T(8,128)}, u32[]{:S(2)}) copy-start(f32[704,1024]{1,0:T(8,128)} %get-tuple-element.89) | copy-start | bytes 8650756
  213.6 11.6 %copy-start = (bf16[704,4096]{1,0:T(8,128)(2,1)}, bf16[704,4096]{1,0:T(8,128)(2,1)S(1)}, u32[]{:S(2)}) copy-start(bf16[704,4096]{1,0:T(8,128)(2,1)S(1)} %get-tuple-element.95.src.refs_2_.refs_3_.refs_4_.refs_5_) | copy-start | bytes 17301508
  213.7 11.6 %copy-start.9 = (f32[704,1024]{1,0:T(8,128)S(1)}, f32[704,1024]{1,0:T(8,128)}, u32[]{:S(2)}) copy-start(f32[704,1024]{1,0:T(8,128)} %get-tuple-element.90) | copy-start | bytes 8650756
  230.3 7.4 %collective-permute-start.8 = (bf16[704,1024]{1,0:T(8,128)(2,1)}, bf16[704,1024]{1,0:T(8,128)(2,1)}, u32[]{:S(2)}, u32[]{:S(2)}) collective-permute-start(bf16[704,1024]{1,0:T(8,128)(2,1)} %get-tuple-element.41.refs_2_), channel_id=1, source_target_pairs={{0,4},{1,5},{2,6},{3,7},{4,0},{5,1},{6,2},{7,3},{8,12},{9,13},{10,... | collective-permute-start | bytes 4325384 | tf_op jit(solution)/shard_map/ppermute | solution.py:415
  232.0 64.9 %collective-permute-start.12 = (bf16[704,1024]{1,0:T(8,128)(2,1)}, bf16[704,1024]{1,0:T(8,128)(2,1)}, u32[]{:S(2)}, u32[]{:S(2)}) collective-permute-start(bf16[704,1024]{1,0:T(8,128)(2,1)} %add_convert_fusion.2.refs_0_), channel_id=1, source_target_pairs={{0,4},{1,5},{2,6},{3,7},{4,0},{5,1},{6,2},{7,3},{8,12},{9,13},{10,... | collective-permute-start | bytes 4325384 | tf_op jit(solution)/shard_map/ppermute | solution.py:415
  242.6 107.5 %reduce-scatter.5.cloned.1.call-start = ((), (), s32[]{:S(2)}) async-start(), calls=%async_computation.13 | async-start | bytes 3932160 | tf_op jit(solution)/shard_map/reduce_scatter | solution.py:430
  306.1 137.0 %all-reduce.6.cloned.1.call-start = ((), (), s32[]{:S(2)}) async-start(), calls=%async_computation.17 | async-start | bytes 2097152 | tf_op jit(solution)/shard_map/psum | solution.py:654
  311.0 39.2 %collective-permute-start.15 = (bf16[704,2048]{1,0:T(8,128)(2,1)}, bf16[704,2048]{1,0:T(8,128)(2,1)}, u32[]{:S(2)}, u32[]{:S(2)}) collective-permute-start(bf16[704,2048]{1,0:T(8,128)(2,1)} %shard_map.338), channel_id=1, source_target_pairs={{0,4},{1,5},{2,6},{3,7},{4,0},{5,1},{6,2},{7,3},{8,12},{9,13},{10,... | collective-permute-start | bytes 8650760 | tf_op jit(solution)/shard_map/ppermute | solution.py:415
  311.2 39.0 %collective-permute-start.14 = (bf16[704,1024]{1,0:T(8,128)(2,1)}, bf16[704,1024]{1,0:T(8,128)(2,1)}, u32[]{:S(2)}, u32[]{:S(2)}) collective-permute-start(bf16[704,1024]{1,0:T(8,128)(2,1)} %add_convert_fusion.1.refs_0_), channel_id=1, source_target_pairs={{0,4},{1,5},{2,6},{3,7},{4,0},{5,1},{6,2},{7,3},{8,12},{9,13},{10,... | collective-permute-start | bytes 4325384 | tf_op jit(solution)/shard_map/ppermute | solution.py:415
  350.1 126.5 %reduce-scatter.9.cloned.1.call-start = ((), (), s32[]{:S(2)}) async-start(), calls=%async_computation.15 | async-start | bytes 5242880 | tf_op jit(solution)/shard_map/reduce_scatter | solution.py:430
  361.7 170.5 %reduce-scatter.11.cloned.1.call-start = ((), (), s32[]{:S(2)}) async-start(), calls=%async_computation.16 | async-start | bytes 5242880 | tf_op jit(solution)/shard_map/reduce_scatter | solution.py:430
  366.7 8.7 %collective-permute-start.17 = (bf16[704,2048]{1,0:T(8,128)(2,1)}, bf16[704,2048]{1,0:T(8,128)(2,1)S(1)}, u32[]{:S(2)}, u32[]{:S(2)}) collective-permute-start(bf16[704,2048]{1,0:T(8,128)(2,1)} %shard_map.340), channel_id=1, source_target_pairs={{0,4},{1,5},{2,6},{3,7},{4,0},{5,1},{6,2},{7,3},{8,12},{9,13},{10,... | collective-permute-start | bytes 8650760 | tf_op jit(solution)/shard_map/ppermute | solution.py:415
  366.7 7.6 %collective-permute-start.18 = (bf16[704,1024]{1,0:T(8,128)(2,1)S(1)}, bf16[704,1024]{1,0:T(8,128)(2,1)S(1)}, u32[]{:S(2)}, u32[]{:S(2)}) collective-permute-start(bf16[704,1024]{1,0:T(8,128)(2,1)S(1)} %copy-done.12), channel_id=1, source_target_pairs={{0,4},{1,5},{2,6},{3,7},{4,0},{5,1},{6,2},{7,3},{8,12},{9,13},{10,... | collective-permute-start | bytes 4325384 | tf_op jit(solution)/shard_map/ppermute | solution.py:415
  392.1 12.1 %collective-permute-start.9 = (bf16[704,1536]{1,0:T(8,128)(2,1)}, bf16[704,1536]{1,0:T(8,128)(2,1)}, u32[]{:S(2)}, u32[]{:S(2)}) collective-permute-start(bf16[704,1536]{1,0:T(8,128)(2,1)} %slice.175), channel_id=1, source_target_pairs={{0,4},{1,5},{2,6},{3,7},{4,0},{5,1},{6,2},{7,3},{8,12},{9,13},{10,... | collective-permute-start | bytes 6488072 | tf_op jit(solution)/shard_map/ppermute | solution.py:415
  394.9 86.3 %collective-permute-start.5 = (bf16[344,1024]{1,0:T(8,128)(2,1)}, bf16[344,1024]{1,0:T(8,128)(2,1)}, u32[]{:S(2)}, u32[]{:S(2)}) collective-permute-start(bf16[344,1024]{1,0:T(8,128)(2,1)} %get-tuple-element.57), channel_id=1, source_target_pairs={{1,0},{5,1},{0,2},{4,3},{3,4},{7,5},{2,6},{6,7},{9,8},{13,9},{8,10... | collective-permute-start | bytes 2113544 | tf_op jit(solution)/shard_map/ppermute | solution.py:403
  397.5 83.7 %collective-permute-start.4 = (bf16[344,1024]{1,0:T(8,128)(2,1)}, bf16[344,1024]{1,0:T(8,128)(2,1)}, u32[]{:S(2)}, u32[]{:S(2)}) collective-permute-start(bf16[344,1024]{1,0:T(8,128)(2,1)} %get-tuple-element.56), channel_id=1, source_target_pairs={{0,0},{4,1},{1,2},{5,3},{2,4},{6,5},{3,6},{7,7},{8,8},{12,9},{9,10... | collective-permute-start | bytes 2113544 | tf_op jit(solution)/shard_map/ppermute | solution.py:403
  423.6 17.2 %all-to-all-start.1 = ((f32[32,15,128]{2,1,0:T(8,128)}), f32[32,15,128]{2,1,0:T(8,128)S(1)}, u32[]{:S(2)}, u32[]{:S(2)}) async-start(f32[32,15,128]{2,1,0:T(8,128)} %bitcast.63), calls=%async_computation.1 | async-start | bytes 524288 | tf_op jit(solution)/shard_map/all_to_all | solution.py:681
  430.8 50.4 %collective-permute-start.10 = (bf16[344,1024]{1,0:T(8,128)(2,1)S(1)}, bf16[344,1024]{1,0:T(8,128)(2,1)}, u32[]{:S(2)}, u32[]{:S(2)}) collective-permute-start(bf16[344,1024]{1,0:T(8,128)(2,1)S(1)} %get-tuple-element.52), channel_id=1, source_target_pairs={{0,0},{4,1},{1,2},{5,3},{2,4},{6,5},{3,6},{7,7},{8,8},{12,9},{9,10... | collective-permute-start | bytes 2113544 | tf_op jit(solution)/shard_map/ppermute | solution.py:403
  432.4 48.9 %collective-permute-start.11 = (bf16[344,1024]{1,0:T(8,128)(2,1)S(1)}, bf16[344,1024]{1,0:T(8,128)(2,1)}, u32[]{:S(2)}, u32[]{:S(2)}) collective-permute-start(bf16[344,1024]{1,0:T(8,128)(2,1)S(1)} %get-tuple-element.53), channel_id=1, source_target_pairs={{1,0},{5,1},{0,2},{4,3},{3,4},{7,5},{2,6},{6,7},{9,8},{13,9},{8,10... | collective-permute-start | bytes 2113544 | tf_op jit(solution)/shard_map/ppermute | solution.py:403
  445.2 41.8 %collective-permute-start.13 = (bf16[128,1536]{1,0:T(8,128)(2,1)}, bf16[128,1536]{1,0:T(8,128)(2,1)S(1)}, u32[]{:S(2)}, u32[]{:S(2)}) collective-permute-start(bf16[128,1536]{1,0:T(8,128)(2,1)} %get-tuple-element.65), channel_id=1, source_target_pairs={{0,4},{1,5},{2,6},{3,7},{4,0},{5,1},{6,2},{7,3},{8,12},{9,13},{10,... | collective-permute-start | bytes 1179656 | tf_op jit(solution)/shard_map/ppermute | solution.py:415
  476.6 55.6 %all-to-all-start.2 = ((bf16[4,64,2048]{2,1,0:T(8,128)(2,1)}), bf16[4,64,2048]{2,1,0:T(8,128)(2,1)S(1)}, u32[]{:S(2)}, u32[]{:S(2)}) async-start(bf16[4,64,2048]{2,1,0:T(8,128)(2,1)} %bitcast.164), calls=%async_computation.5 | async-start | bytes 2097152 | tf_op jit(solution)/shard_map/all_to_all | solution.py:438
  487.0 76.5 %copy-start.10 = (bf16[128,1536]{1,0:T(8,128)(2,1)}, bf16[128,1536]{1,0:T(8,128)(2,1)S(1)}, u32[]{:S(2)}) copy-start(bf16[128,1536]{1,0:T(8,128)(2,1)S(1)} %collective-permute-done.13) | copy-start | bytes 1179652
  532.2 30.2 %all-to-all-start.4 = ((bf16[4,128,1024]{2,1,0:T(8,128)(2,1)}), bf16[4,128,1024]{2,1,0:T(8,128)(2,1)S(1)}, u32[]{:S(2)}, u32[]{:S(2)}) async-start(bf16[4,128,1024]{2,1,0:T(8,128)(2,1)} %bitcast.165), calls=%async_computation.8 | async-start | bytes 2097152 | tf_op jit(solution)/shard_map/all_to_all | solution.py:438
  563.4 28.8 %all-to-all-start.3 = ((bf16[4,64,2048]{2,1,0:T(8,128)(2,1)}), bf16[4,64,2048]{2,1,0:T(8,128)(2,1)S(1)}, u32[]{:S(2)}, u32[]{:S(2)}) async-start(bf16[4,64,2048]{2,1,0:T(8,128)(2,1)} %broadcast_in_dim.90), calls=%async_computation.6 | async-start | bytes 2097152 | tf_op jit(solution)/shard_map/all_to_all | solution.py:440
  593.3 28.8 %all-to-all-start.5 = ((bf16[4,128,1024]{2,1,0:T(8,128)(2,1)}), bf16[4,128,1024]{2,1,0:T(8,128)(2,1)S(1)}, u32[]{:S(2)}, u32[]{:S(2)}) async-start(bf16[4,128,1024]{2,1,0:T(8,128)(2,1)} %broadcast_in_dim.91), calls=%async_computation.9 | async-start | bytes 2097152 | tf_op jit(solution)/shard_map/all_to_all | solution.py:440
  604.7 19.1 %collective-permute-start.16 = (bf16[128,2048]{1,0:T(8,128)(2,1)}, bf16[128,2048]{1,0:T(8,128)(2,1)S(1)}, u32[]{:S(2)}, u32[]{:S(2)}) collective-permute-start(bf16[128,2048]{1,0:T(8,128)(2,1)} %get-tuple-element.63), channel_id=1, source_target_pairs={{0,4},{1,5},{2,6},{3,7},{4,0},{5,1},{6,2},{7,3},{8,12},{9,13},{10,... | collective-permute-start | bytes 1572872 | tf_op jit(solution)/shard_map/ppermute | solution.py:415
  (31 other events, 107.6 us)
Sparse Core Ops, SparseCore 0:
  10.0 48.2 all-gather.3
  60.1 69.1 all-gather.5
  131.2 54.2 all-gather.7
  242.8 27.8 reduce-scatter.6
  306.2 43.8 reduce-scatter.4
  352.4 68.6 all-reduce.5
  424.0 52.5 reduce-scatter.8
  479.6 52.5 reduce-scatter.10

commit v3 on v2

--- a/solution.py
+++ b/solution.py
@@ -69,9 +69,13 @@
     o_ref,
     lse_ref,
     bias_ref,
-    *rest,
+    d_ref,
+    q_s,
+    k_s,
+    v_s,
+    g_s,
+    dqt_s,
 ):
-    d_ref, q_s, k_s, v_s, g_s, dqt_s = rest[-6:]
     half = q_own.shape[0]
     width = d_ref.shape[1] // 3
     pair = pl.program_id(0)
@@ -140,14 +144,17 @@
     )(core, *args)
 
 
-def head_blocks(half, pairs):
+def head_blocks(half, pairs, first=0):
     wide = 2 * HEAD_DIM
     own = [
-        pl.BlockSpec((half, wide), lambda pair, core, part=part: (0, 2 * (part * pairs + pair) + core[0]))
+        pl.BlockSpec(
+            (half, wide),
+            lambda pair, core, part=part: (0, 2 * (part * pairs + pair + first) + core[0]),
+        )
         for part in range(3)
     ]
     rec = [
-        pl.BlockSpec((half, wide), lambda pair, core, part=part: (0, part * pairs + pair))
+        pl.BlockSpec((half, wide), lambda pair, core, part=part: (0, part * pairs + pair + first))
         for part in range(3)
     ]
     return own + rec
@@ -180,30 +187,29 @@
     )
 
 
-def attention_back(core, qkv, rec, g_own, g_rec, mixed, lse, bias, after):
+def attention_back(core, qkv, rec, g_own, g_rec, mixed, lse, bias, first, last):
     half = rec.shape[0]
-    width = rec.shape[1] // 3
     wide = 2 * HEAD_DIM
-    pairs = width // wide
+    pairs = rec.shape[1] // 3 // wide
+    here = last - first
     full = 2 * half
-    col = pl.BlockSpec((half, wide), lambda pair, core: (0, pair))
-    ops = pairs * 2 * full * full
+    col = pl.BlockSpec((half, wide), lambda pair, core: (0, pair + first))
+    ops = here * 2 * full * full
     return call(
         backward_kernel,
         core,
-        (qkv, qkv, qkv, rec, rec, rec, g_own, g_rec, mixed, lse, bias.reshape(full, 1)) + tuple(after),
-        (pairs,),
-        head_blocks(half, pairs)
+        (qkv, qkv, qkv, rec, rec, rec, g_own, g_rec, mixed, lse, bias.reshape(full, 1)),
+        (here,),
+        head_blocks(half, pairs, first)
         + [
             col,
             col,
-            pl.BlockSpec((full, wide), lambda pair, core: (0, pair)),
-            pl.BlockSpec((1, 16, full), lambda pair, core: (pair, 0, 0)),
+            pl.BlockSpec((full, wide), lambda pair, core: (0, pair + first)),
+            pl.BlockSpec((1, 16, full), lambda pair, core: (pair + first, 0, 0)),
             pl.BlockSpec((full, 1), lambda pair, core: (0, 0)),
-        ]
-        + [pl.BlockSpec(memory_space=pl.ANY)] * len(after),
-        pl.BlockSpec((full, 3 * width), lambda pair, core: (0, 0)),
-        jax.ShapeDtypeStruct((full, 3 * width), BF16),
+        ],
+        pl.BlockSpec((full, 3 * here * wide), lambda pair, core: (0, 0)),
+        jax.ShapeDtypeStruct((full, 3 * here * wide), BF16),
         [
             pltpu.VMEM((2, full, wide), BF16),
             pltpu.VMEM((full, wide), BF16),
@@ -216,20 +222,18 @@
     )
 
 
-def grad_kernel(core_ref, *refs):
-    a_own, a_rec = refs[:2]
-    b_rec, out = refs[-2:]
+def grad_kernel(core_ref, a_own, a_rec, *refs):
+    out = refs[-1]
+    count = len(refs) // 2
     start = 0
-    for b_own in refs[2:-2]:
-        cols = slice(start, start + b_own.shape[1])
+    for b_own, b_rec in zip(refs[:count], refs[count:-1]):
         total = lax.dot_general(a_own[...], b_own[...], TN, preferred_element_type=F32)
-        total += lax.dot_general(a_rec[...], b_rec[:, cols], TN, preferred_element_type=F32)
-        out[:, cols] = total.astype(BF16)
+        total += lax.dot_general(a_rec[...], b_rec[...], TN, preferred_element_type=F32)
+        out[:, start : start + b_own.shape[1]] = total.astype(BF16)
         start += b_own.shape[1]
 
 
-def weight_grad(core, a_own, a_rec, b_owns, b_rec, specs, shape, tile):
-    args = (a_own, a_rec) + tuple(b_owns) + (b_rec,)
+def weight_grad(core, args, specs, shape, tile):
     rows = 4 * SPAN
     return call(
         grad_kernel,
@@ -272,30 +276,34 @@
     )
 
 
-def merge_kernel(unit, core_ref, own, rec, dst):
+def merge_kernel(unit, core_ref, *refs):
+    dst = refs[-1]
+    count = len(refs) // 2
     for parity in range(2):
 
         @pl.when(core_ref[0] == parity)
         def _():
-            for idx in range(own.shape[1] // unit):
-                cols = slice(idx * unit, (idx + 1) * unit)
-                for side, src in enumerate((own, rec)):
-                    low = (2 * idx + (parity + side) % 2) * unit
-                    dst[:, low : low + unit] = src[:, cols]
-
-
-def merge(core, own, rec, rows, unit):
-    width = rec.shape[1]
-    wide = 512
-    spec = pl.BlockSpec((rows, wide), lambda i, core: (0, i))
+            at = 0
+            for own, rec in zip(refs[:count], refs[count:-1]):
+                for idx in range(own.shape[1] // unit):
+                    cols = slice(idx * unit, (idx + 1) * unit)
+                    for side, src in enumerate((own, rec)):
+                        low = at + (parity + side) % 2 * unit
+                        dst[:, low : low + unit] = src[:, cols]
+                    at += 2 * unit
+
+
+def merge(core, owns, recs, rows, unit, steps):
+    width = sum(rec.shape[1] for rec in recs)
+    specs = [pl.BlockSpec((rows, rec.shape[1] // steps), lambda i, core: (0, i)) for rec in recs]
     return call(
         functools.partial(merge_kernel, unit),
         core,
-        (own, rec),
-        (width // wide,),
-        [spec, spec],
-        pl.BlockSpec((rows, 2 * wide), lambda i, core: (0, i)),
-        jax.ShapeDtypeStruct((rows, 2 * width), rec.dtype),
+        tuple(owns) + tuple(recs),
+        (steps,),
+        specs + specs,
+        pl.BlockSpec((rows, 2 * width // steps), lambda i, core: (0, i)),
+        jax.ShapeDtypeStruct((rows, 2 * width), recs[0].dtype),
         [],
         0,
         0,
@@ -416,21 +424,22 @@
 
         halves = dl % (2 * HEAD_DIM) == 0
 
-        def interleave(own, other, part, axis):
+        def interleave(own, other, part, axis, order=None):
             own = jnp.split(own, own.shape[axis] // part, axis)
             other = jnp.split(other, len(own), axis)
             blocks = []
-            for mine, his in zip(own, other):
+            for idx in order or range(len(own)):
+                mine, his = own[idx], other[idx]
                 blocks.append(jnp.where(core == 0, mine, his))
                 blocks.append(jnp.where(core == 0, his, mine))
             return jnp.concatenate(blocks, axis)
 
-        def scatter(array, part, axis):
+        def scatter(array, part, axis, order=None):
             if halves:
                 return lax.psum_scatter(
                     array, "shard", scatter_dimension=0, axis_index_groups=chips, tiled=True
                 )
-            array = interleave(array, jnp.zeros_like(array), part, axis)
+            array = interleave(array, jnp.zeros_like(array), part, axis, order)
             return lax.psum_scatter(array, "shard", scatter_dimension=0, tiled=True)
 
         def z_reduce(array):
@@ -442,13 +451,13 @@
             )
             return got.reshape(array.shape)
 
-        def spread(array, part):
+        def spread(array, part, order=None):
             if not halves:
                 return array
             array = array.reshape(2, dl, array.shape[1])
             keep = lax.dynamic_index_in_dim(array, core, 0, keepdims=False)
             away = lax.dynamic_index_in_dim(array, 1 - core, 0, keepdims=False)
-            return interleave(keep, exchange(away), part, 1)
+            return interleave(keep, exchange(away), part, 1, order)
 
         lengths = jnp.sum(token_valid, axis=1) * image_real
         sizes = jnp.stack([lengths // 64, lengths % 64], axis=1).reshape(1, 2 * images)
@@ -523,14 +532,14 @@
         both = bring(jnp.concatenate([teacher, cotangent], axis=-1))
         teach_rows = both[:, :width].astype(F32)
         cot_rows = both[:, width:].astype(F32)
-        mixed = merge(core_arr, mixed_mine, exchange(mixed_mine[rows:]), rows, unit)
+        mixed = merge(core_arr, (mixed_mine,), (exchange(mixed_mine[rows:]),), rows, unit, 1)
         attn_out = jnp.dot(mixed, out_mat, preferred_element_type=F32) + obias
         resid1 = x_rows + layer1 * attn_out
         normed2 = (norm_parts(resid1)[0] * gain2 + shift2).astype(BF16)
         normed2_rec = exchange(normed2)
         pre = jnp.dot(normed2, up_mat, preferred_element_type=F32) + ubias
         act = (pre * gelu_parts(pre)[0]).astype(BF16)
-        act_rec = exchange(pick_other(core_arr, act, ff_unit))
+        act_rec = exchange(act)
         branch = jnp.dot(act, down_mat, preferred_element_type=F32) + dbias
         resid2 = resid1 + layer2 * branch
         out_rows = jnp.where(live, resid2, x_rows)
@@ -550,20 +559,13 @@
         whole = pl.BlockSpec((rows, width), lambda i, core: (0, 0))
         strip = pl.BlockSpec((rows, tile), lambda i, core: (0, i))
         per = ff_unit // tile
+        act_spec = pl.BlockSpec(
+            (rows, tile), lambda i, core: (0, (2 * (i // per) + core[0]) * per + i % per)
+        )
         w_down_part = weight_grad(
             core_arr,
-            act,
-            act_rec,
-            (g_branch,),
-            g_branch_rec,
-            [
-                pl.BlockSpec(
-                    (rows, tile), lambda i, core: (0, (2 * (i // per) + core[0]) * per + i % per)
-                ),
-                strip,
-                whole,
-                whole,
-            ],
+            (act, act_rec, g_branch, g_branch_rec),
+            [act_spec, act_spec, whole, whole],
             (ff // 2, width),
             tile,
         )
@@ -572,20 +574,17 @@
         phi_sum, phi = gelu_parts(pre)
         g_pre = (g_hidden * (phi_sum + pre * phi)).astype(BF16)
         d_up_bias = jnp.sum(g_pre.astype(F32), axis=0)
-        g_pre_rec = exchange(pick_other(core_arr, g_pre, ff_unit))
+        g_pre_rec = exchange(g_pre)
         n_units = ff // ff_unit // 2
         w_up_part = weight_grad(
             core_arr,
-            normed2,
-            normed2_rec,
-            (g_pre,) * n_units,
-            g_pre_rec,
+            (normed2, normed2_rec) + (g_pre,) * n_units + (g_pre_rec,) * n_units,
             [strip, strip]
             + [
                 pl.BlockSpec((rows, ff_unit), lambda i, core, j=j: (0, 2 * j + core[0]))
                 for j in range(n_units)
             ]
-            + [pl.BlockSpec((rows, ff // 2), lambda i, core: (0, 0))],
+            * 2,
             (width, ff // 2),
             tile,
         )
@@ -606,44 +605,36 @@
 
         w_out_part = weight_grad(
             core_arr,
-            mixed_mine,
-            mixed_mine,
-            (g_attn,),
-            g_attn_rec,
+            (mixed_mine, mixed_mine, g_attn, g_attn_rec),
             [strip, pl.BlockSpec((rows, tile), lambda i, core: (1, i)), whole, whole],
             (width // 2, width),
             tile,
         )
         p_out = scatter(w_out_part, unit, 0)
-        g_all = attention_back(
-            core_arr,
-            qkv,
-            rec,
-            mixed_grad(g_attn),
-            mixed_grad(g_attn_rec),
-            mixed_mine,
-            lse,
-            key_bias,
-            (),
-        )
-        g_rec = exchange(g_all[rows:])
+        g_mine = (mixed_grad(g_attn), mixed_grad(g_attn_rec))
+        pairs = width // 2 // unit
+        g_alls = [
+            attention_back(
+                core_arr, qkv, rec, *g_mine, mixed_mine, lse, key_bias, first, first + pairs // 2
+            )
+            for first in (0, pairs // 2)
+        ]
+        g_recs = [exchange(part[rows:]) for part in g_alls]
+        order = [
+            pair // 2 * 6 + part * 2 + pair % 2 for part in range(3) for pair in range(pairs)
+        ]
+        half_cols = 3 * width // 4
         w_qkv_part = weight_grad(
             core_arr,
-            normed1,
-            normed1_rec,
-            (g_all,),
-            g_all,
-            [
-                strip,
-                strip,
-                pl.BlockSpec((rows, 3 * width // 2), lambda i, core: (0, 0)),
-                pl.BlockSpec((rows, 3 * width // 2), lambda i, core: (1, 0)),
-            ],
+            (normed1, normed1_rec) + tuple(g_alls) * 2,
+            [strip, strip]
+            + [pl.BlockSpec((rows, half_cols), lambda i, core: (0, 0))] * 2
+            + [pl.BlockSpec((rows, half_cols), lambda i, core: (1, 0))] * 2,
             (width, 3 * width // 2),
             tile,
         )
-        p_qkv = scatter(w_qkv_part, unit, 1)
-        g_qkv = merge(core_arr, g_all, g_rec, rows, unit)
+        p_qkv = scatter(w_qkv_part, unit, 1, order)
+        g_qkv = merge(core_arr, g_alls, g_recs, rows, unit, 3)
         d_qkv_bias = jnp.sum(g_qkv.astype(F32), axis=0)
         g_norm1 = jnp.einsum("re,de->rd", g_qkv, qkv_mat, preferred_element_type=F32)
         g_ln1, d_gain1, d_shift1 = norm_back(x_rows, gain1, g_norm1)
@@ -653,7 +644,7 @@
         p_up = z_reduce(p_up)
         p_out, p_qkv = lax.psum((p_out, p_qkv), "seq")
         p_up = spread(p_up, ff_unit)
-        p_qkv = spread(p_qkv, unit)
+        p_qkv = spread(p_qkv, unit, order)
         sums = jnp.concatenate(
             [
                 jnp.stack(

time: 646 us -> 657 us (1.017)
  other arithmetic: 70.4 us -> 80.2 us
  Pallas kernels: 150 us -> 143 us
  waiting for transfers between devices: 213 us -> 220 us
    reduce_sum x1, other arithmetic: 1.97 us -> 12.5 us  [inner(): d_scale1 = jnp.sum(g_resid1 * attn_out, axis=0)]
    pallas_call x11 -> x10, Pallas kernels: 150 us -> 143 us  [call(): pl.pallas_call(kernel, grid_spec=pltpu.PrefetchScalarGridSpec(num_scalar_...]
    unnamed x93 -> x111, local copies, waits for them, and re-layouts: 8.84 us -> 13.8 us
  transfers between devices with their start and end apart: 33 -> 34, of which waited for: 12 -> 12; matrix products, arithmetic and copies ran while one was open for 21% -> 20% of each run, Pallas kernels for 24% -> 22%
where the time goes in v3:
time: 657 us; the launch traced here: 645 us
  waiting for transfers between devices  220 us (33%)
  Pallas kernels  143 us (22%)
  matrix products  80.4 us (12%)
  other arithmetic  80.2 us (12%)
  starting transfers between devices  58.1 us (9%)
  local copies, waits for them, and re-layouts  34.4 us (5%)
  between operations  17.9 us (3%)
  blocking collectives  10.7 us (2%)
    pallas_call x10, Pallas kernels, call(): pl.pallas_call(kernel, grid_spec=pltpu.PrefetchScalarGridSpec(num_scalar_...  143 us
    reduce_scatter x4, waiting for transfers between devices, scatter(): lax.psum_scatter(array, 'shard', scatter_dimension=0, axis_index_groups=c...  116 us
    ppermute x4, waiting for transfers between devices, bring(): lax.ppermute(lax.dynamic_index_in_dim(array, (turn + turn_out) % 2, 0, ke...  30.2 us
    all_to_all x2, waiting for transfers between devices, z_reduce(): lax.all_to_all(jnp.broadcast_to(total[None], split), 'seq', 0, 0, tiled=T...  29 us
    unnamed x30, other arithmetic  23.8 us
    all_to_all x2, waiting for transfers between devices, z_reduce(): got = lax.all_to_all(array.reshape(split), 'seq', 0, 0, tiled=True)  21 us
    ppermute x4, starting transfers between devices, bring(): lax.ppermute(lax.dynamic_index_in_dim(array, (turn + turn_out) % 2, 0, ke...  17.4 us
    dot_general x1, matrix products, inner(): branch = jnp.dot(act, down_mat, preferred_element_type=F32) + dbias  14.2 us
  transfers between devices with their start and end apart: 34, of which 12 were waited for; matrix products, arithmetic and copies ran while one was open for 20% of the time, Pallas kernels for 22%

profile of v3, /device:TPU:0, one launch (start us, length us, event | category | flops | bytes accessed | tf_op | source)
XLA Modules:
  0.0 645.2 jit_solution(9953279269612100861)
XLA Ops:
  10.4 4.3 collective-permute-start.1
  16.6 10.7 %all_gather.12 = bf16[15,1024]{1,0:T(8,128)(2,1)S(1)} all-gather(bf16[15,128]{1,0:T(8,128)(2,1)S(1)} %concatenate.64), channel_id=1, replica_groups=mesh['shard'=8,'seq'=4] {'shard'}, dimensions={1}, use_global_device_ids=true | all-gather | bytes 34560 | tf_op jit(solution)/shard_map/all_gather | solution.py:486
  28.5 19.4 %collective-permute-done.1 = bf16[344,1024]{1,0:T(8,128)(2,1)} collective-permute-done((bf16[344,1024]{1,0:T(8,128)(2,1)S(1)}, bf16[344,1024]{1,0:T(8,128)(2,1)}, u32[]{:S(2)}, u32[]{:S(2)}) %collective-permute-start.1) | collective-permute-done | bytes 704544 | tf_op jit(solution)/shard_map/ppermute | solution.py:396
  54.0 4.2 all-gather.4.cloned.1.call-done
  58.2 9.9 %fusion.8.src.q_own.k_own.v_own = bf16[704,3072]{1,0:T(8,128)(2,1)} fusion(bf16[704,1024]{1,0:T(8,128)(2,1)} %add_convert_fusion.2.a_own, bf16[1024,3072]{1,0:T(8,128)(2,1)} %all-gather.4.cloned.1.call-done, f32[3072]{0:T(1024)S(1)} %copy-done.43, bf16[3072]{0:T(1024)(128)(2,1)S(1)} %copy-done.54), kind=kOutput, calls=%fused_computation.15 | convolution fusion | flops 4435673088 | bytes 12077056 | tf_op jit(solution)/shard_map/dot_general | solution.py:529
  68.1 4.4 shard_map.331
  74.3 4.4 all-to-all-start
  82.4 12.3 %collective-permute-start.6 = (bf16[344,2048]{1,0:T(8,128)(2,1)}, bf16[344,2048]{1,0:T(8,128)(2,1)}, u32[]{:S(2)}, u32[]{:S(2)}) collective-permute-start(bf16[344,2048]{1,0:T(8,128)(2,1)} %get-tuple-element.48), channel_id=1, source_target_pairs={{0,0},{1,4},{2,1},{3,5},{4,2},{5,6},{6,3},{7,7},{8,8},{9,12},{10,9... | collective-permute-start | bytes 4227080 | tf_op jit(solution)/shard_map/ppermute | solution.py:396
  98.9 38.7 %shard_map.332 = (bf16[1408,512]{1,0:T(8,128)(2,1)}, f32[4,16,1408]{2,1,0:T(8,128)}) custom-call(s32[1]{0:T(128)} %bitcast.22.core_ref, bf16[704,3072]{1,0:T(8,128)(2,1)} %fusion.8.src.q_own.k_own.v_own, bf16[704,3072]{1,0:T(8,128)(2,1)} %fusion.8.src.q_own.k_own.v_own, bf16[704,3072]{1,0:T(8,128)(2,1)} %fusion.8.src.q_own.k_own.v_own, ...), custom_call_target="tpu_custom_call" | custom-call | flops 16240345088 | bytes 19469824 | tf_op jit(solution)/shard_map/pallas_call | solution.py:132
  139.0 10.7 %collective-permute-done.7 = bf16[344,2048]{1,0:T(8,128)(2,1)} collective-permute-done((bf16[344,2048]{1,0:T(8,128)(2,1)}, bf16[344,2048]{1,0:T(8,128)(2,1)}, u32[]{:S(2)}, u32[]{:S(2)}) %collective-permute-start.7) | collective-permute-done | bytes 1409056 | tf_op jit(solution)/shard_map/ppermute | solution.py:396
  154.3 3.1 shard_map.333
  157.4 6.5 %multiply_add_fusion = (f32[704,1024]{1,0:T(8,128)}, f32[704,1024]{1,0:T(8,128)}) fusion(f32[1024]{0:T(1024)S(1)} %bitcast.176, f32[1024]{0:T(1024)S(1)} %bitcast.191, f32[2,352,1024]{2,1,0:T(8,128)S(1)} %fusion.18, bf16[704,1024]{1,0:T(8,128)(2,1)} %shard_map.333, bf16[1024,1024]{1,0:T(8,128)(2,1)} %bitcast.27), kind=kOutput, calls=%fused_computation.43 | convolution fusion | flops 1478557696 | bytes 12197888 | tf_op jit(solution)/shard_map/dot_general | solution.py:536
  163.9 2.1 reduce_sum.241
  166.0 2.4 multiply_reduce_fusion.6
  170.4 13.4 %multiply_convert_fusion = (bf16[704,4096]{1,0:T(8,128)(2,1)}, f32[704,4096]{1,0:T(8,128)}) fusion(f32[4096]{0:T(1024)S(1)} %bitcast.183, bf16[704,1024]{1,0:T(8,128)(2,1)} %add_convert_fusion.1.a_own, bf16[1024,4096]{1,0:T(8,128)(2,1)} %all-gather.6.cloned.1.call-done), kind=kOutput, calls=%fused_computation.8 | convolution fusion | flops 5922881536 | bytes 27148288 | tf_op jit(solution)/shard_map/dot_general | solution.py:540
  185.5 14.2 %multiply_reduce_fusion.1 = (f32[]{:T(128)}, f32[1024]{0:T(1024)}, f32[704,1024]{1,0:T(8,128)S(1)}, bf16[704,1024]{1,0:T(8,128)(2,1)}) fusion(pred[704]{0:T(1024)(128)(4,1)S(1)} %fusion.26, bf16[704,2048]{1,0:T(8,128)(2,1)} %bitcast.160, f32[1024]{0:T(1024)S(1)} %bitcast.199, f32[]{:T(128)S(6)} %mul.311, f32[2,352,1024]{2,1,0:T(8,128)S(1)} %fusion.18, ...), kind=kOutput, calls=%fused_computation.30 | convolution fusion | flops 5917834240 | bytes 27144904 | tf_op jit(solution)/shard_map/dot_general | solution.py:543
  201.0 12.7 %convert_reduce_fusion = (f32[4096]{0:T(1024)S(1)}, bf16[704,4096]{1,0:T(8,128)(2,1)S(1)}) fusion(f32[704,4096]{1,0:T(8,128)} %get-tuple-element.92, f32[4096]{0:T(1024)S(1)} %bitcast.184, bf16[704,1024]{1,0:T(8,128)(2,1)S(1)} %get-tuple-element.37.refs_0_, bf16[4096,1024]{1,0:T(8,128)(2,1)S(1)} %copy-done.52), kind=kOutput, calls=%fused_computation.7 | convolution fusion | flops 5943062528 | bytes 27164672 | tf_op jit(solution)/shard_map/rd,fd->rf/dot_general | solution.py:573
  213.7 11.5 %multiply_reduce_fusion.2 = (f32[1024]{0:T(1024)S(1)}, f32[704]{0:T(1024)S(1)}, f32[704]{0:T(1024)S(1)}, f32[1024]{0:T(1024)S(1)}, f32[704,1024]{1,0:T(8,128)S(1)}) fusion(f32[704,1024]{1,0:T(8,128)S(1)} %copy-done.4, f32[704]{0:T(1024)S(1)} %add_rsqrt_fusion, f32[704]{0:T(1024)S(1)} %broadcast_multiply_fusion.4, f32[1024]{0:T(1024)S(1)} %bitcast.172, ...), kind=kOutput, calls=%fused_computation.32 | convolution fusion | flops 5912065024 | bytes 19946496 | tf_op jit(solution)/shard_map/rf,df->rd/dot_general | solution.py:592
  225.3 12.5 %multiply_reduce_fusion.3 = (f32[1024]{0:T(1024)S(1)}, f32[704,1024]{1,0:T(8,128)S(1)}) fusion(f32[704,1024]{1,0:T(8,128)S(1)} %copy-done.15, f32[1024]{0:T(1024)S(1)} %bitcast.177, f32[704]{0:T(1024)S(1)} %broadcast_multiply_fusion.2, f32[704,1024]{1,0:T(8,128)S(1)} %copy-done.4, f32[704]{0:T(1024)S(1)} %broadcast_multiply_fusion.4, ...), kind=kLoop, calls=%fused_computation.33 | loop fusion | flops 8649728 | bytes 14442176 | tf_op jit(solution)/shard_map/reduce_sum | solution.py:595
  246.1 4.9 shard_map.338
  251.1 3.2 convolution_convert_fusion.g_rec
  254.3 26.7 %shard_map.334.refs_0_.refs_2_ = bf16[1408,768]{1,0:T(8,128)(2,1)} custom-call(s32[1]{0:T(128)} %bitcast.22.core_ref, bf16[704,3072]{1,0:T(8,128)(2,1)} %fusion.8.src.q_own.k_own.v_own, bf16[704,3072]{1,0:T(8,128)(2,1)} %fusion.8.src.q_own.k_own.v_own, bf16[704,3072]{1,0:T(8,128)(2,1)} %fusion.8.src.q_own.k_own.v_own, ...), custom_call_target="tpu_custom_call" | custom-call | flops 20300431360 | bytes 22713856 | tf_op jit(solution)/shard_map/pallas_call | solution.py:132
  281.0 26.7 %shard_map.335.refs_1_.refs_3_ = bf16[1408,768]{1,0:T(8,128)(2,1)} custom-call(s32[1]{0:T(128)} %bitcast.22.core_ref, bf16[704,3072]{1,0:T(8,128)(2,1)} %fusion.8.src.q_own.k_own.v_own, bf16[704,3072]{1,0:T(8,128)(2,1)} %fusion.8.src.q_own.k_own.v_own, bf16[704,3072]{1,0:T(8,128)(2,1)} %fusion.8.src.q_own.k_own.v_own, ...), custom_call_target="tpu_custom_call" | custom-call | flops 20300431360 | bytes 22713856 | tf_op jit(solution)/shard_map/pallas_call | solution.py:132
  307.8 9.1 %shard_map.337 = bf16[1024,1536]{1,0:T(8,128)(2,1)} custom-call(s32[1]{0:T(128)} %bitcast.22.core_ref, bf16[704,1024]{1,0:T(8,128)(2,1)} %add_convert_fusion.2.a_own, bf16[704,1024]{1,0:T(8,128)(2,1)} %collective-permute-done.13.a_rec, bf16[1408,768]{1,0:T(8,128)(2,1)} %shard_map.334.refs_0_.refs_2_, bf16[1408,768]{1,0:T(8,128)(2,1)} %shard_map.335.refs_1_.refs_3_, ...), custom_call_target="tpu_custom_call" | custom-call | flops 4429185024 | bytes 11534336 | tf_op jit(solution)/shard_map/pallas_call | solution.py:132
  318.5 42.5 %reduce-scatter.5.cloned.1.call-done = bf16[256,1536]{1,0:T(8,128)(2,1)} async-done(((bf16[1024,1536]{1,0:T(8,128)(2,1)}), bf16[256,1536]{1,0:T(8,128)(2,1)}) %reduce-scatter.5.cloned.1.call-update) | async-done | bytes 786448 | tf_op jit(solution)/shard_map/reduce_scatter | solution.py:439
  362.2 11.4 %shard_map.339 = bf16[1024,2048]{1,0:T(8,128)(2,1)} custom-call(s32[1]{0:T(128)} %bitcast.22.core_ref, bf16[704,1024]{1,0:T(8,128)(2,1)} %add_convert_fusion.1.a_own, bf16[704,1024]{1,0:T(8,128)(2,1)} %copy-done.17, bf16[704,4096]{1,0:T(8,128)(2,1)} %copy-done, bf16[704,4096]{1,0:T(8,128)(2,1)} %copy-done, bf16[704,4096]{1,0:T(8,128)(2,1)} %copy-done, ...), custom_call_target="tpu_custom_call" | custom-call | flops 5905580032 | bytes 49020928 | tf_op jit(solution)/shard_map/pallas_call | solution.py:132
  374.9 10.4 %collective-permute-done.19.refs_1_ = bf16[704,1024]{1,0:T(8,128)(2,1)S(1)} collective-permute-done((bf16[704,1024]{1,0:T(8,128)(2,1)S(1)}, bf16[704,1024]{1,0:T(8,128)(2,1)S(1)}, u32[]{:S(2)}, u32[]{:S(2)}) %collective-permute-start.19) | collective-permute-done | bytes 1441824 | tf_op jit(solution)/shard_map/ppermute | solution.py:423
  386.5 12.0 %shard_map.340 = bf16[2048,1024]{1,0:T(8,128)(2,1)} custom-call(s32[1]{0:T(128)} %bitcast.22.core_ref, bf16[704,4096]{1,0:T(8,128)(2,1)} %get-tuple-element.91.a_own, bf16[704,4096]{1,0:T(8,128)(2,1)} %collective-permute-done.18.a_rec, bf16[704,1024]{1,0:T(8,128)(2,1)} %copy-done.18, bf16[704,1024]{1,0:T(8,128)(2,1)} %copy-done.53), custom_call_target="tpu_custom_call" | custom-call | flops 5905580032 | bytes 14417920 | tf_op jit(solution)/shard_map/pallas_call | solution.py:132
  404.8 2.4 collective-permute-start.5
  407.2 6.8 %collective-permute-start.4 = (bf16[344,1024]{1,0:T(8,128)(2,1)}, bf16[344,1024]{1,0:T(8,128)(2,1)}, u32[]{:S(2)}, u32[]{:S(2)}) collective-permute-start(bf16[344,1024]{1,0:T(8,128)(2,1)} %get-tuple-element.56), channel_id=1, source_target_pairs={{0,0},{4,1},{1,2},{5,3},{2,4},{6,5},{3,6},{7,7},{8,8},{12,9},{9,10... | collective-permute-start | bytes 2113544 | tf_op jit(solution)/shard_map/ppermute | solution.py:411
  414.0 6.0 shard_map.336
  420.0 3.2 convert_reduce_fusion.1
  423.5 7.2 %fusion.35 = f32[704,1024]{1,0:T(8,128)S(1)} fusion(bf16[704,3072]{1,0:T(8,128)(2,1)S(1)} %copy-done.7, bf16[1024,3072]{1,0:T(8,128)(2,1)} %all-gather.4.cloned.1.call-done), kind=kOutput, calls=%fused_computation.166 | convolution fusion | flops 4429185024 | bytes 13500416 | tf_op jit(solution)/shard_map/re,de->rd/dot_general | solution.py:639
  433.7 2.6 all-to-all-start.1
  436.4 4.2 fusion.13
  442.3 3.1 collective-permute-start.12
  445.5 6.2 all-to-all-done.1
  454.0 2.0 dynamic-slice_bitcast_fusion.11
  457.2 30.6 %reduce-scatter.9.cloned.1.call-done = bf16[256,2048]{1,0:T(8,128)(2,1)} async-done(((bf16[1024,2048]{1,0:T(8,128)(2,1)}), bf16[256,2048]{1,0:T(8,128)(2,1)}) %reduce-scatter.9.cloned.1.call-update) | async-done | bytes 1048592 | tf_op jit(solution)/shard_map/reduce_scatter | solution.py:439
  487.9 4.6 all-to-all-start.2
  500.8 42.6 %reduce-scatter.11.cloned.1.call-done = bf16[512,1024]{1,0:T(8,128)(2,1)} async-done(((bf16[2048,1024]{1,0:T(8,128)(2,1)}), bf16[512,1024]{1,0:T(8,128)(2,1)}) %reduce-scatter.11.cloned.1.call-update) | async-done | bytes 1048592 | tf_op jit(solution)/shard_map/reduce_scatter | solution.py:439
  543.4 4.6 all-to-all-start.4
  552.6 20.9 %all-to-all-done.4 = bf16[4,128,1024]{2,1,0:T(8,128)(2,1)S(1)} async-done(((bf16[4,128,1024]{2,1,0:T(8,128)(2,1)}), bf16[4,128,1024]{2,1,0:T(8,128)(2,1)S(1)}, u32[]{:S(2)}, u32[]{:S(2)}) %all-to-all-start.4) | async-done | bytes 1048608 | tf_op jit(solution)/shard_map/all_to_all | solution.py:447
  574.7 3.5 all-to-all-start.3
  588.1 15.4 %all-to-all-done.3 = bf16[4,64,2048]{2,1,0:T(8,128)(2,1)S(1)} async-done(((bf16[4,64,2048]{2,1,0:T(8,128)(2,1)}), bf16[4,64,2048]{2,1,0:T(8,128)(2,1)S(1)}, u32[]{:S(2)}, u32[]{:S(2)}) %all-to-all-start.3) | async-done | bytes 1048608 | tf_op jit(solution)/shard_map/all_to_all | solution.py:449
  604.6 3.5 all-to-all-start.5
  617.3 2.4 convert_element_type.163
  619.7 13.6 %all-to-all-done.5 = bf16[4,128,1024]{2,1,0:T(8,128)(2,1)S(1)} async-done(((bf16[4,128,1024]{2,1,0:T(8,128)(2,1)}), bf16[4,128,1024]{2,1,0:T(8,128)(2,1)S(1)}, u32[]{:S(2)}, u32[]{:S(2)}) %all-to-all-start.5) | async-done | bytes 1048608 | tf_op jit(solution)/shard_map/all_to_all | solution.py:449
  (277 shorter events, 97.3 us)
Async XLA Ops:
  7.2 7.9 %copy-start.49 = (bf16[128]{0:T(256)(128)(2,1)S(1)}, bf16[128]{0:T(256)(128)(2,1)}, u32[]{:S(2)}) copy-start(bf16[128]{0:T(256)(128)(2,1)} %param.26) | copy-start | bytes 772
  7.2 7.9 %copy-start.50 = (bf16[128]{0:T(256)(128)(2,1)S(1)}, bf16[128]{0:T(256)(128)(2,1)}, u32[]{:S(2)}) copy-start(bf16[128]{0:T(256)(128)(2,1)} %param.27) | copy-start | bytes 772
  7.2 7.9 %copy-start.51 = (bf16[128]{0:T(256)(128)(2,1)S(1)}, bf16[128]{0:T(256)(128)(2,1)}, u32[]{:S(2)}) copy-start(bf16[128]{0:T(256)(128)(2,1)} %param.29) | copy-start | bytes 772
  7.3 50.9 %all-gather.4.cloned.1.call-start = ((), (), s32[]{:S(2)}) async-start(), calls=%async_computation.10 | async-start | bytes 7077888 | tf_op jit(solution)/shard_map/all_gather | solution.py:512
  8.0 162.4 %all-gather.6.cloned.1.call-start = ((), (), s32[]{:S(2)}) async-start(), calls=%async_computation.11 | async-start | bytes 9437184 | tf_op jit(solution)/shard_map/all_gather | solution.py:516
  8.7 176.7 %all-gather.8.cloned.1.call-start = ((), (), s32[]{:S(2)}) async-start(), calls=%async_computation.12 | async-start | bytes 9437184 | tf_op jit(solution)/shard_map/all_gather | solution.py:517
  9.7 18.8 %collective-permute-start = (bf16[344,1024]{1,0:T(8,128)(2,1)S(1)}, bf16[344,1024]{1,0:T(8,128)(2,1)S(1)}, u32[]{:S(2)}, u32[]{:S(2)}) collective-permute-start(bf16[344,1024]{1,0:T(8,128)(2,1)S(1)} %get-tuple-element.60), channel_id=1, source_target_pairs={{0,0},{1,4},{2,1},{3,5},{4,2},{5,6},{6,3},{7,7},{8,8},{9,12},{10,9... | collective-permute-start | bytes 2113544 | tf_op jit(solution)/shard_map/ppermute | solution.py:396
  10.4 37.5 %collective-permute-start.1 = (bf16[344,1024]{1,0:T(8,128)(2,1)S(1)}, bf16[344,1024]{1,0:T(8,128)(2,1)}, u32[]{:S(2)}, u32[]{:S(2)}) collective-permute-start(bf16[344,1024]{1,0:T(8,128)(2,1)S(1)} %get-tuple-element.61), channel_id=1, source_target_pairs={{0,1},{1,5},{2,0},{3,4},{4,3},{5,7},{6,2},{7,6},{8,9},{9,13},{10,8... | collective-permute-start | bytes 2113544 | tf_op jit(solution)/shard_map/ppermute | solution.py:396
  52.0 133.5 %copy-start.1 = (f32[2,352,1024]{2,1,0:T(8,128)}, f32[2,352,1024]{2,1,0:T(8,128)S(1)}, u32[]{:S(2)}) copy-start(f32[2,352,1024]{2,1,0:T(8,128)S(1)} %fusion.18) | copy-start | bytes 8650756
  72.5 26.4 %collective-permute-start.2 = (bf16[704,1536]{1,0:T(8,128)(2,1)}, bf16[704,1536]{1,0:T(8,128)(2,1)}, u32[]{:S(2)}, u32[]{:S(2)}) collective-permute-start(bf16[704,1536]{1,0:T(8,128)(2,1)} %shard_map.331), channel_id=1, source_target_pairs={{0,4},{1,5},{2,6},{3,7},{4,0},{5,1},{6,2},{7,3},{8,12},{9,13},{10,... | collective-permute-start | bytes 6488072 | tf_op jit(solution)/shard_map/ppermute | solution.py:423
  74.3 83.1 %all-to-all-start = ((bf16[8,128,1024]{2,1,0:T(8,128)(2,1)}), bf16[8,128,1024]{2,1,0:T(8,128)(2,1)}, u32[]{:S(2)}, u32[]{:S(2)}) async-start(bf16[8,128,1024]{2,1,0:T(8,128)(2,1)} %broadcast_in_dim.83), calls=%async_computation | async-start | bytes 4194304 | tf_op jit(solution)/shard_map/all_to_all | solution.py:513
  78.7 239.8 %reduce-scatter.7.cloned.1.call-start = ((), (), s32[]{:S(2)}) async-start(), calls=%async_computation.14 | async-start | bytes 1310720 | tf_op jit(solution)/shard_map/reduce_scatter | solution.py:439
  80.6 14.1 %copy-start.39 = (f32[1,1024]{1,0:T(1,128)S(1)}, f32[1,1024]{1,0:T(1,128)}, u32[]{:S(2)}) copy-start(f32[1,1024]{1,0:T(1,128)} %get-tuple-element.72) | copy-start | bytes 12292
  82.4 56.6 %collective-permute-start.6 = (bf16[344,2048]{1,0:T(8,128)(2,1)}, bf16[344,2048]{1,0:T(8,128)(2,1)}, u32[]{:S(2)}, u32[]{:S(2)}) collective-permute-start(bf16[344,2048]{1,0:T(8,128)(2,1)} %get-tuple-element.48), channel_id=1, source_target_pairs={{0,0},{1,4},{2,1},{3,5},{4,2},{5,6},{6,3},{7,7},{8,8},{9,12},{10,9... | collective-permute-start | bytes 4227080 | tf_op jit(solution)/shard_map/ppermute | solution.py:396
  94.7 55.0 %collective-permute-start.7 = (bf16[344,2048]{1,0:T(8,128)(2,1)}, bf16[344,2048]{1,0:T(8,128)(2,1)}, u32[]{:S(2)}, u32[]{:S(2)}) collective-permute-start(bf16[344,2048]{1,0:T(8,128)(2,1)} %get-tuple-element.49), channel_id=1, source_target_pairs={{0,1},{1,5},{2,0},{3,4},{4,3},{5,7},{6,2},{7,6},{8,9},{9,13},{10,8... | collective-permute-start | bytes 4227080 | tf_op jit(solution)/shard_map/ppermute | solution.py:396
  138.9 14.6 %collective-permute-start.3 = (bf16[704,512]{1,0:T(8,128)(2,1)S(1)}, bf16[704,512]{1,0:T(8,128)(2,1)S(1)}, u32[]{:S(2)}, u32[]{:S(2)}) collective-permute-start(bf16[704,512]{1,0:T(8,128)(2,1)S(1)} %slice.133), channel_id=1, source_target_pairs={{0,4},{1,5},{2,6},{3,7},{4,0},{5,1},{6,2},{7,3},{8,12},{9,13},{10,... | collective-permute-start | bytes 2162696 | tf_op jit(solution)/shard_map/ppermute | solution.py:423
  170.4 15.0 %copy-start.38 = (f32[1,1024]{1,0:T(1,128)S(1)}, f32[1,1024]{1,0:T(1,128)}, u32[]{:S(2)}) copy-start(f32[1,1024]{1,0:T(1,128)} %get-tuple-element.66) | copy-start | bytes 12292
  170.4 15.0 %copy-start.46 = (f32[1,1024]{1,0:T(1,128)S(1)}, f32[1,1024]{1,0:T(1,128)}, u32[]{:S(2)}) copy-start(f32[1,1024]{1,0:T(1,128)} %get-tuple-element.67) | copy-start | bytes 12292
  185.5 15.5 %copy-start.52 = (bf16[4096,1024]{1,0:T(8,128)(2,1)S(1)}, bf16[4096,1024]{1,0:T(8,128)(2,1)}, u32[]{:S(2)}) copy-start(bf16[4096,1024]{1,0:T(8,128)(2,1)} %all-gather.8.cloned.1.call-done) | copy-start | bytes 25165828
  199.6 25.7 %copy-start.5 = (f32[704,1024]{1,0:T(8,128)}, f32[704,1024]{1,0:T(8,128)S(1)}, u32[]{:S(2)}) copy-start(f32[704,1024]{1,0:T(8,128)S(1)} %get-tuple-element.34) | copy-start | bytes 8650756
  201.0 12.7 %copy-start.18 = (bf16[704,1024]{1,0:T(8,128)(2,1)}, bf16[704,1024]{1,0:T(8,128)(2,1)S(1)}, u32[]{:S(2)}) copy-start(bf16[704,1024]{1,0:T(8,128)(2,1)S(1)} %get-tuple-element.37.refs_0_) | copy-start | bytes 4325380
  201.0 12.7 %copy-start.4 = (f32[704,1024]{1,0:T(8,128)S(1)}, f32[704,1024]{1,0:T(8,128)}, u32[]{:S(2)}) copy-start(f32[704,1024]{1,0:T(8,128)} %get-tuple-element.89) | copy-start | bytes 8650756
  213.7 11.6 %copy-start = (bf16[704,4096]{1,0:T(8,128)(2,1)}, bf16[704,4096]{1,0:T(8,128)(2,1)S(1)}, u32[]{:S(2)}) copy-start(bf16[704,4096]{1,0:T(8,128)(2,1)S(1)} %get-tuple-element.95.refs_0_.refs_1_.refs_2_.refs_3_) | copy-start | bytes 17301508
  213.7 11.6 %copy-start.15 = (f32[704,1024]{1,0:T(8,128)S(1)}, f32[704,1024]{1,0:T(8,128)}, u32[]{:S(2)}) copy-start(f32[704,1024]{1,0:T(8,128)} %get-tuple-element.90) | copy-start | bytes 8650756
  239.9 6.1 collective-permute-start.8
  241.7 66.1 %collective-permute-start.13 = (bf16[704,1024]{1,0:T(8,128)(2,1)S(1)}, bf16[704,1024]{1,0:T(8,128)(2,1)}, u32[]{:S(2)}, u32[]{:S(2)}) collective-permute-start(bf16[704,1024]{1,0:T(8,128)(2,1)S(1)} %copy-done.20), channel_id=1, source_target_pairs={{0,4},{1,5},{2,6},{3,7},{4,0},{5,1},{6,2},{7,3},{8,12},{9,13},{10,... | collective-permute-start | bytes 4325384 | tf_op jit(solution)/shard_map/ppermute | solution.py:423
  251.0 109.9 %reduce-scatter.5.cloned.1.call-start = ((), (), s32[]{:S(2)}) async-start(), calls=%async_computation.13 | async-start | bytes 3932160 | tf_op jit(solution)/shard_map/reduce_scatter | solution.py:439
  316.9 137.1 %all-reduce.6.cloned.1.call-start = ((), (), s32[]{:S(2)}) async-start(), calls=%async_computation.17 | async-start | bytes 2097152 | tf_op jit(solution)/shard_map/psum | solution.py:645
  317.0 44.1 %collective-permute-start.16 = (bf16[704,4096]{1,0:T(8,128)(2,1)}, bf16[704,4096]{1,0:T(8,128)(2,1)}, u32[]{:S(2)}, u32[]{:S(2)}) collective-permute-start(bf16[704,4096]{1,0:T(8,128)(2,1)} %copy-done), channel_id=1, source_target_pairs={{0,4},{1,5},{2,6},{3,7},{4,0},{5,1},{6,2},{7,3},{8,12},{9,13},{10,... | collective-permute-start | bytes 17301512 | tf_op jit(solution)/shard_map/ppermute | solution.py:423
  318.3 42.8 %collective-permute-start.15 = (bf16[704,1024]{1,0:T(8,128)(2,1)S(1)}, bf16[704,1024]{1,0:T(8,128)(2,1)S(1)}, u32[]{:S(2)}, u32[]{:S(2)}) collective-permute-start(bf16[704,1024]{1,0:T(8,128)(2,1)S(1)} %copy-done.11), channel_id=1, source_target_pairs={{0,4},{1,5},{2,6},{3,7},{4,0},{5,1},{6,2},{7,3},{8,12},{9,13},{10,... | collective-permute-start | bytes 4325384 | tf_op jit(solution)/shard_map/ppermute | solution.py:423
  361.0 126.8 %reduce-scatter.9.cloned.1.call-start = ((), (), s32[]{:S(2)}) async-start(), calls=%async_computation.15 | async-start | bytes 5242880 | tf_op jit(solution)/shard_map/reduce_scatter | solution.py:439
  373.6 169.9 %reduce-scatter.11.cloned.1.call-start = ((), (), s32[]{:S(2)}) async-start(), calls=%async_computation.16 | async-start | bytes 5242880 | tf_op jit(solution)/shard_map/reduce_scatter | solution.py:439
  373.6 11.8 %collective-permute-start.18 = (bf16[704,4096]{1,0:T(8,128)(2,1)}, bf16[704,4096]{1,0:T(8,128)(2,1)}, u32[]{:S(2)}, u32[]{:S(2)}) collective-permute-start(bf16[704,4096]{1,0:T(8,128)(2,1)} %get-tuple-element.91.a_own), channel_id=1, source_target_pairs={{0,4},{1,5},{2,6},{3,7},{4,0},{5,1},{6,2},{7,3},{8,12},{9,13},{10,... | collective-permute-start | bytes 17301512 | tf_op jit(solution)/shard_map/ppermute | solution.py:423
  374.9 10.4 %collective-permute-start.19 = (bf16[704,1024]{1,0:T(8,128)(2,1)S(1)}, bf16[704,1024]{1,0:T(8,128)(2,1)S(1)}, u32[]{:S(2)}, u32[]{:S(2)}) collective-permute-start(bf16[704,1024]{1,0:T(8,128)(2,1)S(1)} %copy-done.19), channel_id=1, source_target_pairs={{0,4},{1,5},{2,6},{3,7},{4,0},{5,1},{6,2},{7,3},{8,12},{9,13},{10,... | collective-permute-start | bytes 4325384 | tf_op jit(solution)/shard_map/ppermute | solution.py:423
  402.2 11.8 %collective-permute-start.9 = (bf16[704,768]{1,0:T(8,128)(2,1)}, bf16[704,768]{1,0:T(8,128)(2,1)}, u32[]{:S(2)}, u32[]{:S(2)}) collective-permute-start(bf16[704,768]{1,0:T(8,128)(2,1)} %slice.179), channel_id=1, source_target_pairs={{0,4},{1,5},{2,6},{3,7},{4,0},{5,1},{6,2},{7,3},{8,12},{9,13},{10,... | collective-permute-start | bytes 3244040 | tf_op jit(solution)/shard_map/ppermute | solution.py:423
  402.4 11.6 %collective-permute-start.10 = (bf16[704,768]{1,0:T(8,128)(2,1)S(1)}, bf16[704,768]{1,0:T(8,128)(2,1)}, u32[]{:S(2)}, u32[]{:S(2)}) collective-permute-start(bf16[704,768]{1,0:T(8,128)(2,1)S(1)} %slice.180), channel_id=1, source_target_pairs={{0,4},{1,5},{2,6},{3,7},{4,0},{5,1},{6,2},{7,3},{8,12},{9,13},{10,... | collective-permute-start | bytes 3244040 | tf_op jit(solution)/shard_map/ppermute | solution.py:423
  404.8 87.7 %collective-permute-start.5 = (bf16[344,1024]{1,0:T(8,128)(2,1)}, bf16[344,1024]{1,0:T(8,128)(2,1)}, u32[]{:S(2)}, u32[]{:S(2)}) collective-permute-start(bf16[344,1024]{1,0:T(8,128)(2,1)} %get-tuple-element.57), channel_id=1, source_target_pairs={{1,0},{5,1},{0,2},{4,3},{3,4},{7,5},{2,6},{6,7},{9,8},{13,9},{8,10... | collective-permute-start | bytes 2113544 | tf_op jit(solution)/shard_map/ppermute | solution.py:411
  407.2 85.3 %collective-permute-start.4 = (bf16[344,1024]{1,0:T(8,128)(2,1)}, bf16[344,1024]{1,0:T(8,128)(2,1)}, u32[]{:S(2)}, u32[]{:S(2)}) collective-permute-start(bf16[344,1024]{1,0:T(8,128)(2,1)} %get-tuple-element.56), channel_id=1, source_target_pairs={{0,0},{4,1},{1,2},{5,3},{2,4},{6,5},{3,6},{7,7},{8,8},{12,9},{9,10... | collective-permute-start | bytes 2113544 | tf_op jit(solution)/shard_map/ppermute | solution.py:411
  433.7 17.9 %all-to-all-start.1 = ((f32[32,15,128]{2,1,0:T(8,128)}), f32[32,15,128]{2,1,0:T(8,128)S(1)}, u32[]{:S(2)}, u32[]{:S(2)}) async-start(f32[32,15,128]{2,1,0:T(8,128)} %bitcast.63), calls=%async_computation.1 | async-start | bytes 524288 | tf_op jit(solution)/shard_map/all_to_all | solution.py:672
  440.8 51.7 %collective-permute-start.11 = (bf16[344,1024]{1,0:T(8,128)(2,1)S(1)}, bf16[344,1024]{1,0:T(8,128)(2,1)}, u32[]{:S(2)}, u32[]{:S(2)}) collective-permute-start(bf16[344,1024]{1,0:T(8,128)(2,1)S(1)} %get-tuple-element.52), channel_id=1, source_target_pairs={{0,0},{4,1},{1,2},{5,3},{2,4},{6,5},{3,6},{7,7},{8,8},{12,9},{9,10... | collective-permute-start | bytes 2113544 | tf_op jit(solution)/shard_map/ppermute | solution.py:411
  442.3 50.1 %collective-permute-start.12 = (bf16[344,1024]{1,0:T(8,128)(2,1)S(1)}, bf16[344,1024]{1,0:T(8,128)(2,1)}, u32[]{:S(2)}, u32[]{:S(2)}) collective-permute-start(bf16[344,1024]{1,0:T(8,128)(2,1)S(1)} %get-tuple-element.53), channel_id=1, source_target_pairs={{1,0},{5,1},{0,2},{4,3},{3,4},{7,5},{2,6},{6,7},{9,8},{13,9},{8,10... | collective-permute-start | bytes 2113544 | tf_op jit(solution)/shard_map/ppermute | solution.py:411
  456.0 42.2 %collective-permute-start.14 = (bf16[128,1536]{1,0:T(8,128)(2,1)}, bf16[128,1536]{1,0:T(8,128)(2,1)S(1)}, u32[]{:S(2)}, u32[]{:S(2)}) collective-permute-start(bf16[128,1536]{1,0:T(8,128)(2,1)} %get-tuple-element.65), channel_id=1, source_target_pairs={{0,4},{1,5},{2,6},{3,7},{4,0},{5,1},{6,2},{7,3},{8,12},{9,13},{10,... | collective-permute-start | bytes 1179656 | tf_op jit(solution)/shard_map/ppermute | solution.py:423
  487.9 55.6 %all-to-all-start.2 = ((bf16[4,64,2048]{2,1,0:T(8,128)(2,1)}), bf16[4,64,2048]{2,1,0:T(8,128)(2,1)S(1)}, u32[]{:S(2)}, u32[]{:S(2)}) async-start(bf16[4,64,2048]{2,1,0:T(8,128)(2,1)} %bitcast.164), calls=%async_computation.5 | async-start | bytes 2097152 | tf_op jit(solution)/shard_map/all_to_all | solution.py:447
  498.2 76.4 %copy-start.16 = (bf16[128,1536]{1,0:T(8,128)(2,1)}, bf16[128,1536]{1,0:T(8,128)(2,1)S(1)}, u32[]{:S(2)}) copy-start(bf16[128,1536]{1,0:T(8,128)(2,1)S(1)} %collective-permute-done.14) | copy-start | bytes 1179652
  543.4 30.1 %all-to-all-start.4 = ((bf16[4,128,1024]{2,1,0:T(8,128)(2,1)}), bf16[4,128,1024]{2,1,0:T(8,128)(2,1)S(1)}, u32[]{:S(2)}, u32[]{:S(2)}) async-start(bf16[4,128,1024]{2,1,0:T(8,128)(2,1)} %bitcast.165), calls=%async_computation.8 | async-start | bytes 2097152 | tf_op jit(solution)/shard_map/all_to_all | solution.py:447
  574.7 28.8 %all-to-all-start.3 = ((bf16[4,64,2048]{2,1,0:T(8,128)(2,1)}), bf16[4,64,2048]{2,1,0:T(8,128)(2,1)S(1)}, u32[]{:S(2)}, u32[]{:S(2)}) async-start(bf16[4,64,2048]{2,1,0:T(8,128)(2,1)} %broadcast_in_dim.90), calls=%async_computation.6 | async-start | bytes 2097152 | tf_op jit(solution)/shard_map/all_to_all | solution.py:449
  604.6 28.8 %all-to-all-start.5 = ((bf16[4,128,1024]{2,1,0:T(8,128)(2,1)}), bf16[4,128,1024]{2,1,0:T(8,128)(2,1)S(1)}, u32[]{:S(2)}, u32[]{:S(2)}) async-start(bf16[4,128,1024]{2,1,0:T(8,128)(2,1)} %broadcast_in_dim.91), calls=%async_computation.9 | async-start | bytes 2097152 | tf_op jit(solution)/shard_map/all_to_all | solution.py:449
  615.9 19.1 %collective-permute-start.17 = (bf16[128,2048]{1,0:T(8,128)(2,1)}, bf16[128,2048]{1,0:T(8,128)(2,1)S(1)}, u32[]{:S(2)}, u32[]{:S(2)}) collective-permute-start(bf16[128,2048]{1,0:T(8,128)(2,1)} %get-tuple-element.63), channel_id=1, source_target_pairs={{0,4},{1,5},{2,6},{3,7},{4,0},{5,1},{6,2},{7,3},{8,12},{9,13},{10,... | collective-permute-start | bytes 1572872 | tf_op jit(solution)/shard_map/ppermute | solution.py:423
  (41 other events, 149.0 us)
Sparse Core Ops, SparseCore 0:
  10.0 48.2 all-gather.3
  60.1 69.1 all-gather.5
  131.2 54.2 all-gather.7
  251.2 27.9 reduce-scatter.6
  317.1 43.8 reduce-scatter.4
  363.3 69.2 all-reduce.5
  435.5 52.2 reduce-scatter.8
  490.8 52.5 reduce-scatter.10

commit v4 on v3

--- a/solution.py
+++ b/solution.py
@@ -344,7 +344,8 @@
                 dst = place(
                     shard // 2 * 2 + seq % 2, 2 * (shard % 2) + (turn + seq // 2) % 2
                 )
-                moves.append((src, dst))
+                if src != dst:
+                    moves.append((src, dst))
         return moves
 
     there = (route(0), route(1))
@@ -391,11 +392,15 @@
         pad = SPAN - tok_dev
         rows = 2 * SPAN
 
+        def move(array, turn, moves):
+            stays = (core == turn_in) & (seq_pos == 2 * core + (turn + turn_out) % 2)
+            return jnp.where(stays, array, lax.ppermute(array, axes, moves))
+
         def bring(array):
             got = [
-                lax.ppermute(
+                move(
                     lax.dynamic_index_in_dim(array, (turn + turn_out) % 2, 0, keepdims=False),
-                    axes,
+                    turn,
                     there[turn],
                 )
                 for turn in range(2)
@@ -408,9 +413,9 @@
         def give(array):
             parts = array.reshape(2, SPAN, array.shape[-1])[:, :tok_dev]
             got = [
-                lax.ppermute(
+                move(
                     lax.dynamic_index_in_dim(parts, (turn + seq_pos) % 2, 0, keepdims=False),
-                    axes,
+                    turn,
                     back[turn],
                 )
                 for turn in range(2)
@@ -510,8 +515,17 @@
         live = live[:, None]
 
         qkv_mat = lax.all_gather(w_qkv, "shard", axis=0, tiled=True)
-        out_mat = lax.all_to_all(
-            jnp.broadcast_to(w_out[None], (n_shard, dl, width)), "shard", 0, 0, tiled=True
+        out_own = lax.all_to_all(
+            jnp.broadcast_to(w_out[None], (n_shard // 2, dl, width)),
+            "shard",
+            0,
+            0,
+            axis_index_groups=chips,
+            tiled=True,
+        )
+        out_rec = exchange(out_own)
+        out_mat = jnp.stack(
+            [jnp.where(core == 0, out_own, out_rec), jnp.where(core == 0, out_rec, out_own)], axis=1
         ).reshape(width, width)
         up_mat = lax.all_gather(w_up, "shard", axis=0, tiled=True)
         down_mat = lax.all_gather(w_down, "shard", axis=0, tiled=True)

time: 657 us -> 678 us (1.032)
  waiting for transfers between devices: 220 us -> 243 us
  starting transfers between devices: 58.1 us -> 50.9 us
    all_to_all x1, waiting for transfers between devices: 0.01 us -> 17.1 us  [inner(): lax.all_to_all(jnp.broadcast_to(w_out[None], (n_shard // 2, dl, width)),...]
    ppermute x8, waiting for transfers between devices: 30.2 us -> 47.3 us  [move(): return jnp.where(stays, array, lax.ppermute(array, axes, moves))]
    reduce_scatter x4, waiting for transfers between devices: 116 us -> 101 us  [scatter(): lax.psum_scatter(array, 'shard', scatter_dimension=0, axis_index_groups=c...]
    ppermute x8, starting transfers between devices: 31.3 us -> 18.5 us  [move(): return jnp.where(stays, array, lax.ppermute(array, axes, moves))]
    unnamed x111 -> x131, local copies, waits for them, and re-layouts: 13.8 us -> 15.5 us
  transfers between devices with their start and end apart: 34 -> 35, of which waited for: 12 -> 12; matrix products, arithmetic and copies ran while one was open for 20% -> 19% of each run, Pallas kernels for 22% -> 22%
where the time goes in v4:
time: 678 us; the launch traced here: 667 us
  waiting for transfers between devices  243 us (36%)
  Pallas kernels  144 us (21%)
  other arithmetic  84.3 us (12%)
  matrix products  80.4 us (12%)
  starting transfers between devices  50.9 us (8%)
  local copies, waits for them, and re-layouts  36.1 us (5%)
  between operations  18 us (3%)
  blocking collectives  10.7 us (2%)
    pallas_call x10, Pallas kernels, call(): pl.pallas_call(kernel, grid_spec=pltpu.PrefetchScalarGridSpec(num_scalar_...  144 us
    reduce_scatter x4, waiting for transfers between devices, scatter(): lax.psum_scatter(array, 'shard', scatter_dimension=0, axis_index_groups=c...  101 us
    ppermute x8, waiting for transfers between devices, move(): return jnp.where(stays, array, lax.ppermute(array, axes, moves))  47.3 us
    all_to_all x2, waiting for transfers between devices, z_reduce(): lax.all_to_all(jnp.broadcast_to(total[None], split), 'seq', 0, 0, tiled=T...  29 us
    unnamed x30, other arithmetic  23.8 us
    all_to_all x2, waiting for transfers between devices, z_reduce(): got = lax.all_to_all(array.reshape(split), 'seq', 0, 0, tiled=True)  21 us
    ppermute x8, starting transfers between devices, move(): return jnp.where(stays, array, lax.ppermute(array, axes, moves))  18.5 us
    all_to_all x1, waiting for transfers between devices, inner(): lax.all_to_all(jnp.broadcast_to(w_out[None], (n_shard // 2, dl, width)),...  17.1 us
  transfers between devices with their start and end apart: 35, of which 12 were waited for; matrix products, arithmetic and copies ran while one was open for 19% of the time, Pallas kernels for 22%

profile of v4, /device:TPU:0, one launch (start us, length us, event | category | flops | bytes accessed | tf_op | source)
XLA Modules:
  0.0 667.5 jit_solution(8709092217102705175)
XLA Ops:
  10.5 4.3 collective-permute-start.1
  15.2 2.6 concatenate.64
  17.8 10.7 %all_gather.12 = bf16[15,1024]{1,0:T(8,128)(2,1)S(1)} all-gather(bf16[15,128]{1,0:T(8,128)(2,1)} %concatenate.64), channel_id=1, replica_groups=mesh['shard'=8,'seq'=4] {'shard'}, dimensions={1}, use_global_device_ids=true | all-gather | bytes 34560 | tf_op jit(solution)/shard_map/all_gather | solution.py:491
  33.0 15.1 %collective-permute-done.1 = bf16[344,1024]{1,0:T(8,128)(2,1)} collective-permute-done((bf16[344,1024]{1,0:T(8,128)(2,1)S(1)}, bf16[344,1024]{1,0:T(8,128)(2,1)}, u32[]{:S(2)}, u32[]{:S(2)}) %collective-permute-start.1) | collective-permute-done | bytes 704544 | tf_op jit(solution)/shard_map/ppermute | solution.py:397
  54.2 4.0 all-gather.4.cloned.1.call-done
  58.2 9.9 %fusion.8.src.q_own.k_own.v_own = bf16[704,3072]{1,0:T(8,128)(2,1)} fusion(bf16[704,1024]{1,0:T(8,128)(2,1)} %add_convert_fusion.2.a_own, bf16[1024,3072]{1,0:T(8,128)(2,1)} %all-gather.4.cloned.1.call-done, f32[3072]{0:T(1024)S(1)} %copy-done.50, bf16[3072]{0:T(1024)(128)(2,1)S(1)} %copy-done.64), kind=kOutput, calls=%fused_computation.15 | convolution fusion | flops 4435673088 | bytes 12077056 | tf_op jit(solution)/shard_map/dot_general | solution.py:543
  68.1 4.8 shard_map.331
  76.9 2.1 collective-permute-start.8
  80.1 4.3 all-to-all-start
  89.2 17.1 %all-to-all-done = bf16[4,128,1024]{2,1,0:T(8,128)(2,1)} async-done(((bf16[4,128,1024]{2,1,0:T(8,128)(2,1)}), bf16[4,128,1024]{2,1,0:T(8,128)(2,1)}, u32[]{:S(2)}, u32[]{:S(2)}) %all-to-all-start) | async-done | bytes 1048608 | tf_op jit(solution)/shard_map/all_to_all | solution.py:518
  106.3 4.0 collective-permute-start.4
  110.3 32.2 %collective-permute-done.8 = bf16[344,2048]{1,0:T(8,128)(2,1)} collective-permute-done((bf16[344,2048]{1,0:T(8,128)(2,1)}, bf16[344,2048]{1,0:T(8,128)(2,1)}, u32[]{:S(2)}, u32[]{:S(2)}) %collective-permute-start.8) | collective-permute-done | bytes 1409056 | tf_op jit(solution)/shard_map/ppermute | solution.py:397
  144.6 38.8 %shard_map.332 = (bf16[1408,512]{1,0:T(8,128)(2,1)}, f32[4,16,1408]{2,1,0:T(8,128)}) custom-call(s32[1]{0:T(128)} %bitcast.22.core_ref, bf16[704,3072]{1,0:T(8,128)(2,1)} %fusion.8.src.q_own.k_own.v_own, bf16[704,3072]{1,0:T(8,128)(2,1)} %fusion.8.src.q_own.k_own.v_own, bf16[704,3072]{1,0:T(8,128)(2,1)} %fusion.8.src.q_own.k_own.v_own, ...), custom_call_target="tpu_custom_call" | custom-call | flops 16240345088 | bytes 19469824 | tf_op jit(solution)/shard_map/pallas_call | solution.py:132
  189.2 3.1 shard_map.333
  192.3 5.5 multiply_add_fusion
  199.8 2.4 multiply_reduce_fusion.6
  204.1 13.3 %multiply_convert_fusion = (bf16[704,4096]{1,0:T(8,128)(2,1)}, f32[704,4096]{1,0:T(8,128)}) fusion(f32[4096]{0:T(1024)S(1)} %bitcast.189, bf16[704,1024]{1,0:T(8,128)(2,1)} %add_convert_fusion.1.a_own, bf16[1024,4096]{1,0:T(8,128)(2,1)} %all-gather.6.cloned.1.call-done), kind=kOutput, calls=%fused_computation.8 | convolution fusion | flops 5922881536 | bytes 27148288 | tf_op jit(solution)/shard_map/dot_general | solution.py:554
  217.4 14.1 %multiply_reduce_fusion.1 = (f32[]{:T(128)}, f32[1024]{0:T(1024)}, f32[704,1024]{1,0:T(8,128)S(1)}, bf16[704,1024]{1,0:T(8,128)(2,1)}) fusion(pred[704]{0:T(1024)(128)(4,1)S(1)} %fusion.27, bf16[704,2048]{1,0:T(8,128)(2,1)} %bitcast.165, f32[1024]{0:T(1024)S(1)} %bitcast.205, f32[]{:T(128)S(6)} %mul.322, f32[2,352,1024]{2,1,0:T(8,128)S(1)} %fusion.18, ...), kind=kOutput, calls=%fused_computation.30 | convolution fusion | flops 5917834240 | bytes 27144904 | tf_op jit(solution)/shard_map/dot_general | solution.py:557
  232.9 13.3 %convert_reduce_fusion = (f32[4096]{0:T(1024)}, bf16[704,4096]{1,0:T(8,128)(2,1)S(1)}) fusion(f32[704,4096]{1,0:T(8,128)} %get-tuple-element.94, f32[4096]{0:T(1024)S(1)} %bitcast.190, bf16[704,1024]{1,0:T(8,128)(2,1)S(1)} %get-tuple-element.37.refs_0_, bf16[4096,1024]{1,0:T(8,128)(2,1)S(1)} %copy-done.62), kind=kOutput, calls=%fused_computation.7 | convolution fusion | flops 5943062528 | bytes 27164672 | tf_op jit(solution)/shard_map/rd,fd->rf/dot_general | solution.py:587
  246.2 12.1 %multiply_reduce_fusion.2 = (f32[1024]{0:T(1024)}, f32[704]{0:T(1024)S(1)}, f32[704]{0:T(1024)S(1)}, f32[1024]{0:T(1024)}, f32[704,1024]{1,0:T(8,128)S(1)}) fusion(f32[704,1024]{1,0:T(8,128)S(1)} %copy-done.4, f32[704]{0:T(1024)S(1)} %add_rsqrt_fusion, f32[704]{0:T(1024)S(1)} %broadcast_multiply_fusion.4, f32[1024]{0:T(1024)S(1)} %bitcast.178, ...), kind=kOutput, calls=%fused_computation.32 | convolution fusion | flops 5912065024 | bytes 19946496 | tf_op jit(solution)/shard_map/rf,df->rd/dot_general | solution.py:606
  258.4 12.7 %multiply_reduce_fusion.3 = (f32[1024]{0:T(1024)S(1)}, f32[704,1024]{1,0:T(8,128)S(1)}) fusion(f32[704,1024]{1,0:T(8,128)S(1)} %copy-done.21, f32[1024]{0:T(1024)S(1)} %bitcast.183, f32[704]{0:T(1024)S(1)} %broadcast_multiply_fusion.2, f32[704,1024]{1,0:T(8,128)S(1)} %copy-done.4, f32[704]{0:T(1024)S(1)} %broadcast_multiply_fusion.4, ...), kind=kLoop, calls=%fused_computation.33 | loop fusion | flops 8649728 | bytes 14442176 | tf_op jit(solution)/shard_map/reduce_sum | solution.py:609
  280.5 5.0 shard_map.338
  285.5 3.2 convolution_convert_fusion.g_rec
  288.7 26.9 %shard_map.334.refs_0_.refs_2_ = bf16[1408,768]{1,0:T(8,128)(2,1)} custom-call(s32[1]{0:T(128)} %bitcast.22.core_ref, bf16[704,3072]{1,0:T(8,128)(2,1)} %fusion.8.src.q_own.k_own.v_own, bf16[704,3072]{1,0:T(8,128)(2,1)} %fusion.8.src.q_own.k_own.v_own, bf16[704,3072]{1,0:T(8,128)(2,1)} %fusion.8.src.q_own.k_own.v_own, ...), custom_call_target="tpu_custom_call" | custom-call | flops 20300431360 | bytes 22713856 | tf_op jit(solution)/shard_map/pallas_call | solution.py:132
  315.6 26.7 %shard_map.335.refs_1_.refs_3_ = bf16[1408,768]{1,0:T(8,128)(2,1)} custom-call(s32[1]{0:T(128)} %bitcast.22.core_ref, bf16[704,3072]{1,0:T(8,128)(2,1)} %fusion.8.src.q_own.k_own.v_own, bf16[704,3072]{1,0:T(8,128)(2,1)} %fusion.8.src.q_own.k_own.v_own, bf16[704,3072]{1,0:T(8,128)(2,1)} %fusion.8.src.q_own.k_own.v_own, ...), custom_call_target="tpu_custom_call" | custom-call | flops 20300431360 | bytes 22713856 | tf_op jit(solution)/shard_map/pallas_call | solution.py:132
  342.4 9.1 %shard_map.337 = bf16[1024,1536]{1,0:T(8,128)(2,1)} custom-call(s32[1]{0:T(128)} %bitcast.22.core_ref, bf16[704,1024]{1,0:T(8,128)(2,1)} %add_convert_fusion.2.a_own, bf16[704,1024]{1,0:T(8,128)(2,1)} %collective-permute-done.14.a_rec, bf16[1408,768]{1,0:T(8,128)(2,1)} %shard_map.334.refs_0_.refs_2_, bf16[1408,768]{1,0:T(8,128)(2,1)} %shard_map.335.refs_1_.refs_3_, ...), custom_call_target="tpu_custom_call" | custom-call | flops 4429185024 | bytes 11534336 | tf_op jit(solution)/shard_map/pallas_call | solution.py:132
  353.3 40.4 %reduce-scatter.5.cloned.1.call-done = bf16[256,1536]{1,0:T(8,128)(2,1)} async-done(((bf16[1024,1536]{1,0:T(8,128)(2,1)}), bf16[256,1536]{1,0:T(8,128)(2,1)}) %reduce-scatter.5.cloned.1.call-update) | async-done | bytes 786448 | tf_op jit(solution)/shard_map/reduce_scatter | solution.py:444
  394.9 11.4 %shard_map.339 = bf16[1024,2048]{1,0:T(8,128)(2,1)} custom-call(s32[1]{0:T(128)} %bitcast.22.core_ref, bf16[704,1024]{1,0:T(8,128)(2,1)} %add_convert_fusion.1.a_own, bf16[704,1024]{1,0:T(8,128)(2,1)} %copy-done.23, bf16[704,4096]{1,0:T(8,128)(2,1)} %copy-done, bf16[704,4096]{1,0:T(8,128)(2,1)} %copy-done, bf16[704,4096]{1,0:T(8,128)(2,1)} %copy-done, ...), custom_call_target="tpu_custom_call" | custom-call | flops 5905580032 | bytes 49020928 | tf_op jit(solution)/shard_map/pallas_call | solution.py:132
  407.6 10.4 %collective-permute-done.20.refs_1_ = bf16[704,1024]{1,0:T(8,128)(2,1)S(1)} collective-permute-done((bf16[704,1024]{1,0:T(8,128)(2,1)S(1)}, bf16[704,1024]{1,0:T(8,128)(2,1)S(1)}, u32[]{:S(2)}, u32[]{:S(2)}) %collective-permute-start.20) | collective-permute-done | bytes 1441824 | tf_op jit(solution)/shard_map/ppermute | solution.py:428
  419.2 12.0 %shard_map.340 = bf16[2048,1024]{1,0:T(8,128)(2,1)} custom-call(s32[1]{0:T(128)} %bitcast.22.core_ref, bf16[704,4096]{1,0:T(8,128)(2,1)} %get-tuple-element.93.a_own, bf16[704,4096]{1,0:T(8,128)(2,1)} %collective-permute-done.19.a_rec, bf16[704,1024]{1,0:T(8,128)(2,1)} %copy-done.24, bf16[704,1024]{1,0:T(8,128)(2,1)} %copy-done.63), custom_call_target="tpu_custom_call" | custom-call | flops 5905580032 | bytes 14417920 | tf_op jit(solution)/shard_map/pallas_call | solution.py:132
  439.0 3.1 collective-permute-start.6
  442.2 6.0 shard_map.336
  448.1 3.2 convert_reduce_fusion.1
  451.7 7.2 %fusion.36 = f32[704,1024]{1,0:T(8,128)S(1)} fusion(bf16[704,3072]{1,0:T(8,128)(2,1)S(1)} %copy-done.7, bf16[1024,3072]{1,0:T(8,128)(2,1)} %all-gather.4.cloned.1.call-done), kind=kOutput, calls=%fused_computation.179 | convolution fusion | flops 4429185024 | bytes 13500416 | tf_op jit(solution)/shard_map/re,de->rd/dot_general | solution.py:653
  462.0 4.3 all-to-all-start.1
  466.3 4.5 fusion.13
  472.6 3.2 collective-permute-start.13
  475.7 11.5 %all-to-all-done.1 = f32[32,15,128]{2,1,0:T(8,128)S(1)} async-done(((f32[32,15,128]{2,1,0:T(8,128)}), f32[32,15,128]{2,1,0:T(8,128)S(1)}, u32[]{:S(2)}, u32[]{:S(2)}) %all-to-all-start.1) | async-done | bytes 245792 | tf_op jit(solution)/shard_map/all_to_all | solution.py:686
  492.2 17.9 %reduce-scatter.9.cloned.1.call-done = bf16[256,2048]{1,0:T(8,128)(2,1)} async-done(((bf16[1024,2048]{1,0:T(8,128)(2,1)}), bf16[256,2048]{1,0:T(8,128)(2,1)}) %reduce-scatter.9.cloned.1.call-update) | async-done | bytes 1048592 | tf_op jit(solution)/shard_map/reduce_scatter | solution.py:444
  510.1 4.6 all-to-all-start.2
  523.0 42.7 %reduce-scatter.11.cloned.1.call-done = bf16[512,1024]{1,0:T(8,128)(2,1)} async-done(((bf16[2048,1024]{1,0:T(8,128)(2,1)}), bf16[512,1024]{1,0:T(8,128)(2,1)}) %reduce-scatter.11.cloned.1.call-update) | async-done | bytes 1048592 | tf_op jit(solution)/shard_map/reduce_scatter | solution.py:444
  565.7 4.6 all-to-all-start.4
  574.9 21.0 %all-to-all-done.4 = bf16[4,128,1024]{2,1,0:T(8,128)(2,1)S(1)} async-done(((bf16[4,128,1024]{2,1,0:T(8,128)(2,1)}), bf16[4,128,1024]{2,1,0:T(8,128)(2,1)S(1)}, u32[]{:S(2)}, u32[]{:S(2)}) %all-to-all-start.4) | async-done | bytes 1048608 | tf_op jit(solution)/shard_map/all_to_all | solution.py:452
  597.0 3.5 all-to-all-start.3
  610.4 15.4 %all-to-all-done.3 = bf16[4,64,2048]{2,1,0:T(8,128)(2,1)S(1)} async-done(((bf16[4,64,2048]{2,1,0:T(8,128)(2,1)}), bf16[4,64,2048]{2,1,0:T(8,128)(2,1)S(1)}, u32[]{:S(2)}, u32[]{:S(2)}) %all-to-all-start.3) | async-done | bytes 1048608 | tf_op jit(solution)/shard_map/all_to_all | solution.py:454
  626.8 3.5 all-to-all-start.5
  639.6 2.4 convert_element_type.163
  642.0 13.6 %all-to-all-done.5 = bf16[4,128,1024]{2,1,0:T(8,128)(2,1)S(1)} async-done(((bf16[4,128,1024]{2,1,0:T(8,128)(2,1)}), bf16[4,128,1024]{2,1,0:T(8,128)(2,1)S(1)}, u32[]{:S(2)}, u32[]{:S(2)}) %all-to-all-start.5) | async-done | bytes 1048608 | tf_op jit(solution)/shard_map/all_to_all | solution.py:454
  (301 shorter events, 105.9 us)
Async XLA Ops:
  7.3 51.0 %all-gather.4.cloned.1.call-start = ((), (), s32[]{:S(2)}) async-start(), calls=%async_computation.10 | async-start | bytes 7077888 | tf_op jit(solution)/shard_map/all_gather | solution.py:517
  8.0 196.1 %all-gather.6.cloned.1.call-start = ((), (), s32[]{:S(2)}) async-start(), calls=%async_computation.11 | async-start | bytes 9437184 | tf_op jit(solution)/shard_map/all_gather | solution.py:530
  8.7 208.7 %all-gather.8.cloned.1.call-start = ((), (), s32[]{:S(2)}) async-start(), calls=%async_computation.12 | async-start | bytes 9437184 | tf_op jit(solution)/shard_map/all_gather | solution.py:531
  9.7 21.6 %copy-start.27 = (bf16[2,344,1024]{2,1,0:T(8,128)(2,1)S(1)}, bf16[2,344,1024]{2,1,0:T(8,128)(2,1)}, u32[]{:S(2)}) copy-start(bf16[2,344,1024]{2,1,0:T(8,128)(2,1)} %param.22) | copy-start | bytes 4227076
  9.7 21.8 %collective-permute-start = (bf16[344,1024]{1,0:T(8,128)(2,1)S(1)}, bf16[344,1024]{1,0:T(8,128)(2,1)S(1)}, u32[]{:S(2)}, u32[]{:S(2)}) collective-permute-start(bf16[344,1024]{1,0:T(8,128)(2,1)S(1)} %get-tuple-element.63), channel_id=1, source_target_pairs={{1,4},{2,1},{3,5},{4,2},{5,6},{6,3},{9,12},{10,9},{11,13},{12,10},... | collective-permute-start | bytes 2113544 | tf_op jit(solution)/shard_map/ppermute | solution.py:397
  10.5 37.5 %collective-permute-start.1 = (bf16[344,1024]{1,0:T(8,128)(2,1)S(1)}, bf16[344,1024]{1,0:T(8,128)(2,1)}, u32[]{:S(2)}, u32[]{:S(2)}) collective-permute-start(bf16[344,1024]{1,0:T(8,128)(2,1)S(1)} %get-tuple-element.62), channel_id=1, source_target_pairs={{0,1},{1,5},{2,0},{3,4},{4,3},{5,7},{6,2},{7,6},{8,9},{9,13},{10,8... | collective-permute-start | bytes 2113544 | tf_op jit(solution)/shard_map/ppermute | solution.py:397
  52.2 165.2 %copy-start.1 = (f32[2,352,1024]{2,1,0:T(8,128)}, f32[2,352,1024]{2,1,0:T(8,128)S(1)}, u32[]{:S(2)}) copy-start(f32[2,352,1024]{2,1,0:T(8,128)S(1)} %fusion.18) | copy-start | bytes 8650756
  72.9 71.7 %collective-permute-start.2 = (bf16[704,1536]{1,0:T(8,128)(2,1)}, bf16[704,1536]{1,0:T(8,128)(2,1)}, u32[]{:S(2)}, u32[]{:S(2)}) collective-permute-start(bf16[704,1536]{1,0:T(8,128)(2,1)} %shard_map.331), channel_id=1, source_target_pairs={{0,4},{1,5},{2,6},{3,7},{4,0},{5,1},{6,2},{7,3},{8,12},{9,13},{10,... | collective-permute-start | bytes 6488072 | tf_op jit(solution)/shard_map/ppermute | solution.py:428
  75.0 9.4 %copy-start.43 = (f32[1,1024]{1,0:T(1,128)S(1)}, f32[1,1024]{1,0:T(1,128)}, u32[]{:S(2)}) copy-start(f32[1,1024]{1,0:T(1,128)} %get-tuple-element.74) | copy-start | bytes 12292
  75.0 35.3 %collective-permute-start.7 = (bf16[344,2048]{1,0:T(8,128)(2,1)}, bf16[344,2048]{1,0:T(8,128)(2,1)}, u32[]{:S(2)}, u32[]{:S(2)}) collective-permute-start(bf16[344,2048]{1,0:T(8,128)(2,1)} %get-tuple-element.55), channel_id=1, source_target_pairs={{1,4},{2,1},{3,5},{4,2},{5,6},{6,3},{9,12},{10,9},{11,13},{12,10},... | collective-permute-start | bytes 4227080 | tf_op jit(solution)/shard_map/ppermute | solution.py:397
  76.9 65.6 %collective-permute-start.8 = (bf16[344,2048]{1,0:T(8,128)(2,1)}, bf16[344,2048]{1,0:T(8,128)(2,1)}, u32[]{:S(2)}, u32[]{:S(2)}) collective-permute-start(bf16[344,2048]{1,0:T(8,128)(2,1)} %get-tuple-element.54), channel_id=1, source_target_pairs={{0,1},{1,5},{2,0},{3,4},{4,3},{5,7},{6,2},{7,6},{8,9},{9,13},{10,8... | collective-permute-start | bytes 4227080 | tf_op jit(solution)/shard_map/ppermute | solution.py:397
  80.1 26.2 %all-to-all-start = ((bf16[4,128,1024]{2,1,0:T(8,128)(2,1)}), bf16[4,128,1024]{2,1,0:T(8,128)(2,1)}, u32[]{:S(2)}, u32[]{:S(2)}) async-start(bf16[4,128,1024]{2,1,0:T(8,128)(2,1)} %broadcast_in_dim.83), calls=%async_computation | async-start | bytes 2097152 | tf_op jit(solution)/shard_map/all_to_all | solution.py:518
  84.4 268.9 %reduce-scatter.7.cloned.1.call-start = ((), (), s32[]{:S(2)}) async-start(), calls=%async_computation.14 | async-start | bytes 1310720 | tf_op jit(solution)/shard_map/reduce_scatter | solution.py:444
  106.3 80.2 %collective-permute-start.4 = (bf16[4,128,1024]{2,1,0:T(8,128)(2,1)}, bf16[4,128,1024]{2,1,0:T(8,128)(2,1)S(1)}, u32[]{:S(2)}, u32[]{:S(2)}) collective-permute-start(bf16[4,128,1024]{2,1,0:T(8,128)(2,1)} %all-to-all-done), channel_id=1, source_target_pairs={{0,4},{1,5},{2,6},{3,7},{4,0},{5,1},{6,2},{7,3},{8,12},{9,13},{10,... | collective-permute-start | bytes 3145736 | tf_op jit(solution)/shard_map/ppermute | solution.py:428
  184.5 4.7 collective-permute-start.3
  204.1 13.3 %copy-start.42 = (f32[1,1024]{1,0:T(1,128)S(1)}, f32[1,1024]{1,0:T(1,128)}, u32[]{:S(2)}) copy-start(f32[1,1024]{1,0:T(1,128)} %get-tuple-element.68) | copy-start | bytes 12292
  204.1 13.3 %copy-start.57 = (f32[1,1024]{1,0:T(1,128)S(1)}, f32[1,1024]{1,0:T(1,128)}, u32[]{:S(2)}) copy-start(f32[1,1024]{1,0:T(1,128)} %get-tuple-element.69) | copy-start | bytes 12292
  217.4 15.5 %copy-start.62 = (bf16[4096,1024]{1,0:T(8,128)(2,1)S(1)}, bf16[4096,1024]{1,0:T(8,128)(2,1)}, u32[]{:S(2)}) copy-start(bf16[4096,1024]{1,0:T(8,128)(2,1)} %all-gather.8.cloned.1.call-done) | copy-start | bytes 25165828
  231.6 26.8 %copy-start.5 = (f32[704,1024]{1,0:T(8,128)}, f32[704,1024]{1,0:T(8,128)S(1)}, u32[]{:S(2)}) copy-start(f32[704,1024]{1,0:T(8,128)S(1)} %get-tuple-element.34) | copy-start | bytes 8650756
  232.9 13.3 %copy-start.24 = (bf16[704,1024]{1,0:T(8,128)(2,1)}, bf16[704,1024]{1,0:T(8,128)(2,1)S(1)}, u32[]{:S(2)}) copy-start(bf16[704,1024]{1,0:T(8,128)(2,1)S(1)} %get-tuple-element.37.refs_0_) | copy-start | bytes 4325380
  232.9 13.3 %copy-start.4 = (f32[704,1024]{1,0:T(8,128)S(1)}, f32[704,1024]{1,0:T(8,128)}, u32[]{:S(2)}) copy-start(f32[704,1024]{1,0:T(8,128)} %get-tuple-element.91) | copy-start | bytes 8650756
  246.2 12.2 %copy-start = (bf16[704,4096]{1,0:T(8,128)(2,1)}, bf16[704,4096]{1,0:T(8,128)(2,1)S(1)}, u32[]{:S(2)}) copy-start(bf16[704,4096]{1,0:T(8,128)(2,1)S(1)} %get-tuple-element.97.refs_0_.refs_1_.refs_2_.refs_3_) | copy-start | bytes 17301508
  246.2 12.2 %copy-start.21 = (f32[704,1024]{1,0:T(8,128)S(1)}, f32[704,1024]{1,0:T(8,128)}, u32[]{:S(2)}) copy-start(f32[704,1024]{1,0:T(8,128)} %get-tuple-element.92) | copy-start | bytes 8650756
  258.4 14.3 %copy-start.46 = (f32[1,1024]{1,0:T(1,128)S(1)}, f32[1,1024]{1,0:T(1,128)}, u32[]{:S(2)}) copy-start(f32[1,1024]{1,0:T(1,128)} %get-tuple-element.72) | copy-start | bytes 12292
  273.8 6.7 %collective-permute-start.9 = (bf16[704,1024]{1,0:T(8,128)(2,1)S(1)}, bf16[704,1024]{1,0:T(8,128)(2,1)}, u32[]{:S(2)}, u32[]{:S(2)}) collective-permute-start(bf16[704,1024]{1,0:T(8,128)(2,1)S(1)} %get-tuple-element.41.refs_0_), channel_id=1, source_target_pairs={{0,4},{1,5},{2,6},{3,7},{4,0},{5,1},{6,2},{7,3},{8,12},{9,13},{10,... | collective-permute-start | bytes 4325384 | tf_op jit(solution)/shard_map/ppermute | solution.py:428
  277.2 65.1 %collective-permute-start.14 = (bf16[704,1024]{1,0:T(8,128)(2,1)}, bf16[704,1024]{1,0:T(8,128)(2,1)}, u32[]{:S(2)}, u32[]{:S(2)}) collective-permute-start(bf16[704,1024]{1,0:T(8,128)(2,1)} %add_convert_fusion.2.a_own), channel_id=1, source_target_pairs={{0,4},{1,5},{2,6},{3,7},{4,0},{5,1},{6,2},{7,3},{8,12},{9,13},{10,... | collective-permute-start | bytes 4325384 | tf_op jit(solution)/shard_map/ppermute | solution.py:428
  285.5 108.2 %reduce-scatter.5.cloned.1.call-start = ((), (), s32[]{:S(2)}) async-start(), calls=%async_computation.13 | async-start | bytes 3932160 | tf_op jit(solution)/shard_map/reduce_scatter | solution.py:444
  351.5 138.0 %all-reduce.6.cloned.1.call-start = ((), (), s32[]{:S(2)}) async-start(), calls=%async_computation.17 | async-start | bytes 2097152 | tf_op jit(solution)/shard_map/psum | solution.py:659
  351.6 42.2 %collective-permute-start.17 = (bf16[704,4096]{1,0:T(8,128)(2,1)}, bf16[704,4096]{1,0:T(8,128)(2,1)}, u32[]{:S(2)}, u32[]{:S(2)}) collective-permute-start(bf16[704,4096]{1,0:T(8,128)(2,1)} %copy-done), channel_id=1, source_target_pairs={{0,4},{1,5},{2,6},{3,7},{4,0},{5,1},{6,2},{7,3},{8,12},{9,13},{10,... | collective-permute-start | bytes 17301512 | tf_op jit(solution)/shard_map/ppermute | solution.py:428
  352.9 40.9 %collective-permute-start.16 = (bf16[704,1024]{1,0:T(8,128)(2,1)S(1)}, bf16[704,1024]{1,0:T(8,128)(2,1)S(1)}, u32[]{:S(2)}, u32[]{:S(2)}) collective-permute-start(bf16[704,1024]{1,0:T(8,128)(2,1)S(1)} %copy-done.17), channel_id=1, source_target_pairs={{0,4},{1,5},{2,6},{3,7},{4,0},{5,1},{6,2},{7,3},{8,12},{9,13},{10,... | collective-permute-start | bytes 4325384 | tf_op jit(solution)/shard_map/ppermute | solution.py:428
  393.7 116.4 %reduce-scatter.9.cloned.1.call-start = ((), (), s32[]{:S(2)}) async-start(), calls=%async_computation.15 | async-start | bytes 5242880 | tf_op jit(solution)/shard_map/reduce_scatter | solution.py:444
  406.3 159.4 %reduce-scatter.11.cloned.1.call-start = ((), (), s32[]{:S(2)}) async-start(), calls=%async_computation.16 | async-start | bytes 5242880 | tf_op jit(solution)/shard_map/reduce_scatter | solution.py:444
  406.3 11.8 %collective-permute-start.19 = (bf16[704,4096]{1,0:T(8,128)(2,1)}, bf16[704,4096]{1,0:T(8,128)(2,1)}, u32[]{:S(2)}, u32[]{:S(2)}) collective-permute-start(bf16[704,4096]{1,0:T(8,128)(2,1)} %get-tuple-element.93.a_own), channel_id=1, source_target_pairs={{0,4},{1,5},{2,6},{3,7},{4,0},{5,1},{6,2},{7,3},{8,12},{9,13},{10,... | collective-permute-start | bytes 17301512 | tf_op jit(solution)/shard_map/ppermute | solution.py:428
  407.6 10.4 %collective-permute-start.20 = (bf16[704,1024]{1,0:T(8,128)(2,1)S(1)}, bf16[704,1024]{1,0:T(8,128)(2,1)S(1)}, u32[]{:S(2)}, u32[]{:S(2)}) collective-permute-start(bf16[704,1024]{1,0:T(8,128)(2,1)S(1)} %copy-done.25), channel_id=1, source_target_pairs={{0,4},{1,5},{2,6},{3,7},{4,0},{5,1},{6,2},{7,3},{8,12},{9,13},{10,... | collective-permute-start | bytes 4325384 | tf_op jit(solution)/shard_map/ppermute | solution.py:428
  434.9 7.2 %collective-permute-start.10 = (bf16[704,768]{1,0:T(8,128)(2,1)}, bf16[704,768]{1,0:T(8,128)(2,1)}, u32[]{:S(2)}, u32[]{:S(2)}) collective-permute-start(bf16[704,768]{1,0:T(8,128)(2,1)} %slice.179), channel_id=1, source_target_pairs={{0,4},{1,5},{2,6},{3,7},{4,0},{5,1},{6,2},{7,3},{8,12},{9,13},{10,... | collective-permute-start | bytes 3244040 | tf_op jit(solution)/shard_map/ppermute | solution.py:428
  435.1 7.0 %collective-permute-start.11 = (bf16[704,768]{1,0:T(8,128)(2,1)S(1)}, bf16[704,768]{1,0:T(8,128)(2,1)}, u32[]{:S(2)}, u32[]{:S(2)}) collective-permute-start(bf16[704,768]{1,0:T(8,128)(2,1)S(1)} %slice.180), channel_id=1, source_target_pairs={{0,4},{1,5},{2,6},{3,7},{4,0},{5,1},{6,2},{7,3},{8,12},{9,13},{10,... | collective-permute-start | bytes 3244040 | tf_op jit(solution)/shard_map/ppermute | solution.py:428
  437.5 77.2 %collective-permute-start.5 = (bf16[344,1024]{1,0:T(8,128)(2,1)}, bf16[344,1024]{1,0:T(8,128)(2,1)}, u32[]{:S(2)}, u32[]{:S(2)}) collective-permute-start(bf16[344,1024]{1,0:T(8,128)(2,1)} %get-tuple-element.61), channel_id=1, source_target_pairs={{4,1},{1,2},{5,3},{2,4},{6,5},{3,6},{12,9},{9,10},{13,11},{10,12},... | collective-permute-start | bytes 2113544 | tf_op jit(solution)/shard_map/ppermute | solution.py:397
  439.0 75.7 %collective-permute-start.6 = (bf16[344,1024]{1,0:T(8,128)(2,1)}, bf16[344,1024]{1,0:T(8,128)(2,1)}, u32[]{:S(2)}, u32[]{:S(2)}) collective-permute-start(bf16[344,1024]{1,0:T(8,128)(2,1)} %get-tuple-element.60), channel_id=1, source_target_pairs={{1,0},{5,1},{0,2},{4,3},{3,4},{7,5},{2,6},{6,7},{9,8},{13,9},{8,10... | collective-permute-start | bytes 2113544 | tf_op jit(solution)/shard_map/ppermute | solution.py:397
  462.0 25.2 %all-to-all-start.1 = ((f32[32,15,128]{2,1,0:T(8,128)}), f32[32,15,128]{2,1,0:T(8,128)S(1)}, u32[]{:S(2)}, u32[]{:S(2)}) async-start(f32[32,15,128]{2,1,0:T(8,128)} %bitcast.65), calls=%async_computation.1 | async-start | bytes 524288 | tf_op jit(solution)/shard_map/all_to_all | solution.py:686
  471.0 43.7 %collective-permute-start.12 = (bf16[344,1024]{1,0:T(8,128)(2,1)S(1)}, bf16[344,1024]{1,0:T(8,128)(2,1)}, u32[]{:S(2)}, u32[]{:S(2)}) collective-permute-start(bf16[344,1024]{1,0:T(8,128)(2,1)S(1)} %get-tuple-element.59), channel_id=1, source_target_pairs={{4,1},{1,2},{5,3},{2,4},{6,5},{3,6},{12,9},{9,10},{13,11},{10,12},... | collective-permute-start | bytes 2113544 | tf_op jit(solution)/shard_map/ppermute | solution.py:397
  472.6 42.2 %collective-permute-start.13 = (bf16[344,1024]{1,0:T(8,128)(2,1)S(1)}, bf16[344,1024]{1,0:T(8,128)(2,1)}, u32[]{:S(2)}, u32[]{:S(2)}) collective-permute-start(bf16[344,1024]{1,0:T(8,128)(2,1)S(1)} %get-tuple-element.58), channel_id=1, source_target_pairs={{1,0},{5,1},{0,2},{4,3},{3,4},{7,5},{2,6},{6,7},{9,8},{13,9},{8,10... | collective-permute-start | bytes 2113544 | tf_op jit(solution)/shard_map/ppermute | solution.py:397
  491.5 28.9 %collective-permute-start.15 = (bf16[128,1536]{1,0:T(8,128)(2,1)}, bf16[128,1536]{1,0:T(8,128)(2,1)S(1)}, u32[]{:S(2)}, u32[]{:S(2)}) collective-permute-start(bf16[128,1536]{1,0:T(8,128)(2,1)} %get-tuple-element.67), channel_id=1, source_target_pairs={{0,4},{1,5},{2,6},{3,7},{4,0},{5,1},{6,2},{7,3},{8,12},{9,13},{10,... | collective-permute-start | bytes 1179656 | tf_op jit(solution)/shard_map/ppermute | solution.py:428
  510.1 55.6 %all-to-all-start.2 = ((bf16[4,64,2048]{2,1,0:T(8,128)(2,1)}), bf16[4,64,2048]{2,1,0:T(8,128)(2,1)S(1)}, u32[]{:S(2)}, u32[]{:S(2)}) async-start(bf16[4,64,2048]{2,1,0:T(8,128)(2,1)} %bitcast.168), calls=%async_computation.5 | async-start | bytes 2097152 | tf_op jit(solution)/shard_map/all_to_all | solution.py:452
  520.4 76.6 %copy-start.22 = (bf16[128,1536]{1,0:T(8,128)(2,1)}, bf16[128,1536]{1,0:T(8,128)(2,1)S(1)}, u32[]{:S(2)}) copy-start(bf16[128,1536]{1,0:T(8,128)(2,1)S(1)} %collective-permute-done.15) | copy-start | bytes 1179652
  565.7 30.2 %all-to-all-start.4 = ((bf16[4,128,1024]{2,1,0:T(8,128)(2,1)}), bf16[4,128,1024]{2,1,0:T(8,128)(2,1)S(1)}, u32[]{:S(2)}, u32[]{:S(2)}) async-start(bf16[4,128,1024]{2,1,0:T(8,128)(2,1)} %bitcast.169), calls=%async_computation.8 | async-start | bytes 2097152 | tf_op jit(solution)/shard_map/all_to_all | solution.py:452
  597.0 28.8 %all-to-all-start.3 = ((bf16[4,64,2048]{2,1,0:T(8,128)(2,1)}), bf16[4,64,2048]{2,1,0:T(8,128)(2,1)S(1)}, u32[]{:S(2)}, u32[]{:S(2)}) async-start(bf16[4,64,2048]{2,1,0:T(8,128)(2,1)} %broadcast_in_dim.90), calls=%async_computation.6 | async-start | bytes 2097152 | tf_op jit(solution)/shard_map/all_to_all | solution.py:454
  626.8 28.8 %all-to-all-start.5 = ((bf16[4,128,1024]{2,1,0:T(8,128)(2,1)}), bf16[4,128,1024]{2,1,0:T(8,128)(2,1)S(1)}, u32[]{:S(2)}, u32[]{:S(2)}) async-start(bf16[4,128,1024]{2,1,0:T(8,128)(2,1)} %broadcast_in_dim.91), calls=%async_computation.9 | async-start | bytes 2097152 | tf_op jit(solution)/shard_map/all_to_all | solution.py:454
  638.2 19.1 %collective-permute-start.18 = (bf16[128,2048]{1,0:T(8,128)(2,1)}, bf16[128,2048]{1,0:T(8,128)(2,1)S(1)}, u32[]{:S(2)}, u32[]{:S(2)}) collective-permute-start(bf16[128,2048]{1,0:T(8,128)(2,1)} %get-tuple-element.65), channel_id=1, source_target_pairs={{0,4},{1,5},{2,6},{3,7},{4,0},{5,1},{6,2},{7,3},{8,12},{9,13},{10,... | collective-permute-start | bytes 1572872 | tf_op jit(solution)/shard_map/ppermute | solution.py:428
  (52 other events, 193.1 us)
Sparse Core Ops, SparseCore 0:
  9.9 48.2 all-gather.3
  60.1 63.6 all-gather.5
  125.7 53.5 all-gather.7
  285.6 26.2 reduce-scatter.6
  351.6 42.0 reduce-scatter.4
  396.0 55.4 all-reduce.5
  454.4 55.6 reduce-scatter.8
  513.0 52.5 reduce-scatter.10

commit v5 on v4

--- a/solution.py
+++ b/solution.py
@@ -147,22 +147,18 @@
 def head_blocks(half, pairs, first=0):
     wide = 2 * HEAD_DIM
     own = [
-        pl.BlockSpec(
-            (half, wide),
-            lambda pair, core, part=part: (0, 2 * (part * pairs + pair + first) + core[0]),
-        )
-        for part in range(3)
+        pl.BlockSpec((half, wide), lambda pair, core, at=at: (0, 2 * (at + pair + first) + core[0]))
+        for at in (0, pairs, 0)
     ]
     rec = [
-        pl.BlockSpec((half, wide), lambda pair, core, part=part: (0, part * pairs + pair + first))
-        for part in range(3)
+        pl.BlockSpec((half, wide), lambda pair, core, at=at: (0, at + pair + first))
+        for at in (0, pairs, 0)
     ]
     return own + rec
 
 
-def attention(core, qkv, rec, bias):
-    half = rec.shape[0]
-    width = rec.shape[1] // 3
+def attention(core, heads, bias):
+    half, width = heads[-1].shape
     wide = 2 * HEAD_DIM
     pairs = width // wide
     full = 2 * half
@@ -170,7 +166,7 @@
     return call(
         forward_kernel,
         core,
-        (qkv, qkv, qkv, rec, rec, rec, bias.reshape(1, full)),
+        heads + (bias.reshape(1, full),),
         (pairs,),
         head_blocks(half, pairs) + [pl.BlockSpec((1, full), lambda pair, core: (0, 0))],
         [
@@ -187,10 +183,10 @@
     )
 
 
-def attention_back(core, qkv, rec, g_own, g_rec, mixed, lse, bias, first, last):
-    half = rec.shape[0]
+def attention_back(core, heads, g_own, g_rec, mixed, lse, bias, first, last):
+    half, width = heads[-1].shape
     wide = 2 * HEAD_DIM
-    pairs = rec.shape[1] // 3 // wide
+    pairs = width // wide
     here = last - first
     full = 2 * half
     col = pl.BlockSpec((half, wide), lambda pair, core: (0, pair + first))
@@ -198,7 +194,7 @@
     return call(
         backward_kernel,
         core,
-        (qkv, qkv, qkv, rec, rec, rec, g_own, g_rec, mixed, lse, bias.reshape(full, 1)),
+        heads + (g_own, g_rec, mixed, lse, bias.reshape(full, 1)),
         (here,),
         head_blocks(half, pairs, first)
         + [
@@ -514,19 +510,22 @@
         key_bias = jnp.where(live_all, 0.0, DEAD).astype(F32)
         live = live[:, None]
 
-        qkv_mat = lax.all_gather(w_qkv, "shard", axis=0, tiled=True)
-        out_own = lax.all_to_all(
-            jnp.broadcast_to(w_out[None], (n_shard // 2, dl, width)),
-            "shard",
-            0,
-            0,
-            axis_index_groups=chips,
-            tiled=True,
-        )
-        out_rec = exchange(out_own)
-        out_mat = jnp.stack(
-            [jnp.where(core == 0, out_own, out_rec), jnp.where(core == 0, out_rec, out_own)], axis=1
-        ).reshape(width, width)
+        def gather(array):
+            own = lax.all_to_all(
+                jnp.broadcast_to(array[None], (n_shard // 2,) + array.shape),
+                "shard",
+                0,
+                0,
+                axis_index_groups=chips,
+                tiled=True,
+            )
+            rec = exchange(own)
+            both = [jnp.where(core == 0, own, rec), jnp.where(core == 0, rec, own)]
+            return jnp.stack(both, axis=1).reshape(n_shard * array.shape[0], array.shape[1])
+
+        qk_mat = lax.all_gather(w_qkv[:, : 2 * width], "shard", axis=0, tiled=True)
+        v_mat = gather(w_qkv[:, 2 * width :])
+        out_mat = gather(w_out)
         up_mat = lax.all_gather(w_up, "shard", axis=0, tiled=True)
         down_mat = lax.all_gather(w_down, "shard", axis=0, tiled=True)
 
@@ -536,13 +535,16 @@
         x_rows = bring(inputs).astype(F32)
         normed1 = (norm_parts(x_rows)[0] * gain1 + shift1).astype(BF16)
         normed1_rec = exchange(normed1)
-        qkv_bias = jnp.concatenate([qbias, jnp.zeros_like(qbias), vbias])
+        qk_bias = jnp.concatenate([qbias, jnp.zeros_like(qbias)])
         scale = jnp.concatenate(
-            [jnp.full((width,), HEAD_DIM ** (-0.5), BF16), jnp.ones((2 * width,), BF16)]
-        )
-        qkv = (jnp.dot(normed1, qkv_mat, preferred_element_type=F32) + qkv_bias).astype(BF16) * scale
-        rec = exchange(pick_other(core_arr, qkv, unit))
-        mixed_mine, lse = attention(core_arr, qkv, rec, key_bias)
+            [jnp.full((width,), HEAD_DIM ** (-0.5), BF16), jnp.ones((width,), BF16)]
+        )
+        qk = (jnp.dot(normed1, qk_mat, preferred_element_type=F32) + qk_bias).astype(BF16) * scale
+        value = (jnp.dot(normed1, v_mat, preferred_element_type=F32) + vbias).astype(BF16)
+        qk_rec = exchange(pick_other(core_arr, qk, unit))
+        value_rec = exchange(pick_other(core_arr, value, unit))
+        heads = (qk, qk, value, qk_rec, qk_rec, value_rec)
+        mixed_mine, lse = attention(core_arr, heads, key_bias)
         both = bring(jnp.concatenate([teacher, cotangent], axis=-1))
         teach_rows = both[:, :width].astype(F32)
         cot_rows = both[:, width:].astype(F32)
@@ -628,29 +630,32 @@
         g_mine = (mixed_grad(g_attn), mixed_grad(g_attn_rec))
         pairs = width // 2 // unit
         g_alls = [
-            attention_back(
-                core_arr, qkv, rec, *g_mine, mixed_mine, lse, key_bias, first, first + pairs // 2
-            )
-            for first in (0, pairs // 2)
+            attention_back(core_arr, heads, *g_mine, mixed_mine, lse, key_bias, first, last)
+            for first, last in ((0, 1), (1, pairs - 1), (pairs - 1, pairs))
         ]
         g_recs = [exchange(part[rows:]) for part in g_alls]
-        order = [
-            pair // 2 * 6 + part * 2 + pair % 2 for part in range(3) for pair in range(pairs)
-        ]
-        half_cols = 3 * width // 4
+        order = []
+        for part in range(3):
+            for first, last in ((0, 1), (1, pairs - 1), (pairs - 1, pairs)):
+                order += [3 * first + part * (last - first) + idx for idx in range(last - first)]
         w_qkv_part = weight_grad(
             core_arr,
             (normed1, normed1_rec) + tuple(g_alls) * 2,
             [strip, strip]
-            + [pl.BlockSpec((rows, half_cols), lambda i, core: (0, 0))] * 2
-            + [pl.BlockSpec((rows, half_cols), lambda i, core: (1, 0))] * 2,
+            + [
+                pl.BlockSpec((rows, part.shape[1]), lambda i, core, side=side: (side, 0))
+                for side in range(2)
+                for part in g_alls
+            ],
             (width, 3 * width // 2),
             tile,
         )
         p_qkv = scatter(w_qkv_part, unit, 1, order)
         g_qkv = merge(core_arr, g_alls, g_recs, rows, unit, 3)
         d_qkv_bias = jnp.sum(g_qkv.astype(F32), axis=0)
-        g_norm1 = jnp.einsum("re,de->rd", g_qkv, qkv_mat, preferred_element_type=F32)
+        g_norm1 = jnp.einsum(
+            "re,de->rd", g_qkv[:, : 2 * width], qk_mat, preferred_element_type=F32
+        ) + jnp.einsum("re,de->rd", g_qkv[:, 2 * width :], v_mat, preferred_element_type=F32)
         g_ln1, d_gain1, d_shift1 = norm_back(x_rows, gain1, g_norm1)
         g_in = give((g_pass + g_resid1 + g_ln1).astype(BF16)).astype(F32)
 

time: 678 us -> 636 us (0.938)
  waiting for transfers between devices: 243 us -> 194 us
    ppermute x8, waiting for transfers between devices: 47.3 us -> 25.1 us  [move(): return jnp.where(stays, array, lax.ppermute(array, axes, moves))]
    all_to_all x1 -> x2, waiting for transfers between devices: 17.1 us -> 0.01 us  [gather(): lax.all_to_all(jnp.broadcast_to(array[None], (n_shard // 2,) + array.shap...]
    reduce_sum x1, other arithmetic: 12.7 us -> 1.72 us  [inner(): d_scale1 = jnp.sum(g_resid1 * attn_out, axis=0)]
    unnamed x30, other arithmetic: 23.8 us -> 32.1 us
    pallas_call x10 -> x12, Pallas kernels: 144 us -> 147 us  [call(): pl.pallas_call(kernel, grid_spec=pltpu.PrefetchScalarGridSpec(num_scalar_...]
    unnamed x131 -> x163, local copies, waits for them, and re-layouts: 15.5 us -> 13.4 us
    dot_general x2 -> x4, matrix products: 17 us -> 16.8 us  [the longest x1 7.43 us: inner(): jnp.dot(normed1, qk_mat, preferred_element_type=F32) + qk_bias]
  transfers between devices with their start and end apart: 35 -> 39, of which waited for: 12 -> 9; matrix products, arithmetic and copies ran while one was open for 19% -> 22% of each run, Pallas kernels for 22% -> 23%
where the time goes in v5:
time: 636 us; the launch traced here: 626 us
  waiting for transfers between devices  194 us (31%)
  Pallas kernels  147 us (23%)
  other arithmetic  80.4 us (13%)
  matrix products  79.8 us (13%)
  starting transfers between devices  54.1 us (9%)
  local copies, waits for them, and re-layouts  39.2 us (6%)
  between operations  18.3 us (3%)
  blocking collectives  13.5 us (2%)
    pallas_call x12, Pallas kernels, call(): pl.pallas_call(kernel, grid_spec=pltpu.PrefetchScalarGridSpec(num_scalar_...  147 us
    reduce_scatter x4, waiting for transfers between devices, scatter(): lax.psum_scatter(array, 'shard', scatter_dimension=0, axis_index_groups=c...  99.7 us
    unnamed x30, other arithmetic  32.1 us
    all_to_all x2, waiting for transfers between devices, z_reduce(): lax.all_to_all(jnp.broadcast_to(total[None], split), 'seq', 0, 0, tiled=T...  29 us
    ppermute x8, waiting for transfers between devices, move(): return jnp.where(stays, array, lax.ppermute(array, axes, moves))  25.1 us
    ppermute x8, starting transfers between devices, move(): return jnp.where(stays, array, lax.ppermute(array, axes, moves))  20.8 us
    all_to_all x2, waiting for transfers between devices, z_reduce(): got = lax.all_to_all(array.reshape(split), 'seq', 0, 0, tiled=True)  15.7 us
    dot_general x1, matrix products, inner(): branch = jnp.dot(act, down_mat, preferred_element_type=F32) + dbias  14.3 us
  transfers between devices with their start and end apart: 39, of which 9 were waited for; matrix products, arithmetic and copies ran while one was open for 22% of the time, Pallas kernels for 23%

profile of v5, /device:TPU:0, one launch (start us, length us, event | category | flops | bytes accessed | tf_op | source)
XLA Modules:
  0.0 625.9 jit_solution(494220235810004538)
XLA Ops:
  12.6 3.5 collective-permute-start.1
  17.2 4.3 all-to-all-start
  26.3 4.0 collective-permute-start.10
  30.8 13.5 %all_gather.12 = bf16[15,1024]{1,0:T(8,128)(2,1)S(1)} all-gather(bf16[15,128]{1,0:T(8,128)(2,1)S(1)} %concatenate.64), channel_id=1, replica_groups=mesh['shard'=8,'seq'=4] {'shard'}, dimensions={1}, use_global_device_ids=true | all-gather | bytes 34560 | tf_op jit(solution)/shard_map/all_gather | solution.py:487
  54.2 4.2 all-to-all-start.1
  62.9 2.6 select_bitcast_fusion.5
  65.6 7.4 %fusion.8.src.q_own.k_own = bf16[704,2048]{1,0:T(8,128)(2,1)} fusion(bf16[704,1024]{1,0:T(8,128)(2,1)} %add_convert_fusion.4.a_own, bf16[1024,2048]{1,0:T(8,128)(2,1)} %all-gather.4.cloned.1.call-done, f32[2048]{0:T(1024)S(1)} %copy-done.58, bf16[2048]{0:T(1024)(128)(2,1)S(1)} %copy-done.80), kind=kOutput, calls=%fused_computation.19 | convolution fusion | flops 2957115392 | bytes 8531968 | tf_op jit(solution)/shard_map/dot_general | solution.py:542
  73.0 2.9 shard_map.331
  77.4 2.8 add_convert_fusion.2.src.v_own
  80.2 2.6 shard_map.332
  84.7 25.1 %collective-permute-done.10 = bf16[344,2048]{1,0:T(8,128)(2,1)} collective-permute-done((bf16[344,2048]{1,0:T(8,128)(2,1)S(1)}, bf16[344,2048]{1,0:T(8,128)(2,1)}, u32[]{:S(2)}, u32[]{:S(2)}) %collective-permute-start.10) | collective-permute-done | bytes 1409056 | tf_op jit(solution)/shard_map/ppermute | solution.py:393
  112.8 38.7 %shard_map.333 = (bf16[1408,512]{1,0:T(8,128)(2,1)}, f32[4,16,1408]{2,1,0:T(8,128)}) custom-call(s32[1]{0:T(128)} %bitcast.22.core_ref, bf16[704,2048]{1,0:T(8,128)(2,1)} %fusion.8.src.q_own.k_own, bf16[704,2048]{1,0:T(8,128)(2,1)} %fusion.8.src.q_own.k_own, bf16[704,1024]{1,0:T(8,128)(2,1)} %add_convert_fusion.2.src.v_own, ...), custom_call_target="tpu_custom_call" | custom-call | flops 16240345088 | bytes 10819072 | tf_op jit(solution)/shard_map/pallas_call | solution.py:132
  158.4 2.9 shard_map.334
  161.3 4.7 multiply_add_fusion
  168.3 13.6 %multiply_convert_fusion = (bf16[704,4096]{1,0:T(8,128)(2,1)}, f32[704,4096]{1,0:T(8,128)}) fusion(f32[4096]{0:T(1024)S(1)} %bitcast.204, bf16[704,1024]{1,0:T(8,128)(2,1)} %add_convert_fusion.1.a_own, bf16[1024,4096]{1,0:T(8,128)(2,1)} %all-gather.6.cloned.1.call-done), kind=kOutput, calls=%fused_computation.8 | convolution fusion | flops 5922881536 | bytes 27148288 | tf_op jit(solution)/shard_map/dot_general | solution.py:556
  182.0 14.3 %multiply_reduce_fusion.1 = (f32[]{:T(128)}, f32[1024]{0:T(1024)}, f32[704,1024]{1,0:T(8,128)S(1)}, bf16[704,1024]{1,0:T(8,128)(2,1)}) fusion(pred[704]{0:T(1024)(128)(4,1)S(1)} %copy-done.43, bf16[704,2048]{1,0:T(8,128)(2,1)} %bitcast.173, f32[1024]{0:T(1024)S(1)} %bitcast.217, f32[]{:T(128)S(6)} %mul.336, bf16[1,344,1024]{2,1,0:T(8,128)(2,1)} %copy-done.4, ...), kind=kOutput, calls=%fused_computation.32 | convolution fusion | flops 5922880512 | bytes 25670344 | tf_op jit(solution)/shard_map/dot_general | solution.py:559
  197.7 13.2 %convert_reduce_fusion = (f32[4096]{0:T(1024)}, bf16[704,4096]{1,0:T(8,128)(2,1)S(1)}) fusion(f32[704,4096]{1,0:T(8,128)} %get-tuple-element.96, f32[4096]{0:T(1024)S(1)} %bitcast.205, bf16[704,1024]{1,0:T(8,128)(2,1)S(1)} %get-tuple-element.37.refs_0_, bf16[4096,1024]{1,0:T(8,128)(2,1)S(1)} %copy-done.76), kind=kOutput, calls=%fused_computation.7 | convolution fusion | flops 5943062528 | bytes 27164672 | tf_op jit(solution)/shard_map/rd,fd->rf/dot_general | solution.py:589
  210.9 12.2 %multiply_reduce_fusion.2 = (f32[1024]{0:T(1024)}, f32[704]{0:T(1024)S(1)}, f32[704]{0:T(1024)S(1)}, f32[1024]{0:T(1024)}, f32[704,1024]{1,0:T(8,128)S(1)}) fusion(f32[704,1024]{1,0:T(8,128)S(1)} %get-tuple-element.93, f32[704]{0:T(1024)S(1)} %add_rsqrt_fusion, f32[704]{0:T(1024)S(1)} %broadcast_multiply_fusion.4, f32[1024]{0:T(1024)S(1)} %bitcast.192, ...), kind=kOutput, calls=%fused_computation.34 | convolution fusion | flops 5912065024 | bytes 19946496 | tf_op jit(solution)/shard_map/rf,df->rd/dot_general | solution.py:608
  234.1 4.9 shard_map.340
  239.2 3.2 convolution_convert_fusion.g_rec
  242.4 14.4 %shard_map.335.refs_0_.refs_3_ = bf16[1408,384]{1,0:T(8,128)(2,1)} custom-call(s32[1]{0:T(128)} %bitcast.22.core_ref, bf16[704,2048]{1,0:T(8,128)(2,1)} %fusion.8.src.q_own.k_own, bf16[704,2048]{1,0:T(8,128)(2,1)} %fusion.8.src.q_own.k_own, bf16[704,1024]{1,0:T(8,128)(2,1)} %add_convert_fusion.2.src.v_own, ...), custom_call_target="tpu_custom_call" | custom-call | flops 10150215680 | bytes 14063104 | tf_op jit(solution)/shard_map/pallas_call | solution.py:132
  256.8 14.5 %shard_map.337.refs_2_.refs_5_ = bf16[1408,384]{1,0:T(8,128)(2,1)} custom-call(s32[1]{0:T(128)} %bitcast.22.core_ref, bf16[704,2048]{1,0:T(8,128)(2,1)} %fusion.8.src.q_own.k_own, bf16[704,2048]{1,0:T(8,128)(2,1)} %fusion.8.src.q_own.k_own, bf16[704,1024]{1,0:T(8,128)(2,1)} %add_convert_fusion.2.src.v_own, ...), custom_call_target="tpu_custom_call" | custom-call | flops 10150215680 | bytes 14063104 | tf_op jit(solution)/shard_map/pallas_call | solution.py:132
  271.3 26.7 %shard_map.336.refs_1_.refs_4_ = bf16[1408,768]{1,0:T(8,128)(2,1)} custom-call(s32[1]{0:T(128)} %bitcast.22.core_ref, bf16[704,2048]{1,0:T(8,128)(2,1)} %fusion.8.src.q_own.k_own, bf16[704,2048]{1,0:T(8,128)(2,1)} %fusion.8.src.q_own.k_own, bf16[704,1024]{1,0:T(8,128)(2,1)} %add_convert_fusion.2.src.v_own, ...), custom_call_target="tpu_custom_call" | custom-call | flops 20300431360 | bytes 14063104 | tf_op jit(solution)/shard_map/pallas_call | solution.py:132
  298.0 10.0 %shard_map.339 = bf16[1024,1536]{1,0:T(8,128)(2,1)} custom-call(s32[1]{0:T(128)} %bitcast.22.core_ref, bf16[704,1024]{1,0:T(8,128)(2,1)} %add_convert_fusion.4.a_own, bf16[704,1024]{1,0:T(8,128)(2,1)} %collective-permute-done.17.a_rec, bf16[1408,384]{1,0:T(8,128)(2,1)} %shard_map.335.refs_0_.refs_3_, bf16[1408,768]{1,0:T(8,128)(2,1)} %shard_map.336.refs_1_.refs_4_, ...), custom_call_target="tpu_custom_call" | custom-call | flops 4429185024 | bytes 11534336 | tf_op jit(solution)/shard_map/pallas_call | solution.py:132
  309.7 41.3 %reduce-scatter.5.cloned.1.call-done = bf16[256,1536]{1,0:T(8,128)(2,1)} async-done(((bf16[1024,1536]{1,0:T(8,128)(2,1)}), bf16[256,1536]{1,0:T(8,128)(2,1)}) %reduce-scatter.5.cloned.1.call-update) | async-done | bytes 786448 | tf_op jit(solution)/shard_map/reduce_scatter | solution.py:440
  352.2 11.6 %shard_map.341 = bf16[1024,2048]{1,0:T(8,128)(2,1)} custom-call(s32[1]{0:T(128)} %bitcast.22.core_ref, bf16[704,1024]{1,0:T(8,128)(2,1)} %add_convert_fusion.1.a_own, bf16[704,1024]{1,0:T(8,128)(2,1)} %copy-done.23, bf16[704,4096]{1,0:T(8,128)(2,1)} %copy-done, bf16[704,4096]{1,0:T(8,128)(2,1)} %copy-done, bf16[704,4096]{1,0:T(8,128)(2,1)} %copy-done, ...), custom_call_target="tpu_custom_call" | custom-call | flops 5905580032 | bytes 49020928 | tf_op jit(solution)/shard_map/pallas_call | solution.py:132
  365.2 10.4 %collective-permute-done.23.refs_1_ = bf16[704,1024]{1,0:T(8,128)(2,1)S(1)} collective-permute-done((bf16[704,1024]{1,0:T(8,128)(2,1)S(1)}, bf16[704,1024]{1,0:T(8,128)(2,1)S(1)}, u32[]{:S(2)}, u32[]{:S(2)}) %collective-permute-start.23) | collective-permute-done | bytes 1441824 | tf_op jit(solution)/shard_map/ppermute | solution.py:424
  376.8 12.0 %shard_map.342 = bf16[2048,1024]{1,0:T(8,128)(2,1)} custom-call(s32[1]{0:T(128)} %bitcast.22.core_ref, bf16[704,4096]{1,0:T(8,128)(2,1)} %get-tuple-element.95.a_own, bf16[704,4096]{1,0:T(8,128)(2,1)} %collective-permute-done.22.a_rec, bf16[704,1024]{1,0:T(8,128)(2,1)} %copy-done.24, bf16[704,1024]{1,0:T(8,128)(2,1)} %copy-done.78), custom_call_target="tpu_custom_call" | custom-call | flops 5905580032 | bytes 14417920 | tf_op jit(solution)/shard_map/pallas_call | solution.py:132
  388.8 2.4 slice.200
  395.4 3.4 collective-permute-start.8
  398.8 5.8 shard_map.338
  404.5 3.2 convert_reduce_fusion.1
  408.1 3.4 fusion.23
  411.5 3.2 fusion.19
  417.8 4.1 all-to-all-start.2
  421.9 4.4 fusion.13
  429.4 3.3 collective-permute-start.16
  432.7 12.1 %all-to-all-done.2 = f32[32,15,128]{2,1,0:T(8,128)S(1)} async-done(((f32[32,15,128]{2,1,0:T(8,128)}), f32[32,15,128]{2,1,0:T(8,128)S(1)}, u32[]{:S(2)}, u32[]{:S(2)}) %all-to-all-start.2) | async-done | bytes 245792 | tf_op jit(solution)/shard_map/all_to_all | solution.py:691
  449.8 18.7 %reduce-scatter.9.cloned.1.call-done = bf16[256,2048]{1,0:T(8,128)(2,1)} async-done(((bf16[1024,2048]{1,0:T(8,128)(2,1)}), bf16[256,2048]{1,0:T(8,128)(2,1)}) %reduce-scatter.9.cloned.1.call-update) | async-done | bytes 1048592 | tf_op jit(solution)/shard_map/reduce_scatter | solution.py:440
  468.5 4.6 all-to-all-start.3
  484.3 39.8 %reduce-scatter.11.cloned.1.call-done = bf16[512,1024]{1,0:T(8,128)(2,1)} async-done(((bf16[2048,1024]{1,0:T(8,128)(2,1)}), bf16[512,1024]{1,0:T(8,128)(2,1)}) %reduce-scatter.11.cloned.1.call-update) | async-done | bytes 1048592 | tf_op jit(solution)/shard_map/reduce_scatter | solution.py:440
  524.1 4.6 all-to-all-start.5
  538.6 15.7 %all-to-all-done.5 = bf16[4,128,1024]{2,1,0:T(8,128)(2,1)S(1)} async-done(((bf16[4,128,1024]{2,1,0:T(8,128)(2,1)}), bf16[4,128,1024]{2,1,0:T(8,128)(2,1)S(1)}, u32[]{:S(2)}, u32[]{:S(2)}) %all-to-all-start.5) | async-done | bytes 1048608 | tf_op jit(solution)/shard_map/all_to_all | solution.py:448
  555.3 3.5 all-to-all-start.4
  568.7 15.4 %all-to-all-done.4 = bf16[4,64,2048]{2,1,0:T(8,128)(2,1)S(1)} async-done(((bf16[4,64,2048]{2,1,0:T(8,128)(2,1)}), bf16[4,64,2048]{2,1,0:T(8,128)(2,1)S(1)}, u32[]{:S(2)}, u32[]{:S(2)}) %all-to-all-start.4) | async-done | bytes 1048608 | tf_op jit(solution)/shard_map/all_to_all | solution.py:450
  585.2 3.5 all-to-all-start.6
  597.9 2.4 convert_element_type.174
  600.4 13.6 %all-to-all-done.6 = bf16[4,128,1024]{2,1,0:T(8,128)(2,1)S(1)} async-done(((bf16[4,128,1024]{2,1,0:T(8,128)(2,1)}), bf16[4,128,1024]{2,1,0:T(8,128)(2,1)S(1)}, u32[]{:S(2)}, u32[]{:S(2)}) %all-to-all-start.6) | async-done | bytes 1048608 | tf_op jit(solution)/shard_map/all_to_all | solution.py:450
  (353 shorter events, 119.1 us)
Async XLA Ops:
  7.2 58.4 %all-gather.4.cloned.1.call-start = ((), (), s32[]{:S(2)}) async-start(), calls=%async_computation.11 | async-start | bytes 4718592 | tf_op jit(solution)/shard_map/all_gather | solution.py:526
  9.3 159.1 %all-gather.6.cloned.1.call-start = ((), (), s32[]{:S(2)}) async-start(), calls=%async_computation.12 | async-start | bytes 9437184 | tf_op jit(solution)/shard_map/all_gather | solution.py:529
  10.0 171.9 %all-gather.8.cloned.1.call-start = ((), (), s32[]{:S(2)}) async-start(), calls=%async_computation.13 | async-start | bytes 9437184 | tf_op jit(solution)/shard_map/all_gather | solution.py:530
  10.9 10.7 %copy-start.19 = (bf16[344,1024]{1,0:T(8,128)(2,1)}, bf16[344,1024]{1,0:T(8,128)(2,1)S(1)}, u32[]{:S(2)}) copy-start(bf16[344,1024]{1,0:T(8,128)(2,1)S(1)} %get-tuple-element.65) | copy-start | bytes 2113540
  11.0 39.1 %collective-permute-start = (bf16[344,1024]{1,0:T(8,128)(2,1)S(1)}, bf16[344,1024]{1,0:T(8,128)(2,1)}, u32[]{:S(2)}, u32[]{:S(2)}) collective-permute-start(bf16[344,1024]{1,0:T(8,128)(2,1)S(1)} %get-tuple-element.65), channel_id=1, source_target_pairs={{1,4},{2,1},{3,5},{4,2},{5,6},{6,3},{9,12},{10,9},{11,13},{12,10},... | collective-permute-start | bytes 2113544 | tf_op jit(solution)/shard_map/ppermute | solution.py:393
  12.6 37.5 %collective-permute-start.1 = (bf16[344,1024]{1,0:T(8,128)(2,1)S(1)}, bf16[344,1024]{1,0:T(8,128)(2,1)}, u32[]{:S(2)}, u32[]{:S(2)}) collective-permute-start(bf16[344,1024]{1,0:T(8,128)(2,1)S(1)} %get-tuple-element.64), channel_id=1, source_target_pairs={{0,1},{1,5},{2,0},{3,4},{4,3},{5,7},{6,2},{7,6},{8,9},{9,13},{10,8... | collective-permute-start | bytes 2113544 | tf_op jit(solution)/shard_map/ppermute | solution.py:393
  17.2 34.8 %all-to-all-start = ((bf16[4,128,1024]{2,1,0:T(8,128)(2,1)}), bf16[4,128,1024]{2,1,0:T(8,128)(2,1)}, u32[]{:S(2)}, u32[]{:S(2)}) async-start(bf16[4,128,1024]{2,1,0:T(8,128)(2,1)} %broadcast_in_dim.49), calls=%async_computation | async-start | bytes 2097152 | tf_op jit(solution)/shard_map/all_to_all | solution.py:514
  24.5 60.2 %collective-permute-start.9 = (bf16[344,2048]{1,0:T(8,128)(2,1)}, bf16[344,2048]{1,0:T(8,128)(2,1)}, u32[]{:S(2)}, u32[]{:S(2)}) collective-permute-start(bf16[344,2048]{1,0:T(8,128)(2,1)} %get-tuple-element.55), channel_id=1, source_target_pairs={{1,4},{2,1},{3,5},{4,2},{5,6},{6,3},{9,12},{10,9},{11,13},{12,10},... | collective-permute-start | bytes 4227080 | tf_op jit(solution)/shard_map/ppermute | solution.py:393
  26.3 83.5 %collective-permute-start.10 = (bf16[344,2048]{1,0:T(8,128)(2,1)S(1)}, bf16[344,2048]{1,0:T(8,128)(2,1)}, u32[]{:S(2)}, u32[]{:S(2)}) collective-permute-start(bf16[344,2048]{1,0:T(8,128)(2,1)S(1)} %get-tuple-element.54), channel_id=1, source_target_pairs={{0,1},{1,5},{2,0},{3,4},{4,3},{5,7},{6,2},{7,6},{8,9},{9,13},{10,8... | collective-permute-start | bytes 4227080 | tf_op jit(solution)/shard_map/ppermute | solution.py:393
  54.2 29.9 %all-to-all-start.1 = ((bf16[4,128,1024]{2,1,0:T(8,128)(2,1)}), bf16[4,128,1024]{2,1,0:T(8,128)(2,1)}, u32[]{:S(2)}, u32[]{:S(2)}) async-start(bf16[4,128,1024]{2,1,0:T(8,128)(2,1)} %broadcast_in_dim.52), calls=%async_computation.1 | async-start | bytes 2097152 | tf_op jit(solution)/shard_map/all_to_all | solution.py:514
  58.4 251.3 %reduce-scatter.7.cloned.1.call-start = ((), (), s32[]{:S(2)}) async-start(), calls=%async_computation.15 | async-start | bytes 1310720 | tf_op jit(solution)/shard_map/reduce_scatter | solution.py:440
  58.5 4.4 collective-permute-start.2
  75.9 36.1 %collective-permute-start.3 = (bf16[704,1024]{1,0:T(8,128)(2,1)}, bf16[704,1024]{1,0:T(8,128)(2,1)}, u32[]{:S(2)}, u32[]{:S(2)}) collective-permute-start(bf16[704,1024]{1,0:T(8,128)(2,1)} %shard_map.331), channel_id=1, source_target_pairs={{0,4},{1,5},{2,6},{3,7},{4,0},{5,1},{6,2},{7,3},{8,12},{9,13},{10,... | collective-permute-start | bytes 4325384 | tf_op jit(solution)/shard_map/ppermute | solution.py:424
  82.8 29.2 %collective-permute-start.4 = (bf16[704,512]{1,0:T(8,128)(2,1)}, bf16[704,512]{1,0:T(8,128)(2,1)S(1)}, u32[]{:S(2)}, u32[]{:S(2)}) collective-permute-start(bf16[704,512]{1,0:T(8,128)(2,1)} %shard_map.332), channel_id=1, source_target_pairs={{0,4},{1,5},{2,6},{3,7},{4,0},{5,1},{6,2},{7,3},{8,12},{9,13},{10,... | collective-permute-start | bytes 2162696 | tf_op jit(solution)/shard_map/ppermute | solution.py:424
  84.1 70.6 %collective-permute-start.6 = (bf16[4,128,1024]{2,1,0:T(8,128)(2,1)}, bf16[4,128,1024]{2,1,0:T(8,128)(2,1)S(1)}, u32[]{:S(2)}, u32[]{:S(2)}) collective-permute-start(bf16[4,128,1024]{2,1,0:T(8,128)(2,1)} %all-to-all-done.1), channel_id=1, source_target_pairs={{0,4},{1,5},{2,6},{3,7},{4,0},{5,1},{6,2},{7,3},{8,12},{9,13},{10,... | collective-permute-start | bytes 3145736 | tf_op jit(solution)/shard_map/ppermute | solution.py:424
  152.7 4.9 collective-permute-start.5
  168.3 13.6 %copy-start.43 = (pred[704]{0:T(1024)(128)(4,1)S(1)}, pred[704]{0:T(1024)(128)(4,1)}, u32[]{:S(2)}) copy-start(pred[704]{0:T(1024)(128)(4,1)} %copy-done.42) | copy-start | bytes 2116
  168.3 13.6 %copy-start.47 = (f32[1,1024]{1,0:T(1,128)S(1)}, f32[1,1024]{1,0:T(1,128)}, u32[]{:S(2)}) copy-start(f32[1,1024]{1,0:T(1,128)} %get-tuple-element.70) | copy-start | bytes 12292
  168.3 13.6 %copy-start.62 = (f32[1,1024]{1,0:T(1,128)S(1)}, f32[1,1024]{1,0:T(1,128)}, u32[]{:S(2)}) copy-start(f32[1,1024]{1,0:T(1,128)} %get-tuple-element.71) | copy-start | bytes 12292
  182.0 15.7 %copy-start.76 = (bf16[4096,1024]{1,0:T(8,128)(2,1)S(1)}, bf16[4096,1024]{1,0:T(8,128)(2,1)}, u32[]{:S(2)}) copy-start(bf16[4096,1024]{1,0:T(8,128)(2,1)} %all-gather.8.cloned.1.call-done) | copy-start | bytes 25165828
  196.3 26.8 %copy-start.7 = (f32[704,1024]{1,0:T(8,128)}, f32[704,1024]{1,0:T(8,128)S(1)}, u32[]{:S(2)}) copy-start(f32[704,1024]{1,0:T(8,128)S(1)} %get-tuple-element.34) | copy-start | bytes 8650756
  197.7 13.2 %copy-start.24 = (bf16[704,1024]{1,0:T(8,128)(2,1)}, bf16[704,1024]{1,0:T(8,128)(2,1)S(1)}, u32[]{:S(2)}) copy-start(bf16[704,1024]{1,0:T(8,128)(2,1)S(1)} %get-tuple-element.37.refs_0_) | copy-start | bytes 4325380
  210.9 12.2 %copy-start = (bf16[704,4096]{1,0:T(8,128)(2,1)}, bf16[704,4096]{1,0:T(8,128)(2,1)S(1)}, u32[]{:S(2)}) copy-start(bf16[704,4096]{1,0:T(8,128)(2,1)S(1)} %get-tuple-element.99.refs_0_.refs_1_.refs_2_.refs_3_) | copy-start | bytes 17301508
  210.9 12.2 %copy-start.18 = (f32[704,1024]{1,0:T(8,128)S(1)}, f32[704,1024]{1,0:T(8,128)}, u32[]{:S(2)}) copy-start(f32[704,1024]{1,0:T(8,128)} %get-tuple-element.94) | copy-start | bytes 8650756
  227.4 6.7 %collective-permute-start.11 = (bf16[704,1024]{1,0:T(8,128)(2,1)S(1)}, bf16[704,1024]{1,0:T(8,128)(2,1)}, u32[]{:S(2)}, u32[]{:S(2)}) collective-permute-start(bf16[704,1024]{1,0:T(8,128)(2,1)S(1)} %get-tuple-element.41.refs_0_), channel_id=1, source_target_pairs={{0,4},{1,5},{2,6},{3,7},{4,0},{5,1},{6,2},{7,3},{8,12},{9,13},{10,... | collective-permute-start | bytes 4325384 | tf_op jit(solution)/shard_map/ppermute | solution.py:424
  230.8 67.2 %collective-permute-start.17 = (bf16[704,1024]{1,0:T(8,128)(2,1)}, bf16[704,1024]{1,0:T(8,128)(2,1)}, u32[]{:S(2)}, u32[]{:S(2)}) collective-permute-start(bf16[704,1024]{1,0:T(8,128)(2,1)} %add_convert_fusion.4.a_own), channel_id=1, source_target_pairs={{0,4},{1,5},{2,6},{3,7},{4,0},{5,1},{6,2},{7,3},{8,12},{9,13},{10,... | collective-permute-start | bytes 4325384 | tf_op jit(solution)/shard_map/ppermute | solution.py:424
  239.1 112.0 %reduce-scatter.5.cloned.1.call-start = ((), (), s32[]{:S(2)}) async-start(), calls=%async_computation.14 | async-start | bytes 3932160 | tf_op jit(solution)/shard_map/reduce_scatter | solution.py:440
  308.0 139.1 %all-reduce.7.cloned.1.call-start = ((), (), s32[]{:S(2)}) async-start(), calls=%async_computation.18 | async-start | bytes 2097152 | tf_op jit(solution)/shard_map/psum | solution.py:664
  308.0 43.1 %collective-permute-start.20 = (bf16[704,4096]{1,0:T(8,128)(2,1)}, bf16[704,4096]{1,0:T(8,128)(2,1)}, u32[]{:S(2)}, u32[]{:S(2)}) collective-permute-start(bf16[704,4096]{1,0:T(8,128)(2,1)} %copy-done), channel_id=1, source_target_pairs={{0,4},{1,5},{2,6},{3,7},{4,0},{5,1},{6,2},{7,3},{8,12},{9,13},{10,... | collective-permute-start | bytes 17301512 | tf_op jit(solution)/shard_map/ppermute | solution.py:424
  309.3 41.8 %collective-permute-start.19 = (bf16[704,1024]{1,0:T(8,128)(2,1)S(1)}, bf16[704,1024]{1,0:T(8,128)(2,1)S(1)}, u32[]{:S(2)}, u32[]{:S(2)}) collective-permute-start(bf16[704,1024]{1,0:T(8,128)(2,1)S(1)} %copy-done.15), channel_id=1, source_target_pairs={{0,4},{1,5},{2,6},{3,7},{4,0},{5,1},{6,2},{7,3},{8,12},{9,13},{10,... | collective-permute-start | bytes 4325384 | tf_op jit(solution)/shard_map/ppermute | solution.py:424
  351.1 117.4 %reduce-scatter.9.cloned.1.call-start = ((), (), s32[]{:S(2)}) async-start(), calls=%async_computation.16 | async-start | bytes 5242880 | tf_op jit(solution)/shard_map/reduce_scatter | solution.py:440
  363.9 160.2 %reduce-scatter.11.cloned.1.call-start = ((), (), s32[]{:S(2)}) async-start(), calls=%async_computation.17 | async-start | bytes 5242880 | tf_op jit(solution)/shard_map/reduce_scatter | solution.py:440
  363.9 11.8 %collective-permute-start.22 = (bf16[704,4096]{1,0:T(8,128)(2,1)}, bf16[704,4096]{1,0:T(8,128)(2,1)}, u32[]{:S(2)}, u32[]{:S(2)}) collective-permute-start(bf16[704,4096]{1,0:T(8,128)(2,1)} %get-tuple-element.95.a_own), channel_id=1, source_target_pairs={{0,4},{1,5},{2,6},{3,7},{4,0},{5,1},{6,2},{7,3},{8,12},{9,13},{10,... | collective-permute-start | bytes 17301512 | tf_op jit(solution)/shard_map/ppermute | solution.py:424
  365.2 10.4 %collective-permute-start.23 = (bf16[704,1024]{1,0:T(8,128)(2,1)S(1)}, bf16[704,1024]{1,0:T(8,128)(2,1)S(1)}, u32[]{:S(2)}, u32[]{:S(2)}) collective-permute-start(bf16[704,1024]{1,0:T(8,128)(2,1)S(1)} %copy-done.25), channel_id=1, source_target_pairs={{0,4},{1,5},{2,6},{3,7},{4,0},{5,1},{6,2},{7,3},{8,12},{9,13},{10,... | collective-permute-start | bytes 4325384 | tf_op jit(solution)/shard_map/ppermute | solution.py:424
  391.3 7.5 %collective-permute-start.13 = (bf16[704,768]{1,0:T(8,128)(2,1)}, bf16[704,768]{1,0:T(8,128)(2,1)}, u32[]{:S(2)}, u32[]{:S(2)}) collective-permute-start(bf16[704,768]{1,0:T(8,128)(2,1)} %slice.200), channel_id=1, source_target_pairs={{0,4},{1,5},{2,6},{3,7},{4,0},{5,1},{6,2},{7,3},{8,12},{9,13},{10,... | collective-permute-start | bytes 3244040 | tf_op jit(solution)/shard_map/ppermute | solution.py:424
  392.3 6.4 %collective-permute-start.12 = (bf16[704,384]{1,0:T(8,128)(2,1)}, bf16[704,384]{1,0:T(8,128)(2,1)}, u32[]{:S(2)}, u32[]{:S(2)}) collective-permute-start(bf16[704,384]{1,0:T(8,128)(2,1)} %slice.199), channel_id=1, source_target_pairs={{0,4},{1,5},{2,6},{3,7},{4,0},{5,1},{6,2},{7,3},{8,12},{9,13},{10,... | collective-permute-start | bytes 1622024 | tf_op jit(solution)/shard_map/ppermute | solution.py:424
  392.8 6.0 collective-permute-start.14
  393.9 79.2 %collective-permute-start.7 = (bf16[344,1024]{1,0:T(8,128)(2,1)S(1)}, bf16[344,1024]{1,0:T(8,128)(2,1)}, u32[]{:S(2)}, u32[]{:S(2)}) collective-permute-start(bf16[344,1024]{1,0:T(8,128)(2,1)S(1)} %get-tuple-element.63), channel_id=1, source_target_pairs={{4,1},{1,2},{5,3},{2,4},{6,5},{3,6},{12,9},{9,10},{13,11},{10,12},... | collective-permute-start | bytes 2113544 | tf_op jit(solution)/shard_map/ppermute | solution.py:393
  395.4 77.7 %collective-permute-start.8 = (bf16[344,1024]{1,0:T(8,128)(2,1)S(1)}, bf16[344,1024]{1,0:T(8,128)(2,1)}, u32[]{:S(2)}, u32[]{:S(2)}) collective-permute-start(bf16[344,1024]{1,0:T(8,128)(2,1)S(1)} %get-tuple-element.62), channel_id=1, source_target_pairs={{1,0},{5,1},{0,2},{4,3},{3,4},{7,5},{2,6},{6,7},{9,8},{13,9},{8,10... | collective-permute-start | bytes 2113544 | tf_op jit(solution)/shard_map/ppermute | solution.py:393
  417.8 26.9 %all-to-all-start.2 = ((f32[32,15,128]{2,1,0:T(8,128)}), f32[32,15,128]{2,1,0:T(8,128)S(1)}, u32[]{:S(2)}, u32[]{:S(2)}) async-start(f32[32,15,128]{2,1,0:T(8,128)} %bitcast.69), calls=%async_computation.2 | async-start | bytes 524288 | tf_op jit(solution)/shard_map/all_to_all | solution.py:691
  427.7 45.4 %collective-permute-start.15 = (bf16[344,1024]{1,0:T(8,128)(2,1)}, bf16[344,1024]{1,0:T(8,128)(2,1)}, u32[]{:S(2)}, u32[]{:S(2)}) collective-permute-start(bf16[344,1024]{1,0:T(8,128)(2,1)} %get-tuple-element.61), channel_id=1, source_target_pairs={{4,1},{1,2},{5,3},{2,4},{6,5},{3,6},{12,9},{9,10},{13,11},{10,12},... | collective-permute-start | bytes 2113544 | tf_op jit(solution)/shard_map/ppermute | solution.py:393
  429.4 43.7 %collective-permute-start.16 = (bf16[344,1024]{1,0:T(8,128)(2,1)}, bf16[344,1024]{1,0:T(8,128)(2,1)}, u32[]{:S(2)}, u32[]{:S(2)}) collective-permute-start(bf16[344,1024]{1,0:T(8,128)(2,1)} %get-tuple-element.60), channel_id=1, source_target_pairs={{1,0},{5,1},{0,2},{4,3},{3,4},{7,5},{2,6},{6,7},{9,8},{13,9},{8,10... | collective-permute-start | bytes 2113544 | tf_op jit(solution)/shard_map/ppermute | solution.py:393
  449.0 29.7 %collective-permute-start.18 = (bf16[128,1536]{1,0:T(8,128)(2,1)}, bf16[128,1536]{1,0:T(8,128)(2,1)}, u32[]{:S(2)}, u32[]{:S(2)}) collective-permute-start(bf16[128,1536]{1,0:T(8,128)(2,1)} %get-tuple-element.69), channel_id=1, source_target_pairs={{0,4},{1,5},{2,6},{3,7},{4,0},{5,1},{6,2},{7,3},{8,12},{9,13},{10,... | collective-permute-start | bytes 1179656 | tf_op jit(solution)/shard_map/ppermute | solution.py:424
  468.5 55.6 %all-to-all-start.3 = ((bf16[4,64,2048]{2,1,0:T(8,128)(2,1)}), bf16[4,64,2048]{2,1,0:T(8,128)(2,1)S(1)}, u32[]{:S(2)}, u32[]{:S(2)}) async-start(bf16[4,64,2048]{2,1,0:T(8,128)(2,1)} %bitcast.179), calls=%async_computation.6 | async-start | bytes 2097152 | tf_op jit(solution)/shard_map/all_to_all | solution.py:448
  524.1 30.1 %all-to-all-start.5 = ((bf16[4,128,1024]{2,1,0:T(8,128)(2,1)}), bf16[4,128,1024]{2,1,0:T(8,128)(2,1)S(1)}, u32[]{:S(2)}, u32[]{:S(2)}) async-start(bf16[4,128,1024]{2,1,0:T(8,128)(2,1)} %bitcast.180), calls=%async_computation.9 | async-start | bytes 2097152 | tf_op jit(solution)/shard_map/all_to_all | solution.py:448
  555.3 28.8 %all-to-all-start.4 = ((bf16[4,64,2048]{2,1,0:T(8,128)(2,1)}), bf16[4,64,2048]{2,1,0:T(8,128)(2,1)S(1)}, u32[]{:S(2)}, u32[]{:S(2)}) async-start(bf16[4,64,2048]{2,1,0:T(8,128)(2,1)} %broadcast_in_dim.94), calls=%async_computation.7 | async-start | bytes 2097152 | tf_op jit(solution)/shard_map/all_to_all | solution.py:450
  585.2 28.8 %all-to-all-start.6 = ((bf16[4,128,1024]{2,1,0:T(8,128)(2,1)}), bf16[4,128,1024]{2,1,0:T(8,128)(2,1)S(1)}, u32[]{:S(2)}, u32[]{:S(2)}) async-start(bf16[4,128,1024]{2,1,0:T(8,128)(2,1)} %broadcast_in_dim.95), calls=%async_computation.10 | async-start | bytes 2097152 | tf_op jit(solution)/shard_map/all_to_all | solution.py:450
  596.5 19.1 %collective-permute-start.21 = (bf16[128,2048]{1,0:T(8,128)(2,1)}, bf16[128,2048]{1,0:T(8,128)(2,1)S(1)}, u32[]{:S(2)}, u32[]{:S(2)}) collective-permute-start(bf16[128,2048]{1,0:T(8,128)(2,1)} %get-tuple-element.67), channel_id=1, source_target_pairs={{0,4},{1,5},{2,6},{3,7},{4,0},{5,1},{6,2},{7,3},{8,12},{9,13},{10,... | collective-permute-start | bytes 1572872 | tf_op jit(solution)/shard_map/ppermute | solution.py:424
  (73 other events, 315.0 us)
Sparse Core Ops, SparseCore 0:
  10.5 49.5 all-gather.3
  61.9 54.6 all-gather.5
  118.5 54.2 all-gather.7
  239.2 26.9 reduce-scatter.6
  308.1 42.8 reduce-scatter.4
  353.3 56.4 all-reduce.6
  412.8 55.6 reduce-scatter.8
  471.4 52.5 reduce-scatter.10

commit v6 on v5

--- a/solution.py
+++ b/solution.py
@@ -22,8 +22,21 @@
     return low.astype(dtype), (1.0 - low).astype(dtype)
 
 
+def store_rows(own, away, idx, cols, value):
+    count = own.shape[0] // SPAN
+    row = pl.multiple_of(lax.rem(idx, count) * SPAN, 16)
+
+    @pl.when(idx < count)
+    def _():
+        own[pl.ds(row, SPAN), cols] = value
+
+    @pl.when(idx >= count)
+    def _():
+        away[pl.ds(row, SPAN), cols] = value
+
+
 def forward_kernel(
-    core_ref, q_own, k_own, v_own, q_rec, k_rec, v_rec, bias_ref, o_ref, lse_ref, q_s, k_s, v_s, lse_s
+    core_ref, q_own, k_own, v_own, q_rec, k_rec, v_rec, bias_ref, o_own, o_away, lse_ref, q_s, k_s, v_s, lse_s
 ):
     half = q_own.shape[0]
     for all_ref, own, rec in ((q_s, q_own, q_rec), (k_s, k_own, k_rec), (v_s, v_own, v_rec)):
@@ -46,7 +59,7 @@
             mixed = jnp.dot(weight.astype(BF16), v_s[...], preferred_element_type=F32)
             outs.append(mixed / total)
             sums.append(peak + jnp.log(total))
-        o_ref[pl.ds(row, SPAN), :] = (outs[0] * low + outs[1] * high).astype(BF16)
+        store_rows(o_own, o_away, idx, slice(None), (outs[0] * low + outs[1] * high).astype(BF16))
         lse_s[pl.ds(row, SPAN), :] = sums[0] * low + sums[1] * high
         return carry
 
@@ -66,10 +79,12 @@
     v_rec,
     g_own,
     g_rec,
-    o_ref,
+    o_own,
+    o_away,
     lse_ref,
     bias_ref,
-    d_ref,
+    d_own,
+    d_away,
     q_s,
     k_s,
     v_s,
@@ -77,7 +92,7 @@
     dqt_s,
 ):
     half = q_own.shape[0]
-    width = d_ref.shape[1] // 3
+    width = d_own.shape[1] // 3
     pair = pl.program_id(0)
     cols = [pl.multiple_of(part * width + pair * 2 * HEAD_DIM, 128) for part in range(3)]
     low, high = lane_masks(BF16)
@@ -88,8 +103,8 @@
         for head, mask in enumerate((low, high)):
             all_ref[head, :half, :] = own[...] * mask
             all_ref[head, half:, :] = rec[...] * mask
-    dots_own = jnp.transpose(g_own[...].astype(F32) * o_ref[:half, :].astype(F32))
-    dots_rec = jnp.transpose(g_rec[...].astype(F32) * o_ref[half:, :].astype(F32))
+    dots_own = jnp.transpose(g_own[...].astype(F32) * o_own[...].astype(F32))
+    dots_rec = jnp.transpose(g_rec[...].astype(F32) * o_away[...].astype(F32))
     dots = jnp.concatenate([dots_own, dots_rec], axis=1)
     inner = (
         jnp.sum(dots[:HEAD_DIM], axis=0, keepdims=True),
@@ -118,13 +133,14 @@
             dk = dk + jnp.dot(g_score, query, preferred_element_type=F32)
             rows = slice(HEAD_DIM * head, HEAD_DIM * (head + 1))
             dqt_s[rows, :] += jnp.dot(key_t[rows, :], g_score, preferred_element_type=F32)
-        d_ref[pl.ds(row, SPAN), pl.ds(cols[1], 2 * HEAD_DIM)] = dk.astype(BF16)
-        d_ref[pl.ds(row, SPAN), pl.ds(cols[2], 2 * HEAD_DIM)] = dv.astype(BF16)
+        store_rows(d_own, d_away, idx, pl.ds(cols[1], 2 * HEAD_DIM), dk.astype(BF16))
+        store_rows(d_own, d_away, idx, pl.ds(cols[2], 2 * HEAD_DIM), dv.astype(BF16))
         return carry
 
     lax.fori_loop(0, 2 * half // SPAN, block, 0)
     dq = (jnp.transpose(dqt_s[...]) * HEAD_DIM ** (-0.5)).astype(BF16)
-    d_ref[:, pl.ds(cols[0], 2 * HEAD_DIM)] = dq
+    d_own[:, pl.ds(cols[0], 2 * HEAD_DIM)] = dq[:half, :]
+    d_away[:, pl.ds(cols[0], 2 * HEAD_DIM)] = dq[half:, :]
 
 
 def call(kernel, core, args, grid, in_specs, out_specs, out_shape, scratch, flops, trans):
@@ -148,17 +164,17 @@
     wide = 2 * HEAD_DIM
     own = [
         pl.BlockSpec((half, wide), lambda pair, core, at=at: (0, 2 * (at + pair + first) + core[0]))
-        for at in (0, pairs, 0)
+        for at in (0, pairs, 2 * pairs)
     ]
     rec = [
         pl.BlockSpec((half, wide), lambda pair, core, at=at: (0, at + pair + first))
-        for at in (0, pairs, 0)
+        for at in (0, pairs, 2 * pairs)
     ]
     return own + rec
 
 
 def attention(core, heads, bias):
-    half, width = heads[-1].shape
+    half, width = heads[-1].shape[0], heads[-1].shape[1] // 3
     wide = 2 * HEAD_DIM
     pairs = width // wide
     full = 2 * half
@@ -170,11 +186,13 @@
         (pairs,),
         head_blocks(half, pairs) + [pl.BlockSpec((1, full), lambda pair, core: (0, 0))],
         [
-            pl.BlockSpec((full, wide), lambda pair, core: (0, pair)),
+            pl.BlockSpec((half, wide), lambda pair, core: (0, pair)),
+            pl.BlockSpec((half, wide), lambda pair, core: (0, pair)),
             pl.BlockSpec((1, 16, full), lambda pair, core: (pair, 0, 0)),
         ],
         [
-            jax.ShapeDtypeStruct((full, width), BF16),
+            jax.ShapeDtypeStruct((half, width), BF16),
+            jax.ShapeDtypeStruct((half, width), BF16),
             jax.ShapeDtypeStruct((pairs, 16, full), F32),
         ],
         [pltpu.VMEM((full, wide), BF16)] * 3 + [pltpu.VMEM((full, wide), F32)],
@@ -183,8 +201,8 @@
     )
 
 
-def attention_back(core, heads, g_own, g_rec, mixed, lse, bias, first, last):
-    half, width = heads[-1].shape
+def attention_back(core, heads, g_own, g_rec, o_own, o_away, lse, bias, first, last):
+    half, width = heads[-1].shape[0], heads[-1].shape[1] // 3
     wide = 2 * HEAD_DIM
     pairs = width // wide
     here = last - first
@@ -194,18 +212,19 @@
     return call(
         backward_kernel,
         core,
-        heads + (g_own, g_rec, mixed, lse, bias.reshape(full, 1)),
+        heads + (g_own, g_rec, o_own, o_away, lse, bias.reshape(full, 1)),
         (here,),
         head_blocks(half, pairs, first)
         + [
             col,
             col,
-            pl.BlockSpec((full, wide), lambda pair, core: (0, pair + first)),
+            col,
+            col,
             pl.BlockSpec((1, 16, full), lambda pair, core: (pair + first, 0, 0)),
             pl.BlockSpec((full, 1), lambda pair, core: (0, 0)),
         ],
-        pl.BlockSpec((full, 3 * here * wide), lambda pair, core: (0, 0)),
-        jax.ShapeDtypeStruct((full, 3 * here * wide), BF16),
+        [pl.BlockSpec((half, 3 * here * wide), lambda pair, core: (0, 0))] * 2,
+        [jax.ShapeDtypeStruct((half, 3 * here * wide), BF16)] * 2,
         [
             pltpu.VMEM((2, full, wide), BF16),
             pltpu.VMEM((full, wide), BF16),
@@ -523,8 +542,7 @@
             both = [jnp.where(core == 0, own, rec), jnp.where(core == 0, rec, own)]
             return jnp.stack(both, axis=1).reshape(n_shard * array.shape[0], array.shape[1])
 
-        qk_mat = lax.all_gather(w_qkv[:, : 2 * width], "shard", axis=0, tiled=True)
-        v_mat = gather(w_qkv[:, 2 * width :])
+        qkv_mat = lax.all_gather(w_qkv, "shard", axis=0, tiled=True)
         out_mat = gather(w_out)
         up_mat = lax.all_gather(w_up, "shard", axis=0, tiled=True)
         down_mat = lax.all_gather(w_down, "shard", axis=0, tiled=True)
@@ -535,20 +553,18 @@
         x_rows = bring(inputs).astype(F32)
         normed1 = (norm_parts(x_rows)[0] * gain1 + shift1).astype(BF16)
         normed1_rec = exchange(normed1)
-        qk_bias = jnp.concatenate([qbias, jnp.zeros_like(qbias)])
+        qkv_bias = jnp.concatenate([qbias, jnp.zeros_like(qbias), vbias])
         scale = jnp.concatenate(
-            [jnp.full((width,), HEAD_DIM ** (-0.5), BF16), jnp.ones((width,), BF16)]
-        )
-        qk = (jnp.dot(normed1, qk_mat, preferred_element_type=F32) + qk_bias).astype(BF16) * scale
-        value = (jnp.dot(normed1, v_mat, preferred_element_type=F32) + vbias).astype(BF16)
-        qk_rec = exchange(pick_other(core_arr, qk, unit))
-        value_rec = exchange(pick_other(core_arr, value, unit))
-        heads = (qk, qk, value, qk_rec, qk_rec, value_rec)
-        mixed_mine, lse = attention(core_arr, heads, key_bias)
+            [jnp.full((width,), HEAD_DIM ** (-0.5), BF16), jnp.ones((2 * width,), BF16)]
+        )
+        qkv = (jnp.dot(normed1, qkv_mat, preferred_element_type=F32) + qkv_bias).astype(BF16) * scale
+        rec = exchange(pick_other(core_arr, qkv, unit))
+        heads = (qkv, qkv, qkv, rec, rec, rec)
+        mixed_own, mixed_away, lse = attention(core_arr, heads, key_bias)
         both = bring(jnp.concatenate([teacher, cotangent], axis=-1))
         teach_rows = both[:, :width].astype(F32)
         cot_rows = both[:, width:].astype(F32)
-        mixed = merge(core_arr, (mixed_mine,), (exchange(mixed_mine[rows:]),), rows, unit, 1)
+        mixed = merge(core_arr, (mixed_own,), (exchange(mixed_away),), rows, unit, 1)
         attn_out = jnp.dot(mixed, out_mat, preferred_element_type=F32) + obias
         resid1 = x_rows + layer1 * attn_out
         normed2 = (norm_parts(resid1)[0] * gain2 + shift2).astype(BF16)
@@ -621,8 +637,8 @@
 
         w_out_part = weight_grad(
             core_arr,
-            (mixed_mine, mixed_mine, g_attn, g_attn_rec),
-            [strip, pl.BlockSpec((rows, tile), lambda i, core: (1, i)), whole, whole],
+            (mixed_own, mixed_away, g_attn, g_attn_rec),
+            [strip, strip, whole, whole],
             (width // 2, width),
             tile,
         )
@@ -630,34 +646,33 @@
         g_mine = (mixed_grad(g_attn), mixed_grad(g_attn_rec))
         pairs = width // 2 // unit
         g_alls = [
-            attention_back(core_arr, heads, *g_mine, mixed_mine, lse, key_bias, first, last)
+            attention_back(
+                core_arr, heads, *g_mine, mixed_own, mixed_away, lse, key_bias, first, last
+            )
             for first, last in ((0, 1), (1, pairs - 1), (pairs - 1, pairs))
         ]
-        g_recs = [exchange(part[rows:]) for part in g_alls]
+        g_owns = [part[0] for part in g_alls]
+        g_aways = [part[1] for part in g_alls]
+        g_recs = [exchange(part) for part in g_aways]
         order = []
         for part in range(3):
             for first, last in ((0, 1), (1, pairs - 1), (pairs - 1, pairs)):
                 order += [3 * first + part * (last - first) + idx for idx in range(last - first)]
         w_qkv_part = weight_grad(
             core_arr,
-            (normed1, normed1_rec) + tuple(g_alls) * 2,
+            (normed1, normed1_rec) + tuple(g_owns) + tuple(g_aways),
             [strip, strip]
-            + [
-                pl.BlockSpec((rows, part.shape[1]), lambda i, core, side=side: (side, 0))
-                for side in range(2)
-                for part in g_alls
-            ],
+            + [pl.BlockSpec((rows, part.shape[1]), lambda i, core: (0, 0)) for part in g_owns] * 2,
             (width, 3 * width // 2),
             tile,
         )
         p_qkv = scatter(w_qkv_part, unit, 1, order)
-        g_qkv = merge(core_arr, g_alls, g_recs, rows, unit, 3)
+        g_qkv = merge(core_arr, g_owns, g_recs, rows, unit, 3)
         d_qkv_bias = jnp.sum(g_qkv.astype(F32), axis=0)
-        g_norm1 = jnp.einsum(
-            "re,de->rd", g_qkv[:, : 2 * width], qk_mat, preferred_element_type=F32
-        ) + jnp.einsum("re,de->rd", g_qkv[:, 2 * width :], v_mat, preferred_element_type=F32)
+        g_norm1 = jnp.einsum("re,de->rd", g_qkv, qkv_mat, preferred_element_type=F32)
         g_ln1, d_gain1, d_shift1 = norm_back(x_rows, gain1, g_norm1)
-        g_in = give((g_pass + g_resid1 + g_ln1).astype(BF16)).astype(F32)
+        g_in = (g_pass + g_resid1 + g_ln1).astype(BF16)
+        g_in = give(g_in).astype(F32)
 
         p_down = z_reduce(p_down)
         p_up = z_reduce(p_up)

time: 636 us -> 685 us (1.077)
  waiting for transfers between devices: 194 us -> 252 us
  local copies, waits for them, and re-layouts: 39.2 us -> 29.4 us
    ppermute x8, waiting for transfers between devices: 25.1 us -> 47.2 us  [move(): return jnp.where(stays, array, lax.ppermute(array, axes, moves))]
    all_to_all x2 -> x1, waiting for transfers between devices: 0.01 us -> 17.8 us  [gather(): lax.all_to_all(jnp.broadcast_to(array[None], (n_shard // 2,) + array.shap...]
    all_to_all x1, waiting for transfers between devices: 12.1 us -> 26.5 us  [inner(): lax.all_to_all(sums.reshape(n_shard * n_seq, kinds, dl), axes, 0, 0, tile...]
    reduce_sum x1, other arithmetic: 1.72 us -> 13.1 us  [inner(): d_scale1 = jnp.sum(g_resid1 * attn_out, axis=0)]
    unnamed x30, other arithmetic: 32.1 us -> 23.8 us
    pallas_call x12 -> x11, Pallas kernels: 147 us -> 148 us  [call(): pl.pallas_call(kernel, grid_spec=pltpu.PrefetchScalarGridSpec(num_scalar_...]
    dot_general x4 -> x2, matrix products: 16.8 us -> 16.9 us  [the longest x1 9.89 us: inner(): jnp.dot(normed1, qkv_mat, preferred_element_type=F32) + qkv_bias]
  transfers between devices with their start and end apart: 39 -> 36, of which waited for: 9 -> 12; matrix products, arithmetic and copies ran while one was open for 22% -> 19% of each run, Pallas kernels for 23% -> 22%
where the time goes in v6:
time: 685 us; the launch traced here: 674 us
  waiting for transfers between devices  252 us (37%)
  Pallas kernels  148 us (22%)
  other arithmetic  84.6 us (12%)
  matrix products  81.3 us (12%)
  starting transfers between devices  50.5 us (7%)
  local copies, waits for them, and re-layouts  29.4 us (4%)
  between operations  17.9 us (3%)
  blocking collectives  10.7 us (2%)
    pallas_call x11, Pallas kernels, call(): pl.pallas_call(kernel, grid_spec=pltpu.PrefetchScalarGridSpec(num_scalar_...  148 us
    reduce_scatter x4, waiting for transfers between devices, scatter(): lax.psum_scatter(array, 'shard', scatter_dimension=0, axis_index_groups=c...  93.2 us
    ppermute x8, waiting for transfers between devices, move(): return jnp.where(stays, array, lax.ppermute(array, axes, moves))  47.2 us
    all_to_all x2, waiting for transfers between devices, z_reduce(): lax.all_to_all(jnp.broadcast_to(total[None], split), 'seq', 0, 0, tiled=T...  29 us
    all_to_all x1, waiting for transfers between devices, inner(): lax.all_to_all(sums.reshape(n_shard * n_seq, kinds, dl), axes, 0, 0, tile...  26.5 us
    unnamed x30, other arithmetic  23.8 us
    all_to_all x2, waiting for transfers between devices, z_reduce(): got = lax.all_to_all(array.reshape(split), 'seq', 0, 0, tiled=True)  21 us
    ppermute x8, starting transfers between devices, move(): return jnp.where(stays, array, lax.ppermute(array, axes, moves))  18.8 us
  transfers between devices with their start and end apart: 36, of which 12 were waited for; matrix products, arithmetic and copies ran while one was open for 19% of the time, Pallas kernels for 22%

profile of v6, /device:TPU:0, one launch (start us, length us, event | category | flops | bytes accessed | tf_op | source)
XLA Modules:
  0.0 674.3 jit_solution(2850026748483678388)
XLA Ops:
  10.5 4.3 collective-permute-start.1
  15.2 2.6 concatenate.64
  17.8 10.7 %all_gather.12 = bf16[15,1024]{1,0:T(8,128)(2,1)S(1)} all-gather(bf16[15,128]{1,0:T(8,128)(2,1)} %concatenate.64), channel_id=1, replica_groups=mesh['shard'=8,'seq'=4] {'shard'}, dimensions={1}, use_global_device_ids=true | all-gather | bytes 34560 | tf_op jit(solution)/shard_map/all_gather | solution.py:506
  33.0 15.1 %collective-permute-done.1 = bf16[344,1024]{1,0:T(8,128)(2,1)} collective-permute-done((bf16[344,1024]{1,0:T(8,128)(2,1)S(1)}, bf16[344,1024]{1,0:T(8,128)(2,1)}, u32[]{:S(2)}, u32[]{:S(2)}) %collective-permute-start.1) | collective-permute-done | bytes 704544 | tf_op jit(solution)/shard_map/ppermute | solution.py:412
  53.9 4.3 all-gather.4.cloned.1.call-done
  58.2 9.9 %fusion.8.src.q_own.k_own.v_own = bf16[704,3072]{1,0:T(8,128)(2,1)} fusion(bf16[704,1024]{1,0:T(8,128)(2,1)} %add_convert_fusion.2.a_own, bf16[1024,3072]{1,0:T(8,128)(2,1)} %all-gather.4.cloned.1.call-done, f32[3072]{0:T(1024)S(1)} %copy-done.36, bf16[3072]{0:T(1024)(128)(2,1)S(1)} %copy-done.46), kind=kOutput, calls=%fused_computation.15 | convolution fusion | flops 4435673088 | bytes 12077056 | tf_op jit(solution)/shard_map/dot_general | solution.py:560
  68.1 4.8 shard_map.331
  80.2 4.3 all-to-all-start
  88.7 17.8 %all-to-all-done = bf16[4,128,1024]{2,1,0:T(8,128)(2,1)} async-done(((bf16[4,128,1024]{2,1,0:T(8,128)(2,1)}), bf16[4,128,1024]{2,1,0:T(8,128)(2,1)}, u32[]{:S(2)}, u32[]{:S(2)}) %all-to-all-start) | async-done | bytes 1048608 | tf_op jit(solution)/shard_map/all_to_all | solution.py:533
  106.5 3.9 collective-permute-start.4
  110.4 32.1 %collective-permute-done.8 = bf16[344,2048]{1,0:T(8,128)(2,1)} collective-permute-done((bf16[344,2048]{1,0:T(8,128)(2,1)}, bf16[344,2048]{1,0:T(8,128)(2,1)}, u32[]{:S(2)}, u32[]{:S(2)}) %collective-permute-start.8) | collective-permute-done | bytes 1409056 | tf_op jit(solution)/shard_map/ppermute | solution.py:412
  144.6 39.2 %shard_map.332 = (bf16[704,512]{1,0:T(8,128)(2,1)}, bf16[704,512]{1,0:T(8,128)(2,1)}, f32[4,16,1408]{2,1,0:T(8,128)}) custom-call(s32[1]{0:T(128)} %bitcast.22.core_ref, bf16[704,3072]{1,0:T(8,128)(2,1)} %fusion.8.src.q_own.k_own.v_own, bf16[704,3072]{1,0:T(8,128)(2,1)} %fusion.8.src.q_own.k_own.v_own, bf16[704,3072]{1,0:T(8,128)(2,1)} %fusion.8.src.q_own.k_own.v_own, ...), custom_call_target="tpu_custom_call" | custom-call | flops 16240345088 | bytes 19469824 | tf_op jit(solution)/shard_map/pallas_call | solution.py:148
  189.4 3.1 shard_map.333
  192.5 5.5 multiply_add_fusion
  204.4 13.3 %multiply_convert_fusion = (bf16[704,4096]{1,0:T(8,128)(2,1)}, f32[704,4096]{1,0:T(8,128)}) fusion(f32[4096]{0:T(1024)S(1)} %bitcast.189, bf16[704,1024]{1,0:T(8,128)(2,1)} %add_convert_fusion.1.a_own, bf16[1024,4096]{1,0:T(8,128)(2,1)} %all-gather.6.cloned.1.call-done), kind=kOutput, calls=%fused_computation.8 | convolution fusion | flops 5922881536 | bytes 27148288 | tf_op jit(solution)/shard_map/dot_general | solution.py:572
  217.7 14.1 %multiply_reduce_fusion.1 = (f32[]{:T(128)}, f32[1024]{0:T(1024)}, f32[704,1024]{1,0:T(8,128)S(1)}, bf16[704,1024]{1,0:T(8,128)(2,1)}) fusion(pred[704]{0:T(1024)(128)(4,1)S(1)} %fusion.27, bf16[704,2048]{1,0:T(8,128)(2,1)} %bitcast.165, f32[1024]{0:T(1024)S(1)} %bitcast.205, f32[]{:T(128)S(6)} %mul.322, f32[2,352,1024]{2,1,0:T(8,128)S(1)} %fusion.18, ...), kind=kOutput, calls=%fused_computation.30 | convolution fusion | flops 5917834240 | bytes 27144904 | tf_op jit(solution)/shard_map/dot_general | solution.py:575
  232.2 13.2 %convert_reduce_fusion = (f32[4096]{0:T(1024)S(1)}, bf16[704,4096]{1,0:T(8,128)(2,1)S(1)}) fusion(f32[704,4096]{1,0:T(8,128)} %get-tuple-element.108, f32[4096]{0:T(1024)S(1)} %bitcast.190, bf16[704,1024]{1,0:T(8,128)(2,1)S(1)} %get-tuple-element.51.refs_0_, bf16[4096,1024]{1,0:T(8,128)(2,1)S(1)} %copy-done.44), kind=kOutput, calls=%fused_computation.7 | convolution fusion | flops 5943062528 | bytes 27164672 | tf_op jit(solution)/shard_map/rd,fd->rf/dot_general | solution.py:605
  245.5 11.6 %multiply_reduce_fusion.2 = (f32[1024]{0:T(1024)S(1)}, f32[704]{0:T(1024)S(1)}, f32[704]{0:T(1024)S(1)}, f32[1024]{0:T(1024)S(1)}, f32[704,1024]{1,0:T(8,128)S(1)}) fusion(f32[704,1024]{1,0:T(8,128)S(1)} %copy-done.2, f32[704]{0:T(1024)S(1)} %add_rsqrt_fusion, f32[704]{0:T(1024)S(1)} %broadcast_multiply_fusion.4, f32[1024]{0:T(1024)S(1)} %bitcast.178, ...), kind=kOutput, calls=%fused_computation.32 | convolution fusion | flops 5912065024 | bytes 19946496 | tf_op jit(solution)/shard_map/rf,df->rd/dot_general | solution.py:624
  257.1 13.1 %multiply_reduce_fusion.3 = (f32[1024]{0:T(1024)S(1)}, f32[704,1024]{1,0:T(8,128)S(1)}) fusion(f32[704,1024]{1,0:T(8,128)S(1)} %copy-done.13, f32[1024]{0:T(1024)S(1)} %bitcast.183, f32[704]{0:T(1024)S(1)} %broadcast_multiply_fusion.2, f32[704,1024]{1,0:T(8,128)S(1)} %copy-done.2, f32[704]{0:T(1024)S(1)} %broadcast_multiply_fusion.4, ...), kind=kLoop, calls=%fused_computation.33 | loop fusion | flops 8649728 | bytes 14442176 | tf_op jit(solution)/shard_map/reduce_sum | solution.py:627
  277.9 3.2 convolution_convert_fusion.1.g_own
  281.0 4.9 shard_map.339
  286.0 3.5 convolution_convert_fusion.g_rec
  289.5 14.6 %shard_map.334 = (bf16[704,384]{1,0:T(8,128)(2,1)}, bf16[704,384]{1,0:T(8,128)(2,1)}) custom-call(s32[1]{0:T(128)} %bitcast.22.core_ref, bf16[704,3072]{1,0:T(8,128)(2,1)} %fusion.8.src.q_own.k_own.v_own, bf16[704,3072]{1,0:T(8,128)(2,1)} %fusion.8.src.q_own.k_own.v_own, bf16[704,3072]{1,0:T(8,128)(2,1)} %fusion.8.src.q_own.k_own.v_own, ...), custom_call_target="tpu_custom_call" | custom-call | flops 10150215680 | bytes 22713856 | tf_op jit(solution)/shard_map/pallas_call | solution.py:148
  304.1 14.5 %shard_map.336 = (bf16[704,384]{1,0:T(8,128)(2,1)}, bf16[704,384]{1,0:T(8,128)(2,1)}) custom-call(s32[1]{0:T(128)} %bitcast.22.core_ref, bf16[704,3072]{1,0:T(8,128)(2,1)} %fusion.8.src.q_own.k_own.v_own, bf16[704,3072]{1,0:T(8,128)(2,1)} %fusion.8.src.q_own.k_own.v_own, bf16[704,3072]{1,0:T(8,128)(2,1)} %fusion.8.src.q_own.k_own.v_own, ...), custom_call_target="tpu_custom_call" | custom-call | flops 10150215680 | bytes 22713856 | tf_op jit(solution)/shard_map/pallas_call | solution.py:148
  318.6 27.0 %shard_map.335 = (bf16[704,768]{1,0:T(8,128)(2,1)}, bf16[704,768]{1,0:T(8,128)(2,1)}) custom-call(s32[1]{0:T(128)} %bitcast.22.core_ref, bf16[704,3072]{1,0:T(8,128)(2,1)} %fusion.8.src.q_own.k_own.v_own, bf16[704,3072]{1,0:T(8,128)(2,1)} %fusion.8.src.q_own.k_own.v_own, bf16[704,3072]{1,0:T(8,128)(2,1)} %fusion.8.src.q_own.k_own.v_own, ...), custom_call_target="tpu_custom_call" | custom-call | flops 20300431360 | bytes 22713856 | tf_op jit(solution)/shard_map/pallas_call | solution.py:148
  345.7 10.0 %shard_map.338 = bf16[1024,1536]{1,0:T(8,128)(2,1)} custom-call(s32[1]{0:T(128)} %bitcast.22.core_ref, bf16[704,1024]{1,0:T(8,128)(2,1)} %add_convert_fusion.2.a_own, bf16[704,1024]{1,0:T(8,128)(2,1)} %collective-permute-done.15.a_rec, bf16[704,384]{1,0:T(8,128)(2,1)} %get-tuple-element.30.refs_0_, bf16[704,768]{1,0:T(8,128)(2,1)} %get-tuple-element.31.refs_1_, ...), custom_call_target="tpu_custom_call" | custom-call | flops 4429185024 | bytes 7208960 | tf_op jit(solution)/shard_map/pallas_call | solution.py:148
  356.4 41.6 %reduce-scatter.5.cloned.1.call-done = bf16[256,1536]{1,0:T(8,128)(2,1)} async-done(((bf16[1024,1536]{1,0:T(8,128)(2,1)}), bf16[256,1536]{1,0:T(8,128)(2,1)}) %reduce-scatter.5.cloned.1.call-update) | async-done | bytes 786448 | tf_op jit(solution)/shard_map/reduce_scatter | solution.py:459
  398.1 11.6 %shard_map.340 = bf16[1024,2048]{1,0:T(8,128)(2,1)} custom-call(s32[1]{0:T(128)} %bitcast.22.core_ref, bf16[704,1024]{1,0:T(8,128)(2,1)} %add_convert_fusion.1.a_own, bf16[704,1024]{1,0:T(8,128)(2,1)} %collective-permute-done.17.a_rec, bf16[704,4096]{1,0:T(8,128)(2,1)} %copy-done, bf16[704,4096]{1,0:T(8,128)(2,1)} %copy-done, bf16[704,4096]{1,0:T(8,128)(2,1)} %copy-done, ...), custom_call_target="tpu_custom_call" | custom-call | flops 5905580032 | bytes 49020928 | tf_op jit(solution)/shard_map/pallas_call | solution.py:148
  410.4 11.2 %collective-permute-done.21.refs_1_ = bf16[704,1024]{1,0:T(8,128)(2,1)S(1)} collective-permute-done((bf16[704,1024]{1,0:T(8,128)(2,1)}, bf16[704,1024]{1,0:T(8,128)(2,1)S(1)}, u32[]{:S(2)}, u32[]{:S(2)}) %collective-permute-start.21) | collective-permute-done | bytes 1441824 | tf_op jit(solution)/shard_map/ppermute | solution.py:443
  422.6 12.0 %shard_map.341 = bf16[2048,1024]{1,0:T(8,128)(2,1)} custom-call(s32[1]{0:T(128)} %bitcast.22.core_ref, bf16[704,4096]{1,0:T(8,128)(2,1)} %get-tuple-element.107.a_own, bf16[704,4096]{1,0:T(8,128)(2,1)} %collective-permute-done.20.a_rec, bf16[704,1024]{1,0:T(8,128)(2,1)} %copy-done.15, bf16[704,1024]{1,0:T(8,128)(2,1)} %copy-done.45), custom_call_target="tpu_custom_call" | custom-call | flops 5905580032 | bytes 14417920 | tf_op jit(solution)/shard_map/pallas_call | solution.py:148
  439.6 3.3 collective-permute-start.6
  443.7 5.7 shard_map.337
  449.5 3.2 convert_reduce_fusion.1
  453.0 7.0 %fusion.36 = f32[704,1024]{1,0:T(8,128)S(1)} fusion(bf16[704,3072]{1,0:T(8,128)(2,1)S(1)} %copy-done.5, bf16[1024,3072]{1,0:T(8,128)(2,1)} %all-gather.4.cloned.1.call-done), kind=kOutput, calls=%fused_computation.179 | convolution fusion | flops 4429185024 | bytes 13500416 | tf_op jit(solution)/shard_map/re,de->rd/dot_general | solution.py:672
  463.1 4.1 all-to-all-start.1
  467.2 4.9 fusion.13
  473.8 3.2 collective-permute-start.14
  477.1 26.5 %all-to-all-done.1 = f32[32,15,128]{2,1,0:T(8,128)S(1)} async-done(((f32[32,15,128]{2,1,0:T(8,128)}), f32[32,15,128]{2,1,0:T(8,128)S(1)}, u32[]{:S(2)}, u32[]{:S(2)}) %all-to-all-start.1) | async-done | bytes 245792 | tf_op jit(solution)/shard_map/all_to_all | solution.py:706
  508.1 8.8 %reduce-scatter.9.cloned.1.call-done = bf16[256,2048]{1,0:T(8,128)(2,1)} async-done(((bf16[1024,2048]{1,0:T(8,128)(2,1)}), bf16[256,2048]{1,0:T(8,128)(2,1)}) %reduce-scatter.9.cloned.1.call-update) | async-done | bytes 1048592 | tf_op jit(solution)/shard_map/reduce_scatter | solution.py:459
  516.9 4.6 all-to-all-start.2
  529.8 42.8 %reduce-scatter.11.cloned.1.call-done = bf16[512,1024]{1,0:T(8,128)(2,1)} async-done(((bf16[2048,1024]{1,0:T(8,128)(2,1)}), bf16[512,1024]{1,0:T(8,128)(2,1)}) %reduce-scatter.11.cloned.1.call-update) | async-done | bytes 1048592 | tf_op jit(solution)/shard_map/reduce_scatter | solution.py:459
  572.5 4.6 all-to-all-start.4
  581.7 21.0 %all-to-all-done.4 = bf16[4,128,1024]{2,1,0:T(8,128)(2,1)S(1)} async-done(((bf16[4,128,1024]{2,1,0:T(8,128)(2,1)}), bf16[4,128,1024]{2,1,0:T(8,128)(2,1)S(1)}, u32[]{:S(2)}, u32[]{:S(2)}) %all-to-all-start.4) | async-done | bytes 1048608 | tf_op jit(solution)/shard_map/all_to_all | solution.py:467
  603.8 3.5 all-to-all-start.3
  617.2 15.4 %all-to-all-done.3 = bf16[4,64,2048]{2,1,0:T(8,128)(2,1)S(1)} async-done(((bf16[4,64,2048]{2,1,0:T(8,128)(2,1)}), bf16[4,64,2048]{2,1,0:T(8,128)(2,1)S(1)}, u32[]{:S(2)}, u32[]{:S(2)}) %all-to-all-start.3) | async-done | bytes 1048608 | tf_op jit(solution)/shard_map/all_to_all | solution.py:469
  633.7 3.5 all-to-all-start.5
  646.4 2.4 convert_element_type.163
  648.8 13.6 %all-to-all-done.5 = bf16[4,128,1024]{2,1,0:T(8,128)(2,1)S(1)} async-done(((bf16[4,128,1024]{2,1,0:T(8,128)(2,1)}), bf16[4,128,1024]{2,1,0:T(8,128)(2,1)S(1)}, u32[]{:S(2)}, u32[]{:S(2)}) %all-to-all-start.5) | async-done | bytes 1048608 | tf_op jit(solution)/shard_map/all_to_all | solution.py:469
  (265 shorter events, 101.1 us)
Async XLA Ops:
  7.2 8.0 %copy-start.42 = (bf16[128]{0:T(256)(128)(2,1)S(1)}, bf16[128]{0:T(256)(128)(2,1)}, u32[]{:S(2)}) copy-start(bf16[128]{0:T(256)(128)(2,1)} %param.26) | copy-start | bytes 772
  7.3 51.0 %all-gather.4.cloned.1.call-start = ((), (), s32[]{:S(2)}) async-start(), calls=%async_computation.10 | async-start | bytes 7077888 | tf_op jit(solution)/shard_map/all_gather | solution.py:545
  8.0 196.4 %all-gather.6.cloned.1.call-start = ((), (), s32[]{:S(2)}) async-start(), calls=%async_computation.11 | async-start | bytes 9437184 | tf_op jit(solution)/shard_map/all_gather | solution.py:547
  8.7 208.9 %all-gather.8.cloned.1.call-start = ((), (), s32[]{:S(2)}) async-start(), calls=%async_computation.12 | async-start | bytes 9437184 | tf_op jit(solution)/shard_map/all_gather | solution.py:548
  9.7 21.6 %copy-start.17 = (bf16[2,344,1024]{2,1,0:T(8,128)(2,1)S(1)}, bf16[2,344,1024]{2,1,0:T(8,128)(2,1)}, u32[]{:S(2)}) copy-start(bf16[2,344,1024]{2,1,0:T(8,128)(2,1)} %param.22) | copy-start | bytes 4227076
  9.7 21.7 %collective-permute-start = (bf16[344,1024]{1,0:T(8,128)(2,1)S(1)}, bf16[344,1024]{1,0:T(8,128)(2,1)S(1)}, u32[]{:S(2)}, u32[]{:S(2)}) collective-permute-start(bf16[344,1024]{1,0:T(8,128)(2,1)S(1)} %get-tuple-element.77), channel_id=1, source_target_pairs={{1,4},{2,1},{3,5},{4,2},{5,6},{6,3},{9,12},{10,9},{11,13},{12,10},... | collective-permute-start | bytes 2113544 | tf_op jit(solution)/shard_map/ppermute | solution.py:412
  10.5 37.5 %collective-permute-start.1 = (bf16[344,1024]{1,0:T(8,128)(2,1)S(1)}, bf16[344,1024]{1,0:T(8,128)(2,1)}, u32[]{:S(2)}, u32[]{:S(2)}) collective-permute-start(bf16[344,1024]{1,0:T(8,128)(2,1)S(1)} %get-tuple-element.76), channel_id=1, source_target_pairs={{0,1},{1,5},{2,0},{3,4},{4,3},{5,7},{6,2},{7,6},{8,9},{9,13},{10,8... | collective-permute-start | bytes 2113544 | tf_op jit(solution)/shard_map/ppermute | solution.py:412
  72.9 71.7 %collective-permute-start.2 = (bf16[704,1536]{1,0:T(8,128)(2,1)}, bf16[704,1536]{1,0:T(8,128)(2,1)}, u32[]{:S(2)}, u32[]{:S(2)}) collective-permute-start(bf16[704,1536]{1,0:T(8,128)(2,1)} %shard_map.331), channel_id=1, source_target_pairs={{0,4},{1,5},{2,6},{3,7},{4,0},{5,1},{6,2},{7,3},{8,12},{9,13},{10,... | collective-permute-start | bytes 6488072 | tf_op jit(solution)/shard_map/ppermute | solution.py:443
  75.0 9.5 %copy-start.32 = (f32[1,1024]{1,0:T(1,128)S(1)}, f32[1,1024]{1,0:T(1,128)}, u32[]{:S(2)}) copy-start(f32[1,1024]{1,0:T(1,128)} %get-tuple-element.88) | copy-start | bytes 12292
  75.0 35.3 %collective-permute-start.7 = (bf16[344,2048]{1,0:T(8,128)(2,1)}, bf16[344,2048]{1,0:T(8,128)(2,1)}, u32[]{:S(2)}, u32[]{:S(2)}) collective-permute-start(bf16[344,2048]{1,0:T(8,128)(2,1)} %get-tuple-element.69), channel_id=1, source_target_pairs={{1,4},{2,1},{3,5},{4,2},{5,6},{6,3},{9,12},{10,9},{11,13},{12,10},... | collective-permute-start | bytes 4227080 | tf_op jit(solution)/shard_map/ppermute | solution.py:412
  76.9 65.6 %collective-permute-start.8 = (bf16[344,2048]{1,0:T(8,128)(2,1)}, bf16[344,2048]{1,0:T(8,128)(2,1)}, u32[]{:S(2)}, u32[]{:S(2)}) collective-permute-start(bf16[344,2048]{1,0:T(8,128)(2,1)} %get-tuple-element.68), channel_id=1, source_target_pairs={{0,1},{1,5},{2,0},{3,4},{4,3},{5,7},{6,2},{7,6},{8,9},{9,13},{10,8... | collective-permute-start | bytes 4227080 | tf_op jit(solution)/shard_map/ppermute | solution.py:412
  80.2 26.3 %all-to-all-start = ((bf16[4,128,1024]{2,1,0:T(8,128)(2,1)}), bf16[4,128,1024]{2,1,0:T(8,128)(2,1)}, u32[]{:S(2)}, u32[]{:S(2)}) async-start(bf16[4,128,1024]{2,1,0:T(8,128)(2,1)} %broadcast_in_dim.83), calls=%async_computation | async-start | bytes 2097152 | tf_op jit(solution)/shard_map/all_to_all | solution.py:533
  84.4 272.0 %reduce-scatter.7.cloned.1.call-start = ((), (), s32[]{:S(2)}) async-start(), calls=%async_computation.14 | async-start | bytes 1310720 | tf_op jit(solution)/shard_map/reduce_scatter | solution.py:459
  106.5 79.4 %collective-permute-start.4 = (bf16[4,128,1024]{2,1,0:T(8,128)(2,1)}, bf16[4,128,1024]{2,1,0:T(8,128)(2,1)S(1)}, u32[]{:S(2)}, u32[]{:S(2)}) collective-permute-start(bf16[4,128,1024]{2,1,0:T(8,128)(2,1)} %all-to-all-done), channel_id=1, source_target_pairs={{0,4},{1,5},{2,6},{3,7},{4,0},{5,1},{6,2},{7,3},{8,12},{9,13},{10,... | collective-permute-start | bytes 3145736 | tf_op jit(solution)/shard_map/ppermute | solution.py:443
  183.8 4.7 collective-permute-start.3
  204.4 13.3 %copy-start.31 = (f32[1,1024]{1,0:T(1,128)S(1)}, f32[1,1024]{1,0:T(1,128)}, u32[]{:S(2)}) copy-start(f32[1,1024]{1,0:T(1,128)} %get-tuple-element.82) | copy-start | bytes 12292
  204.4 13.3 %copy-start.39 = (f32[1,1024]{1,0:T(1,128)S(1)}, f32[1,1024]{1,0:T(1,128)}, u32[]{:S(2)}) copy-start(f32[1,1024]{1,0:T(1,128)} %get-tuple-element.83) | copy-start | bytes 12292
  217.7 14.5 %copy-start.44 = (bf16[4096,1024]{1,0:T(8,128)(2,1)S(1)}, bf16[4096,1024]{1,0:T(8,128)(2,1)}, u32[]{:S(2)}) copy-start(bf16[4096,1024]{1,0:T(8,128)(2,1)} %all-gather.8.cloned.1.call-done) | copy-start | bytes 25165828
  231.8 25.3 %copy-start.3 = (f32[704,1024]{1,0:T(8,128)}, f32[704,1024]{1,0:T(8,128)S(1)}, u32[]{:S(2)}) copy-start(f32[704,1024]{1,0:T(8,128)S(1)} %get-tuple-element.48) | copy-start | bytes 8650756
  232.2 13.3 %copy-start.15 = (bf16[704,1024]{1,0:T(8,128)(2,1)}, bf16[704,1024]{1,0:T(8,128)(2,1)S(1)}, u32[]{:S(2)}) copy-start(bf16[704,1024]{1,0:T(8,128)(2,1)S(1)} %get-tuple-element.51.refs_0_) | copy-start | bytes 4325380
  232.2 13.3 %copy-start.2 = (f32[704,1024]{1,0:T(8,128)S(1)}, f32[704,1024]{1,0:T(8,128)}, u32[]{:S(2)}) copy-start(f32[704,1024]{1,0:T(8,128)} %get-tuple-element.105) | copy-start | bytes 8650756
  245.5 11.6 %copy-start = (bf16[704,4096]{1,0:T(8,128)(2,1)}, bf16[704,4096]{1,0:T(8,128)(2,1)S(1)}, u32[]{:S(2)}) copy-start(bf16[704,4096]{1,0:T(8,128)(2,1)S(1)} %get-tuple-element.111.refs_0_.refs_1_.refs_2_.refs_3_) | copy-start | bytes 17301508
  245.5 11.6 %copy-start.13 = (f32[704,1024]{1,0:T(8,128)S(1)}, f32[704,1024]{1,0:T(8,128)}, u32[]{:S(2)}) copy-start(f32[704,1024]{1,0:T(8,128)} %get-tuple-element.106) | copy-start | bytes 8650756
  273.3 7.7 %collective-permute-start.9 = (bf16[704,1024]{1,0:T(8,128)(2,1)}, bf16[704,1024]{1,0:T(8,128)(2,1)}, u32[]{:S(2)}, u32[]{:S(2)}) collective-permute-start(bf16[704,1024]{1,0:T(8,128)(2,1)} %get-tuple-element.55.refs_0_), channel_id=1, source_target_pairs={{0,4},{1,5},{2,6},{3,7},{4,0},{5,1},{6,2},{7,3},{8,12},{9,13},{10,... | collective-permute-start | bytes 4325384 | tf_op jit(solution)/shard_map/ppermute | solution.py:443
  275.2 70.4 %collective-permute-start.15 = (bf16[704,1024]{1,0:T(8,128)(2,1)}, bf16[704,1024]{1,0:T(8,128)(2,1)}, u32[]{:S(2)}, u32[]{:S(2)}) collective-permute-start(bf16[704,1024]{1,0:T(8,128)(2,1)} %add_convert_fusion.2.a_own), channel_id=1, source_target_pairs={{0,4},{1,5},{2,6},{3,7},{4,0},{5,1},{6,2},{7,3},{8,12},{9,13},{10,... | collective-permute-start | bytes 4325384 | tf_op jit(solution)/shard_map/ppermute | solution.py:443
  285.9 112.0 %reduce-scatter.5.cloned.1.call-start = ((), (), s32[]{:S(2)}) async-start(), calls=%async_computation.13 | async-start | bytes 3932160 | tf_op jit(solution)/shard_map/reduce_scatter | solution.py:459
  355.7 150.2 %all-reduce.6.cloned.1.call-start = ((), (), s32[]{:S(2)}) async-start(), calls=%async_computation.17 | async-start | bytes 2097152 | tf_op jit(solution)/shard_map/psum | solution.py:679
  355.8 42.3 %collective-permute-start.18 = (bf16[704,4096]{1,0:T(8,128)(2,1)}, bf16[704,4096]{1,0:T(8,128)(2,1)}, u32[]{:S(2)}, u32[]{:S(2)}) collective-permute-start(bf16[704,4096]{1,0:T(8,128)(2,1)} %copy-done), channel_id=1, source_target_pairs={{0,4},{1,5},{2,6},{3,7},{4,0},{5,1},{6,2},{7,3},{8,12},{9,13},{10,... | collective-permute-start | bytes 17301512 | tf_op jit(solution)/shard_map/ppermute | solution.py:443
  356.3 41.7 %collective-permute-start.17 = (bf16[704,1024]{1,0:T(8,128)(2,1)}, bf16[704,1024]{1,0:T(8,128)(2,1)}, u32[]{:S(2)}, u32[]{:S(2)}) collective-permute-start(bf16[704,1024]{1,0:T(8,128)(2,1)} %add_convert_fusion.1.a_own), channel_id=1, source_target_pairs={{0,4},{1,5},{2,6},{3,7},{4,0},{5,1},{6,2},{7,3},{8,12},{9,13},{10,... | collective-permute-start | bytes 4325384 | tf_op jit(solution)/shard_map/ppermute | solution.py:443
  398.0 118.9 %reduce-scatter.9.cloned.1.call-start = ((), (), s32[]{:S(2)}) async-start(), calls=%async_computation.15 | async-start | bytes 5242880 | tf_op jit(solution)/shard_map/reduce_scatter | solution.py:459
  409.7 162.8 %reduce-scatter.11.cloned.1.call-start = ((), (), s32[]{:S(2)}) async-start(), calls=%async_computation.16 | async-start | bytes 5242880 | tf_op jit(solution)/shard_map/reduce_scatter | solution.py:459
  409.8 11.8 %collective-permute-start.20 = (bf16[704,4096]{1,0:T(8,128)(2,1)}, bf16[704,4096]{1,0:T(8,128)(2,1)}, u32[]{:S(2)}, u32[]{:S(2)}) collective-permute-start(bf16[704,4096]{1,0:T(8,128)(2,1)} %get-tuple-element.107.a_own), channel_id=1, source_target_pairs={{0,4},{1,5},{2,6},{3,7},{4,0},{5,1},{6,2},{7,3},{8,12},{9,13},{10,... | collective-permute-start | bytes 17301512 | tf_op jit(solution)/shard_map/ppermute | solution.py:443
  409.9 11.7 %collective-permute-start.21 = (bf16[704,1024]{1,0:T(8,128)(2,1)}, bf16[704,1024]{1,0:T(8,128)(2,1)S(1)}, u32[]{:S(2)}, u32[]{:S(2)}) collective-permute-start(bf16[704,1024]{1,0:T(8,128)(2,1)} %copy-done.15), channel_id=1, source_target_pairs={{0,4},{1,5},{2,6},{3,7},{4,0},{5,1},{6,2},{7,3},{8,12},{9,13},{10,... | collective-permute-start | bytes 4325384 | tf_op jit(solution)/shard_map/ppermute | solution.py:443
  434.7 8.3 %collective-permute-start.11 = (bf16[704,768]{1,0:T(8,128)(2,1)}, bf16[704,768]{1,0:T(8,128)(2,1)}, u32[]{:S(2)}, u32[]{:S(2)}) collective-permute-start(bf16[704,768]{1,0:T(8,128)(2,1)} %get-tuple-element.34.refs_4_), channel_id=1, source_target_pairs={{0,4},{1,5},{2,6},{3,7},{4,0},{5,1},{6,2},{7,3},{8,12},{9,13},{10,... | collective-permute-start | bytes 3244040 | tf_op jit(solution)/shard_map/ppermute | solution.py:443
  434.9 8.0 %collective-permute-start.10 = (bf16[704,384]{1,0:T(8,128)(2,1)}, bf16[704,384]{1,0:T(8,128)(2,1)S(1)}, u32[]{:S(2)}, u32[]{:S(2)}) collective-permute-start(bf16[704,384]{1,0:T(8,128)(2,1)} %get-tuple-element.33.refs_3_), channel_id=1, source_target_pairs={{0,4},{1,5},{2,6},{3,7},{4,0},{5,1},{6,2},{7,3},{8,12},{9,13},{10,... | collective-permute-start | bytes 1622024 | tf_op jit(solution)/shard_map/ppermute | solution.py:443
  435.3 7.7 %collective-permute-start.12 = (bf16[704,384]{1,0:T(8,128)(2,1)}, bf16[704,384]{1,0:T(8,128)(2,1)}, u32[]{:S(2)}, u32[]{:S(2)}) collective-permute-start(bf16[704,384]{1,0:T(8,128)(2,1)} %get-tuple-element.35.refs_5_), channel_id=1, source_target_pairs={{0,4},{1,5},{2,6},{3,7},{4,0},{5,1},{6,2},{7,3},{8,12},{9,13},{10,... | collective-permute-start | bytes 1622024 | tf_op jit(solution)/shard_map/ppermute | solution.py:443
  438.1 83.4 %collective-permute-start.5 = (bf16[344,1024]{1,0:T(8,128)(2,1)}, bf16[344,1024]{1,0:T(8,128)(2,1)}, u32[]{:S(2)}, u32[]{:S(2)}) collective-permute-start(bf16[344,1024]{1,0:T(8,128)(2,1)} %get-tuple-element.75), channel_id=1, source_target_pairs={{4,1},{1,2},{5,3},{2,4},{6,5},{3,6},{12,9},{9,10},{13,11},{10,12},... | collective-permute-start | bytes 2113544 | tf_op jit(solution)/shard_map/ppermute | solution.py:412
  439.6 81.9 %collective-permute-start.6 = (bf16[344,1024]{1,0:T(8,128)(2,1)}, bf16[344,1024]{1,0:T(8,128)(2,1)}, u32[]{:S(2)}, u32[]{:S(2)}) collective-permute-start(bf16[344,1024]{1,0:T(8,128)(2,1)} %get-tuple-element.74), channel_id=1, source_target_pairs={{1,0},{5,1},{0,2},{4,3},{3,4},{7,5},{2,6},{6,7},{9,8},{13,9},{8,10... | collective-permute-start | bytes 2113544 | tf_op jit(solution)/shard_map/ppermute | solution.py:412
  463.1 40.5 %all-to-all-start.1 = ((f32[32,15,128]{2,1,0:T(8,128)}), f32[32,15,128]{2,1,0:T(8,128)S(1)}, u32[]{:S(2)}, u32[]{:S(2)}) async-start(f32[32,15,128]{2,1,0:T(8,128)} %bitcast.65), calls=%async_computation.1 | async-start | bytes 524288 | tf_op jit(solution)/shard_map/all_to_all | solution.py:706
  472.3 49.2 %collective-permute-start.13 = (bf16[344,1024]{1,0:T(8,128)(2,1)S(1)}, bf16[344,1024]{1,0:T(8,128)(2,1)}, u32[]{:S(2)}, u32[]{:S(2)}) collective-permute-start(bf16[344,1024]{1,0:T(8,128)(2,1)S(1)} %get-tuple-element.73), channel_id=1, source_target_pairs={{4,1},{1,2},{5,3},{2,4},{6,5},{3,6},{12,9},{9,10},{13,11},{10,12},... | collective-permute-start | bytes 2113544 | tf_op jit(solution)/shard_map/ppermute | solution.py:412
  473.8 47.7 %collective-permute-start.14 = (bf16[344,1024]{1,0:T(8,128)(2,1)S(1)}, bf16[344,1024]{1,0:T(8,128)(2,1)}, u32[]{:S(2)}, u32[]{:S(2)}) collective-permute-start(bf16[344,1024]{1,0:T(8,128)(2,1)S(1)} %get-tuple-element.72), channel_id=1, source_target_pairs={{1,0},{5,1},{0,2},{4,3},{3,4},{7,5},{2,6},{6,7},{9,8},{13,9},{8,10... | collective-permute-start | bytes 2113544 | tf_op jit(solution)/shard_map/ppermute | solution.py:412
  507.8 19.4 %collective-permute-start.16 = (bf16[128,1536]{1,0:T(8,128)(2,1)}, bf16[128,1536]{1,0:T(8,128)(2,1)S(1)}, u32[]{:S(2)}, u32[]{:S(2)}) collective-permute-start(bf16[128,1536]{1,0:T(8,128)(2,1)} %get-tuple-element.81), channel_id=1, source_target_pairs={{0,4},{1,5},{2,6},{3,7},{4,0},{5,1},{6,2},{7,3},{8,12},{9,13},{10,... | collective-permute-start | bytes 1179656 | tf_op jit(solution)/shard_map/ppermute | solution.py:443
  516.9 55.6 %all-to-all-start.2 = ((bf16[4,64,2048]{2,1,0:T(8,128)(2,1)}), bf16[4,64,2048]{2,1,0:T(8,128)(2,1)S(1)}, u32[]{:S(2)}, u32[]{:S(2)}) async-start(bf16[4,64,2048]{2,1,0:T(8,128)(2,1)} %bitcast.168), calls=%async_computation.5 | async-start | bytes 2097152 | tf_op jit(solution)/shard_map/all_to_all | solution.py:467
  527.2 76.6 %copy-start.14 = (bf16[128,1536]{1,0:T(8,128)(2,1)}, bf16[128,1536]{1,0:T(8,128)(2,1)S(1)}, u32[]{:S(2)}) copy-start(bf16[128,1536]{1,0:T(8,128)(2,1)S(1)} %collective-permute-done.16) | copy-start | bytes 1179652
  572.5 30.2 %all-to-all-start.4 = ((bf16[4,128,1024]{2,1,0:T(8,128)(2,1)}), bf16[4,128,1024]{2,1,0:T(8,128)(2,1)S(1)}, u32[]{:S(2)}, u32[]{:S(2)}) async-start(bf16[4,128,1024]{2,1,0:T(8,128)(2,1)} %bitcast.169), calls=%async_computation.8 | async-start | bytes 2097152 | tf_op jit(solution)/shard_map/all_to_all | solution.py:467
  603.8 28.8 %all-to-all-start.3 = ((bf16[4,64,2048]{2,1,0:T(8,128)(2,1)}), bf16[4,64,2048]{2,1,0:T(8,128)(2,1)S(1)}, u32[]{:S(2)}, u32[]{:S(2)}) async-start(bf16[4,64,2048]{2,1,0:T(8,128)(2,1)} %broadcast_in_dim.90), calls=%async_computation.6 | async-start | bytes 2097152 | tf_op jit(solution)/shard_map/all_to_all | solution.py:469
  633.7 28.8 %all-to-all-start.5 = ((bf16[4,128,1024]{2,1,0:T(8,128)(2,1)}), bf16[4,128,1024]{2,1,0:T(8,128)(2,1)S(1)}, u32[]{:S(2)}, u32[]{:S(2)}) async-start(bf16[4,128,1024]{2,1,0:T(8,128)(2,1)} %broadcast_in_dim.91), calls=%async_computation.9 | async-start | bytes 2097152 | tf_op jit(solution)/shard_map/all_to_all | solution.py:469
  645.0 19.1 %collective-permute-start.19 = (bf16[128,2048]{1,0:T(8,128)(2,1)}, bf16[128,2048]{1,0:T(8,128)(2,1)S(1)}, u32[]{:S(2)}, u32[]{:S(2)}) collective-permute-start(bf16[128,2048]{1,0:T(8,128)(2,1)} %get-tuple-element.79), channel_id=1, source_target_pairs={{0,4},{1,5},{2,6},{3,7},{4,0},{5,1},{6,2},{7,3},{8,12},{9,13},{10,... | collective-permute-start | bytes 1572872 | tf_op jit(solution)/shard_map/ppermute | solution.py:443
  (35 other events, 132.5 us)
Sparse Core Ops, SparseCore 0:
  9.9 48.2 all-gather.3
  60.1 63.7 all-gather.5
  125.7 53.4 all-gather.7
  286.1 26.2 reduce-scatter.6
  355.8 42.1 reduce-scatter.4
  400.3 59.0 all-reduce.5
  462.3 54.5 reduce-scatter.8
  519.9 52.5 reduce-scatter.10
